TPU v7x, 128 devices: a whole 4x4x4 slice. The times are simulated.
128 devices in a mesh: seg: 8 (over y_lo, z), grp: 16 (over x, y_hi, core).
Axes of the slice: x: 4, y: 4 (y_hi: 2, y_lo: 2; y = y_hi * 2 + y_lo), z: 4, core: 2. Of those that a mesh axis runs over, the one named last changes fastest.
Arguments:
- frames_in: bfloat16 [128, 32, 120, 128], P(('seg', 'grp')), may hold values from -6 to 6
- spatial_weight: bfloat16 [9, 128, 128], replicated, may hold values from -0.1875 to 0.1875
- temporal_weight: bfloat16 [2, 5, 128, 128], replicated, may hold values from -0.25 to 0.25
- uniting_weight: bfloat16 [2, 128, 128], replicated, may hold values from -0.375 to 0.375
- key_index: int32 [8], replicated, may hold values from 0 to 15
- dilation: int32 [2], replicated, may hold values from 1 to 8, as said below
- cotangent: bfloat16 [128, 32, 120, 128], P(('seg', 'grp')), may hold values from -6 to 6
Outputs:
- united: bfloat16 [128, 32, 120, 128], P(('seg', 'grp'))
- grad_frames: bfloat16 [128, 32, 120, 128], P(('seg', 'grp'))
- grad_spatial: float32 [9, 128, 128], replicated
- grad_temporal: float32 [2, 5, 128, 128], replicated
- grad_uniting: float32 [2, 128, 128], replicated
Inputs may be any that keep to these rules, and one draw needn't show every extreme that they name: `key_index`: position of a segment's keyframe within its 16 frames. Exactly one layer uses dilation 8; the others use less.
All inputs are finite; a program needn't handle non-finite values.
Results may differ from a plain program's by a relative error of at most 0.0095.
Values may be sent and summed in bfloat16 or wider, within the bound.
A program may use at most 128 MiB of HBM per device.

v0:
```python
import functools

import jax
import jax.numpy as jnp
from jax import lax
from jax.sharding import PartitionSpec as P
from jax.experimental import pallas as pl
from jax.experimental.pallas import tpu as pltpu

LAYERS = 2
DMAX = 8


def from_root(value, axis, root):
    mine = lax.axis_index(axis) == root
    return lax.psum(jnp.where(mine, value, jnp.zeros_like(value)), axis)


def silu_grad(value):
    sigma = jax.nn.sigmoid(value)
    return sigma * (1.0 + value * (1.0 - sigma))


def inner(left, right):
    return lax.dot_general(
        left, right, (((0,), (0,)), ((), ())), preferred_element_type=jnp.float32
    )


def spatial_forward(frames, kernel):
    count, rows, cols, chans = frames.shape
    padded = jnp.pad(frames, ((0, 0), (1, 1), (1, 1), (0, 0)))
    total = jnp.zeros((count * rows * cols, chans), jnp.float32)
    for row_tap in range(3):
        for col_tap in range(3):
            piece = padded[:, row_tap : row_tap + rows, col_tap : col_tap + cols, :].reshape(
                -1, chans
            )
            total = total + jnp.dot(
                piece, kernel[3 * row_tap + col_tap], preferred_element_type=jnp.float32
            )
    return total.reshape(frames.shape)


def spatial_back(grads, kernel):
    count, rows, cols, chans = grads.shape
    padded = jnp.pad(grads, ((0, 0), (1, 1), (1, 1), (0, 0)))
    total = jnp.zeros((count * rows * cols, chans), jnp.float32)
    for row_tap in range(3):
        for col_tap in range(3):
            piece = padded[
                :, 2 - row_tap : 2 - row_tap + rows, 2 - col_tap : 2 - col_tap + cols, :
            ].reshape(-1, chans)
            total = total + jnp.dot(
                piece, kernel[3 * row_tap + col_tap].T, preferred_element_type=jnp.float32
            )
    return total.reshape(grads.shape)


def spatial_wgrad(frames, grads):
    count, rows, cols, chans = frames.shape
    padded = jnp.pad(frames, ((0, 0), (1, 1), (1, 1), (0, 0)))
    flat_grads = grads.reshape(-1, chans)
    result = []
    for row_tap in range(3):
        for col_tap in range(3):
            piece = padded[:, row_tap : row_tap + rows, col_tap : col_tap + cols, :].reshape(
                -1, chans
            )
            result.append(inner(piece, flat_grads))
    return jnp.stack(result)


def shifted(values, offset):
    padded = jnp.pad(values, ((2 * DMAX, 2 * DMAX), (0, 0), (0, 0)))
    start = 2 * DMAX + offset
    return lax.dynamic_slice_in_dim(padded, start, values.shape[0], 0)


def temporal_forward(acts, kernel, step_size):
    chans = acts.shape[2]
    total = jnp.zeros((acts.shape[0] * acts.shape[1], chans), jnp.float32)
    for tap in range(5):
        piece = shifted(acts, (tap - 2) * step_size).reshape(-1, chans)
        total = total + jnp.dot(piece, kernel[tap], preferred_element_type=jnp.float32)
    return total.reshape(acts.shape)


def temporal_back(grads, kernel, step_size):
    chans = grads.shape[2]
    total = jnp.zeros((grads.shape[0] * grads.shape[1], chans), jnp.float32)
    for tap in range(5):
        piece = shifted(grads, (2 - tap) * step_size).reshape(-1, chans)
        total = total + jnp.dot(piece, kernel[tap].T, preferred_element_type=jnp.float32)
    return total.reshape(grads.shape)


def temporal_wgrad(acts, grads, step_size):
    chans = acts.shape[2]
    flat_grads = grads.reshape(-1, chans)
    return jnp.stack(
        [
            inner(shifted(acts, (tap - 2) * step_size).reshape(-1, chans), flat_grads)
            for tap in range(5)
        ]
    )


def to_pixels(flat):
    count = lax.axis_size(("seg", "grp"))
    chans = flat.shape[-1]
    strided = flat.reshape(-1, count, chans)
    return lax.all_to_all(strided, ("seg", "grp"), split_axis=1, concat_axis=1, tiled=True)


def to_frames(blocks):
    out = lax.all_to_all(blocks, ("seg", "grp"), split_axis=1, concat_axis=1, tiled=True)
    return out.reshape(1, -1, blocks.shape[-1])


def shifted1(values, offset):
    padded = jnp.pad(values, ((0, 0), (2 * DMAX, 2 * DMAX), (0, 0)))
    start = 2 * DMAX + offset
    return lax.dynamic_slice_in_dim(padded, start, values.shape[1], 1)


def temporal_forward1(acts, kernel, step_size):
    chans = acts.shape[2]
    total = jnp.zeros((acts.shape[0] * acts.shape[1], chans), jnp.float32)
    for tap in range(5):
        piece = shifted1(acts, (tap - 2) * step_size).reshape(-1, chans)
        total = total + jnp.dot(piece, kernel[tap], preferred_element_type=jnp.float32)
    return total.reshape(acts.shape)


def temporal_back1(grads, kernel, step_size):
    chans = grads.shape[2]
    total = jnp.zeros((grads.shape[0] * grads.shape[1], chans), jnp.float32)
    for tap in range(5):
        piece = shifted1(grads, (2 - tap) * step_size).reshape(-1, chans)
        total = total + jnp.dot(piece, kernel[tap].T, preferred_element_type=jnp.float32)
    return total.reshape(grads.shape)


def temporal_wgrad1(acts, grads, step_size):
    chans = acts.shape[2]
    flat_grads = grads.reshape(-1, chans)
    return jnp.stack(
        [
            inner(shifted1(acts, (tap - 2) * step_size).reshape(-1, chans), flat_grads)
            for tap in range(5)
        ]
    )


JB = 10


def shift_matrix(offset, size):
    rows = lax.broadcasted_iota(jnp.int32, (size, size), 0)
    cols = lax.broadcasted_iota(jnp.int32, (size, size), 1)
    return (cols == rows + offset).astype(jnp.bfloat16)


def shifted_taps(x_ref, step, sign):
    blocks, frames, chans = x_ref.shape
    wide = jnp.concatenate([x_ref[j] for j in range(blocks)], axis=1)
    taps = []
    for tap in range(5):
        if tap == 2:
            taps.append(None)
            continue
        moved = jnp.dot(
            shift_matrix(sign * (tap - 2) * step, frames), wide,
            preferred_element_type=jnp.float32,
        ).astype(jnp.bfloat16)
        taps.append(moved)
    rows = []
    for j in range(blocks):
        parts = []
        for tap in range(5):
            if tap == 2:
                parts.append(x_ref[j])
            else:
                parts.append(taps[tap][:, j * chans : (j + 1) * chans])
        rows.append(jnp.concatenate(parts, axis=1))
    return jnp.concatenate(rows, axis=0)


def tfwd_kernel(dil_ref, act_ref, w_ref, pre_ref, out_ref):
    blocks, frames, chans = act_ref.shape
    stacked = shifted_taps(act_ref, dil_ref[0], 1)
    pre = jnp.dot(stacked, w_ref[...], preferred_element_type=jnp.float32)
    pre_ref[...] = pre.reshape(blocks, frames, chans)
    out_ref[...] = (pre / (1.0 + jnp.exp(-pre))).astype(jnp.bfloat16).reshape(blocks, frames, chans)


def temporal_forward_k(acts, kernel, step_size):
    count, frames, chans = acts.shape
    spec = pl.BlockSpec((JB, frames, chans), lambda j, d: (j, 0, 0))
    return pl.pallas_call(
        tfwd_kernel,
        grid_spec=pltpu.PrefetchScalarGridSpec(
            num_scalar_prefetch=1,
            grid=(count // JB,),
            in_specs=[spec, pl.BlockSpec((5 * chans, chans), lambda j, d: (0, 0))],
            out_specs=[spec, spec],
        ),
        out_shape=[
            jax.ShapeDtypeStruct(acts.shape, jnp.float32),
            jax.ShapeDtypeStruct(acts.shape, jnp.bfloat16),
        ],
    )(step_size.reshape(1), acts, kernel.reshape(5 * chans, chans))


def tbwd_kernel(with_pre, dil_ref, act_ref, grad_ref, wt_ref, *rest):
    if with_pre:
        pre_ref, out_ref, tg_ref = rest
    else:
        out_ref, tg_ref = rest
    blocks, frames, chans = act_ref.shape
    stacked = shifted_taps(grad_ref, dil_ref[0], -1)
    grad_act = jnp.dot(stacked, wt_ref[...], preferred_element_type=jnp.float32)
    flat_act = act_ref[...].reshape(blocks * frames, chans)
    part = lax.dot_general(
        flat_act, stacked, (((0,), (0,)), ((), ())), preferred_element_type=jnp.float32
    )

    @pl.when(pl.program_id(0) == 0)
    def _():
        tg_ref[...] = jnp.zeros_like(tg_ref)

    tg_ref[...] += part
    if with_pre:
        pre = pre_ref[...].reshape(blocks * frames, chans)
        sigma = 1.0 / (1.0 + jnp.exp(-pre))
        grad_act = grad_act * (sigma * (1.0 + pre * (1.0 - sigma)))
    out_ref[...] = grad_act.astype(jnp.bfloat16).reshape(blocks, frames, chans)


def temporal_backward_k(acts, grads, kernel, step_size, pre_below):
    count, frames, chans = acts.shape
    spec = pl.BlockSpec((JB, frames, chans), lambda j, d: (j, 0, 0))
    wt = jnp.concatenate([kernel[tap].T for tap in range(5)], axis=0)
    with_pre = pre_below is not None
    in_specs = [spec, spec, pl.BlockSpec((5 * chans, chans), lambda j, d: (0, 0))]
    operands = [step_size.reshape(1), acts, grads, wt]
    if with_pre:
        in_specs.append(spec)
        operands.append(pre_below)
    out, tg = pl.pallas_call(
        functools.partial(tbwd_kernel, with_pre),
        grid_spec=pltpu.PrefetchScalarGridSpec(
            num_scalar_prefetch=1,
            grid=(count // JB,),
            in_specs=in_specs,
            out_specs=[spec, pl.BlockSpec((chans, 5 * chans), lambda j, d: (0, 0))],
        ),
        out_shape=[
            jax.ShapeDtypeStruct(acts.shape, jnp.bfloat16),
            jax.ShapeDtypeStruct((chans, 5 * chans), jnp.float32),
        ],
        compiler_params=pltpu.CompilerParams(dimension_semantics=("arbitrary",)),
    )(*operands)
    tgrad = tg.reshape(chans, 5, chans).transpose(1, 0, 2)
    return out, tgrad


def all_sum(parts, scale):
    flat = jnp.concatenate([p.reshape(-1) for p in parts])
    count = lax.axis_size(("seg", "grp"))
    chunk = flat.shape[0] // count
    pieces = lax.all_to_all(
        flat.reshape(count, chunk), ("seg", "grp"), split_axis=0, concat_axis=0, tiled=True
    )
    mine = jnp.sum(pieces, axis=0) * scale
    spread = jnp.broadcast_to(mine[None], (count, chunk))
    whole = lax.all_to_all(spread, ("seg", "grp"), split_axis=0, concat_axis=0, tiled=True)
    whole = whole.reshape(-1)
    out = []
    offset = 0
    for p in parts:
        out.append(whole[offset : offset + p.size].reshape(p.shape))
        offset += p.size
    return out


def local(
    frames_in, spatial_weight, temporal_weight, uniting_weight, key_index, dilation, cotangent
):
    local_frames, rows, cols, chans = frames_in.shape
    pixels = rows * cols
    seg_count = lax.axis_size("seg")
    pre_spatial = spatial_forward(frames_in, spatial_weight)
    act_zero = jax.nn.silu(pre_spatial).astype(jnp.bfloat16).reshape(local_frames, pixels, chans)
    cot_local = cotangent.reshape(local_frames, pixels, chans)
    act_blocks = to_pixels(act_zero)
    cot_blocks = to_pixels(cot_local)
    acts = [act_blocks]
    block, total_frames = act_blocks.shape[0], act_blocks.shape[1]
    seg_frames = total_frames // seg_count
    pres = []
    for layer in range(LAYERS):
        pre, act = temporal_forward_k(acts[-1], temporal_weight[layer], dilation[layer])
        pres.append(pre)
        acts.append(act)
    feat = acts[-1]
    seg_shape = (block, seg_count, seg_frames, chans)
    feat_seg = feat.reshape(seg_shape)
    positions = jnp.arange(seg_frames, dtype=jnp.int32)
    onehot = positions[None, :] == key_index[:, None]
    keys = jnp.einsum(
        "ns,jnsc->jnc", onehot.astype(jnp.bfloat16), feat_seg, preferred_element_type=jnp.float32
    ).astype(jnp.bfloat16)
    key_full = jnp.broadcast_to(keys[:, :, None], seg_shape).reshape(-1, chans)
    feat_flat = feat.reshape(-1, chans)
    key_part = jnp.dot(
        keys.reshape(-1, chans), uniting_weight[1], preferred_element_type=jnp.float32
    ).reshape(block, seg_count, 1, chans)
    main_part = jnp.dot(feat_flat, uniting_weight[0], preferred_element_type=jnp.float32)
    united_blocks = (main_part.reshape(seg_shape) + key_part).astype(jnp.bfloat16)
    united = to_frames(united_blocks.reshape(block, total_frames, chans))
    cot_flat = cot_blocks.reshape(-1, chans)
    grad_feat = jnp.dot(cot_flat, uniting_weight[0].T, preferred_element_type=jnp.float32)
    seg_cot = jnp.sum(cot_blocks.reshape(seg_shape).astype(jnp.float32), axis=2)
    key_term = jnp.dot(
        seg_cot.reshape(-1, chans),
        uniting_weight[1].T.astype(jnp.float32),
        precision=lax.Precision.HIGHEST,
    ).reshape(block, seg_count, 1, chans)
    placed = onehot.astype(jnp.float32)[None, :, :, None] * key_term
    grad_feat = grad_feat.reshape(seg_shape) + placed
    grad_feat = grad_feat.reshape(block, total_frames, chans)
    grad_uniting = jnp.stack([inner(feat_flat, cot_flat), inner(key_full, cot_flat)])
    grad_pre = (grad_feat * silu_grad(pres[-1])).astype(jnp.bfloat16)
    tgrads = [None] * LAYERS
    for layer in range(LAYERS - 1, -1, -1):
        below = pres[layer - 1] if layer > 0 else None
        grad_pre, tgrads[layer] = temporal_backward_k(
            acts[layer], grad_pre, temporal_weight[layer], dilation[layer], below
        )
    grad_act0 = grad_pre
    grad_time = to_frames(grad_act0).reshape(frames_in.shape)
    grad_spre = (grad_time.astype(jnp.float32) * silu_grad(pre_spatial)).astype(jnp.bfloat16)
    grad_frames = spatial_back(grad_spre, spatial_weight).astype(jnp.bfloat16)
    grad_spatial = spatial_wgrad(frames_in, grad_spre)
    scale = 1.0 / jnp.sqrt(jnp.float32(total_frames * pixels))
    summed = all_sum((grad_spatial, jnp.stack(tgrads), grad_uniting), scale)
    return (
        united.reshape(frames_in.shape),
        grad_frames,
        summed[0],
        summed[1],
        summed[2],
    )


def solution(mesh):
    placed = (
        P(("seg", "grp"), None, None, None),
        P(),
        P(),
        P(),
        P(),
        P(),
        P(("seg", "grp"), None, None, None),
    )
    return jax.shard_map(
        local,
        mesh=mesh,
        in_specs=placed,
        out_specs=(
            P(("seg", "grp"), None, None, None),
            P(("seg", "grp"), None, None, None),
            P(),
            P(),
            P(),
        ),
        check_vma=False,
    )
```

profile of v0, /device:TPU:1, one launch (start us, length us, event | category | flops | bytes accessed | tf_op | source)
XLA Modules:
  0.0 225.2 jit_solution(10083172729911460202)
XLA Ops:
  0.6 2.9 %copy.118 = bf16[30,128,128]{2,0,1:T(8,128)(2,1)} copy(bf16[30,128,128]{2,1,0:T(8,128)(2,1)} %bitcast.324) | data formatting | bytes 1966080 | tf_op jit(solution)/shard_map/reshape;reshape | solution.py:112
  3.5 11.5 %all-to-all-start.2 = ((bf16[30,128,128]{2,0,1:T(8,128)(2,1)}), bf16[30,128,128]{2,0,1:T(8,128)(2,1)S(1)}, u32[]{:S(2)}, u32[]{:S(2)}) async-start(bf16[30,128,128]{2,0,1:T(8,128)(2,1)} %copy.118), calls=%async_computation.2 | async-start | bytes 2097152 | tf_op jit(solution)/shard_map/all_to_all | solution.py:113
  15.1 2.5 %pad_slice_fusion.8 = (bf16[1,32,120,128]{3,2,1,0:T(8,128)(2,1)S(1)}, bf16[1,32,120,128]{3,2,1,0:T(8,128)(2,1)S(1)}, bf16[1,32,120,128]{3,2,1,0:T(8,128)(2,1)S(1...) fusion(bf16[1,32,120,128]{3,2,1,0:T(8,128)(2,1)S(1)} %copy-done.2), kind=kLoop, calls=%fused_computation.70 | loop fusion | bytes 8847360 | tf_op jit(solution)/shard_map/slice | solution.py:36
  34.6 2.8 %copy.114 = bf16[30,128,128]{2,0,1:T(8,128)(2,1)} copy(bf16[30,128,128]{2,1,0:T(8,128)(2,1)} %multiply_convert_fusion.2) | data formatting | bytes 1966080 | tf_op jit(solution)/shard_map/convert_element_type | solution.py:295
  48.9 10.2 %all-to-all-start = ((bf16[30,128,128]{2,0,1:T(8,128)(2,1)}), bf16[30,128,128]{2,0,1:T(8,128)(2,1)}, u32[]{:S(2)}, u32[]{:S(2)}) async-start(bf16[30,128,128]{2,0,1:T(8,128)(2,1)} %copy.114), calls=%async_computation | async-start | bytes 2097152 | tf_op jit(solution)/shard_map/all_to_all | solution.py:113
  63.3 14.4 %all-to-all-done = bf16[30,128,128]{2,0,1:T(8,128)(2,1)} async-done(((bf16[30,128,128]{2,0,1:T(8,128)(2,1)}), bf16[30,128,128]{2,0,1:T(8,128)(2,1)}, u32[]{:S(2)}, u32[]{:S(2)}) %all-to-all-start) | async-done | bytes 983072 | tf_op jit(solution)/shard_map/all_to_all | solution.py:113
  77.7 2.6 %copy.115.act_ref = bf16[30,128,128]{2,1,0:T(8,128)(2,1)} copy(bf16[30,128,128]{2,0,1:T(8,128)(2,1)} %all-to-all-done) | data formatting | bytes 1966080 | tf_op jit(solution)/shard_map/all_to_all | solution.py:113
  80.3 5.6 %shard_map.110 = (f32[30,128,128]{2,1,0:T(8,128)}, bf16[30,128,128]{2,1,0:T(8,128)(2,1)}) custom-call(s32[1]{0:T(128)} %get-tuple-element.53.dil_ref, bf16[30,128,128]{2,1,0:T(8,128)(2,1)} %copy.115.act_ref, bf16[640,128]{1,0:T(8,128)(2,1)} %bitcast.329), custom_call_target="tpu_custom_call" | custom-call | tf_op jit(solution)/shard_map/pallas_call | solution.py:201
  85.9 5.8 %shard_map.111 = (f32[30,128,128]{2,1,0:T(8,128)}, bf16[30,128,128]{2,1,0:T(8,128)(2,1)}) custom-call(s32[1]{0:T(128)} %get-tuple-element.54.dil_ref, bf16[30,128,128]{2,1,0:T(8,128)(2,1)} %get-tuple-element.13.act_ref, bf16[640,128]{1,0:T(8,128)(2,1)} %bitcast.328), custom_call_target="tpu_custom_call" | custom-call | tf_op jit(solution)/shard_map/pallas_call | solution.py:201
  95.0 7.4 %shard_map.112 = (bf16[30,128,128]{2,1,0:T(8,128)(2,1)}, f32[128,640]{1,0:T(8,128)}) custom-call(s32[1]{0:T(128)} %get-tuple-element.54.dil_ref, bf16[30,128,128]{2,1,0:T(8,128)(2,1)} %get-tuple-element.13.act_ref, bf16[30,128,128]{2,1,0:T(8,128)(2,1)} %fusion.2.grad_ref, bf16[640,128]{1,0:T(8,128)(2,1)} %copy-done.17, f32[30,128,128]{2,1,0:T(8,128)} %get-tuple-element.16.rest_0_), custom_call_target="tpu_custom_call" | custom-call | tf_op jit(solution)/shard_map/pallas_call | solution.py:251
  102.3 6.4 %shard_map.113 = (bf16[30,128,128]{2,1,0:T(8,128)(2,1)}, f32[128,640]{1,0:T(8,128)}) custom-call(s32[1]{0:T(128)} %get-tuple-element.53.dil_ref, bf16[30,128,128]{2,1,0:T(8,128)(2,1)} %copy.115.act_ref, bf16[30,128,128]{2,1,0:T(8,128)(2,1)} %get-tuple-element.17.grad_ref, bf16[640,128]{1,0:T(8,128)(2,1)} %constant_dynamic-update-slice_fusion.5.wt_ref), custom_call_target="tpu_custom_call" | custom-call | tf_op jit(solution)/shard_map/pallas_call | solution.py:251
  108.7 2.8 %copy.131 = bf16[30,128,128]{2,0,1:T(8,128)(2,1)} copy(bf16[30,128,128]{2,1,0:T(8,128)(2,1)} %get-tuple-element.18) | data formatting | bytes 1966080 | tf_op jit(solution)/shard_map/pallas_call | solution.py:251
  111.5 4.8 %all-to-all-start.3 = ((bf16[30,128,128]{2,0,1:T(8,128)(2,1)}), bf16[30,128,128]{2,0,1:T(8,128)(2,1)}, u32[]{:S(2)}, u32[]{:S(2)}) async-start(bf16[30,128,128]{2,0,1:T(8,128)(2,1)} %copy.131), calls=%async_computation.3 | async-start | bytes 2097152 | tf_op jit(solution)/shard_map/all_to_all | solution.py:117
  122.0 2.2 copy.136
  129.1 5.9 %all-to-all-done.3 = bf16[30,128,128]{2,0,1:T(8,128)(2,1)} async-done(((bf16[30,128,128]{2,0,1:T(8,128)(2,1)}), bf16[30,128,128]{2,0,1:T(8,128)(2,1)}, u32[]{:S(2)}, u32[]{:S(2)}) %all-to-all-start.3) | async-done | bytes 983072 | tf_op jit(solution)/shard_map/all_to_all | solution.py:117
  135.0 4.4 %all-to-all-start.1 = ((bf16[30,128,128]{2,0,1:T(8,128)(2,1)}), bf16[30,128,128]{2,0,1:T(8,128)(2,1)S(1)}, u32[]{:S(2)}, u32[]{:S(2)}) async-start(bf16[30,128,128]{2,0,1:T(8,128)(2,1)} %copy.116), calls=%async_computation.1 | async-start | bytes 2097152 | tf_op jit(solution)/shard_map/all_to_all | solution.py:117
  139.4 2.1 multiply_convert_fusion
  149.4 3.3 %pad_slice_fusion = (bf16[1,32,120,128]{3,2,1,0:T(8,128)(2,1)}, bf16[1,32,120,128]{3,2,1,0:T(8,128)(2,1)S(1)}, bf16[1,32,120,128]{3,2,1,0:T(8,128)(2,1)S(1)}, bf...) fusion(bf16[1,32,120,128]{3,2,1,0:T(8,128)(2,1)S(1)} %multiply_, ...), kind=kLoop, calls=%fused_computation.62 | loop fusion | bytes 8847360 | tf_op jit(solution)/shard_map/slice | solution.py:51
  157.6 2.4 %convolution_add_fusion.5 = f32[3840,128]{1,0:T(8,128)} fusion(f32[3840,128]{1,0:T(8,128)S(1)} %convolution_add_fusion.6, bf16[3840,128]{1,0:T(8,128)(2,1)S(1)} %bitcast.298, bf16[9,128,128]{2,1,0:T(8,128)(2,1)} %param.8), kind=kOutput, calls=%fused_computation.5 | convolution fusion | flops 126320640 | bytes 4947968 | tf_op jit(solution)/shard_map/dot_general | solution.py:54
  161.0 9.8 %all-to-all-start.4 = ((f32[128,1,2688]{2,1,0:T(1,128)}), f32[128,1,2688]{2,1,0:T(1,128)S(1)}, u32[]{:S(2)}, u32[]{:S(2)}) async-start(f32[128,1,2688]{2,1,0:T(1,128)} %bitcast.112), calls=%async_computation.4 | async-start | bytes 2752512 | tf_op jit(solution)/shard_map/all_to_all | solution.py:273
  170.8 2.7 %copy.117 = bf16[30,128,128]{2,1,0:T(8,128)(2,1)} copy(bf16[30,128,128]{2,0,1:T(8,128)(2,1)} %copy-done.6) | data formatting | bytes 1966080 | tf_op jit(solution)/shard_map/all_to_all | solution.py:117
  176.2 17.1 %all-to-all-done.4 = f32[128,1,2688]{2,1,0:T(1,128)S(1)} async-done(((f32[128,1,2688]{2,1,0:T(1,128)}), f32[128,1,2688]{2,1,0:T(1,128)S(1)}, u32[]{:S(2)}, u32[]{:S(2)}) %all-to-all-start.4) | async-done | bytes 1376288 | tf_op jit(solution)/shard_map/all_to_all | solution.py:273
  196.0 4.3 %all-to-all-start.5 = ((f32[128,1,2688]{2,1,0:T(1,128)}), f32[128,1,2688]{2,1,0:T(1,128)S(1)}, u32[]{:S(2)}, u32[]{:S(2)}) async-start(f32[128,1,2688]{2,1,0:T(1,128)} %broadcast_in_dim.5), calls=%async_computation.5 | async-start | bytes 2752512 | tf_op jit(solution)/shard_map/all_to_all | solution.py:278
  206.7 16.1 %all-to-all-done.5 = f32[128,1,2688]{2,1,0:T(1,128)S(1)} async-done(((f32[128,1,2688]{2,1,0:T(1,128)}), f32[128,1,2688]{2,1,0:T(1,128)S(1)}, u32[]{:S(2)}, u32[]{:S(2)}) %all-to-all-start.5) | async-done | bytes 1376288 | tf_op jit(solution)/shard_map/all_to_all | solution.py:278
  (121 shorter events, 73.9 us)
Async XLA Ops:
  0.6 14.4 %copy-start.2 = (bf16[1,32,120,128]{3,2,1,0:T(8,128)(2,1)S(1)}, bf16[1,32,120,128]{3,2,1,0:T(8,128)(2,1)}, u32[]{:S(2)}) copy-start(bf16[1,32,120,128]{3,2,1,0:T(8,128)(2,1)} %param.7) | copy-start | bytes 2949124
  3.5 45.4 %all-to-all-start.2 = ((bf16[30,128,128]{2,0,1:T(8,128)(2,1)}), bf16[30,128,128]{2,0,1:T(8,128)(2,1)S(1)}, u32[]{:S(2)}, u32[]{:S(2)}) async-start(bf16[30,128,128]{2,0,1:T(8,128)(2,1)} %copy.118), calls=%async_computation.2 | async-start | bytes 2097152 | tf_op jit(solution)/shard_map/all_to_all | solution.py:113
  15.1 2.5 %copy-start.15 = (bf16[9,128,128]{2,1,0:T(8,128)(2,1)S(1)}, bf16[9,128,128]{2,1,0:T(8,128)(2,1)}, u32[]{:S(2)}) copy-start(bf16[9,128,128]{2,1,0:T(8,128)(2,1)} %param.8) | copy-start | bytes 884740
  21.2 1.5 copy-start.14
  21.3 13.2 %copy-start.20 = (s32[8]{0:T(128)S(1)}, s32[8]{0:T(128)}, u32[]{:S(2)}) copy-start(s32[8]{0:T(128)} %param.11) | copy-start | bytes 100
  34.6 24.6 %copy-start.19 = (s32[2]{0:T(128)S(1)}, s32[2]{0:T(128)}, u32[]{:S(2)}) copy-start(s32[2]{0:T(128)} %param.12) | copy-start | bytes 28
  44.8 2.7 %copy-start.17 = (bf16[640,128]{1,0:T(8,128)(2,1)}, bf16[640,128]{1,0:T(8,128)(2,1)S(1)}, u32[]{:S(2)}) copy-start(bf16[640,128]{1,0:T(8,128)(2,1)S(1)} %constant_dynamic-update-slice_fusion.wt_ref) | copy-start | bytes 491524
  48.9 10.9 %copy-start.18 = (bf16[1,1,128,128]{2,3,1,0:T(8,128)(2,1)S(1)}, bf16[1,1,128,128]{2,3,1,0:T(8,128)(2,1)}, u32[]{:S(2)}) copy-start(bf16[1,1,128,128]{2,3,1,0:T(8,128)(2,1)} %copy.158) | copy-start | bytes 98308
  48.9 14.2 %copy-start.16 = (bf16[2,128,128]{2,1,0:T(8,128)(2,1)S(1)}, bf16[2,128,128]{2,1,0:T(8,128)(2,1)}, u32[]{:S(2)}) copy-start(bf16[2,128,128]{2,1,0:T(8,128)(2,1)} %param.10) | copy-start | bytes 196612
  48.9 11.5 %copy-start.5 = (bf16[30,128,128]{2,0,1:T(8,128)(2,1)}, bf16[30,128,128]{2,0,1:T(8,128)(2,1)S(1)}, u32[]{:S(2)}) copy-start(bf16[30,128,128]{2,0,1:T(8,128)(2,1)S(1)} %all-to-all-done.2) | copy-start | bytes 2949124
  48.9 28.8 %all-to-all-start = ((bf16[30,128,128]{2,0,1:T(8,128)(2,1)}), bf16[30,128,128]{2,0,1:T(8,128)(2,1)}, u32[]{:S(2)}, u32[]{:S(2)}) async-start(bf16[30,128,128]{2,0,1:T(8,128)(2,1)} %copy.114), calls=%async_computation | async-start | bytes 2097152 | tf_op jit(solution)/shard_map/all_to_all | solution.py:113
  91.7 1.5 copy-start.12
  111.5 23.5 %all-to-all-start.3 = ((bf16[30,128,128]{2,0,1:T(8,128)(2,1)}), bf16[30,128,128]{2,0,1:T(8,128)(2,1)}, u32[]{:S(2)}, u32[]{:S(2)}) async-start(bf16[30,128,128]{2,0,1:T(8,128)(2,1)} %copy.131), calls=%async_computation.3 | async-start | bytes 2097152 | tf_op jit(solution)/shard_map/all_to_all | solution.py:117
  119.4 1.7 copy-start.13
  135.0 25.0 %all-to-all-start.1 = ((bf16[30,128,128]{2,0,1:T(8,128)(2,1)}), bf16[30,128,128]{2,0,1:T(8,128)(2,1)S(1)}, u32[]{:S(2)}, u32[]{:S(2)}) async-start(bf16[30,128,128]{2,0,1:T(8,128)(2,1)} %copy.116), calls=%async_computation.1 | async-start | bytes 2097152 | tf_op jit(solution)/shard_map/all_to_all | solution.py:117
  139.4 2.1 copy-start.3
  147.3 1.3 copy-start
  161.0 32.3 %all-to-all-start.4 = ((f32[128,1,2688]{2,1,0:T(1,128)}), f32[128,1,2688]{2,1,0:T(1,128)S(1)}, u32[]{:S(2)}, u32[]{:S(2)}) async-start(f32[128,1,2688]{2,1,0:T(1,128)} %bitcast.112), calls=%async_computation.4 | async-start | bytes 2752512 | tf_op jit(solution)/shard_map/all_to_all | solution.py:273
  170.8 2.7 %copy-start.1 = (f32[30,128,128]{2,1,0:T(8,128)S(1)}, f32[30,128,128]{2,1,0:T(8,128)}, u32[]{:S(2)}) copy-start(f32[30,128,128]{2,1,0:T(8,128)} %copy-done) | copy-start | bytes 5898244
  173.5 1.5 copy-start.4
  196.0 26.9 %all-to-all-start.5 = ((f32[128,1,2688]{2,1,0:T(1,128)}), f32[128,1,2688]{2,1,0:T(1,128)S(1)}, u32[]{:S(2)}, u32[]{:S(2)}) async-start(f32[128,1,2688]{2,1,0:T(1,128)} %broadcast_in_dim.5), calls=%async_computation.5 | async-start | bytes 2752512 | tf_op jit(solution)/shard_map/all_to_all | solution.py:278
  200.3 1.7 copy-start.8
  202.0 1.3 copy-start.7
  203.3 1.3 copy-start.10
  (3 other events, 3.4 us)
where the time goes:
time: 228 us; the launch traced here: 225 us
  local copies, waits for them, and re-layouts  61 us (27%)
  waiting for transfers between devices  53.6 us (24%)
  starting transfers between devices  45 us (20%)
  matrix products  26.1 us (11%)
  Pallas kernels  25.2 us (11%)
  other arithmetic  13.2 us (6%)
    unnamed x60, local copies, waits for them, and re-layouts  26.6 us
    all_to_all x2, starting transfers between devices, to_pixels(): lax.all_to_all(strided, ('seg', 'grp'), split_axis=1, concat_axis=1, tile...  21.7 us
    all_to_all x1, waiting for transfers between devices, all_sum(): lax.all_to_all(flat.reshape(count, chunk), ('seg', 'grp'), split_axis=0,...  17.1 us
    all_to_all x1, waiting for transfers between devices, all_sum(): lax.all_to_all(spread, ('seg', 'grp'), split_axis=0, concat_axis=0, tiled...  16.1 us
    all_to_all x2, waiting for transfers between devices, to_pixels(): lax.all_to_all(strided, ('seg', 'grp'), split_axis=1, concat_axis=1, tile...  14.4 us
    pallas_call x2, Pallas kernels, temporal_backward_k(): pl.pallas_call(functools.partial(tbwd_kernel, with_pre), grid_spec=pltpu....  13.7 us
    dot_general x9, matrix products, spatial_back(): jnp.dot(piece, kernel[3 * row_tap + col_tap].T, preferred_element_type=jn...  13.5 us
    pallas_call x2, Pallas kernels, temporal_forward_k(): pl.pallas_call(tfwd_kernel, grid_spec=pltpu.PrefetchScalarGridSpec(num_sc...  11.5 us
  transfers between devices with their start and end apart: 6, of which 4 were waited for; matrix products, arithmetic and copies ran while one was open for 36% of the time, Pallas kernels for 0%

commit v1 on v0

--- a/solution.py
+++ b/solution.py
@@ -340,18 +340,19 @@
             acts[layer], grad_pre, temporal_weight[layer], dilation[layer], below
         )
     grad_act0 = grad_pre
+    scale = 1.0 / jnp.sqrt(jnp.float32(total_frames * pixels))
+    early = lax.psum((jnp.stack(tgrads), grad_uniting), ("seg", "grp"))
     grad_time = to_frames(grad_act0).reshape(frames_in.shape)
     grad_spre = (grad_time.astype(jnp.float32) * silu_grad(pre_spatial)).astype(jnp.bfloat16)
     grad_frames = spatial_back(grad_spre, spatial_weight).astype(jnp.bfloat16)
     grad_spatial = spatial_wgrad(frames_in, grad_spre)
-    scale = 1.0 / jnp.sqrt(jnp.float32(total_frames * pixels))
-    summed = all_sum((grad_spatial, jnp.stack(tgrads), grad_uniting), scale)
+    (summed,) = all_sum((grad_spatial,), scale)
     return (
         united.reshape(frames_in.shape),
         grad_frames,
-        summed[0],
-        summed[1],
-        summed[2],
+        summed,
+        early[0] * scale,
+        early[1] * scale,
     )
 
 

time: 228 us -> 361 us (1.58)
  waiting for transfers between devices: 53.6 us -> 188 us
  between operations: 1.11 us -> 14.5 us
  local copies, waits for them, and re-layouts: 61 us -> 52.3 us
  matrix products: 26.1 us -> 19 us
    psum x0 -> x1, waiting for transfers between devices: none -> 148 us  [local(): early = lax.psum((jnp.stack(tgrads), grad_uniting), ('seg', 'grp'))]
    dot_general x9, matrix products: 13.5 us -> 6.28 us  [spatial_back(): jnp.dot(piece, kernel[3 * row_tap + col_tap].T, preferred_element_type=jn...]
    all_to_all x1, waiting for transfers between devices: 17.1 us -> 11 us  [all_sum(): lax.all_to_all(flat.reshape(count, chunk), ('seg', 'grp'), split_axis=0,...]
    all_to_all x1, waiting for transfers between devices: 16.1 us -> 10.8 us  [all_sum(): lax.all_to_all(spread, ('seg', 'grp'), split_axis=0, concat_axis=0, tiled...]
  transfers between devices with their start and end apart: 6 -> 7, of which waited for: 4 -> 5; matrix products, arithmetic and copies ran while one was open for 36% -> 19% of each run, Pallas kernels for 0% -> 0%
where the time goes in v1:
time: 361 us; the launch traced here: 359 us
  waiting for transfers between devices  188 us (52%)
  local copies, waits for them, and re-layouts  52.3 us (14%)
  starting transfers between devices  43.9 us (12%)
  Pallas kernels  25.2 us (7%)
  matrix products  19 us (5%)
  other arithmetic  16.1 us (4%)
  between operations  14.5 us (4%)
    psum x1, waiting for transfers between devices, local(): early = lax.psum((jnp.stack(tgrads), grad_uniting), ('seg', 'grp'))  148 us
    unnamed x60, local copies, waits for them, and re-layouts  25.9 us
    all_to_all x2, starting transfers between devices, to_pixels(): lax.all_to_all(strided, ('seg', 'grp'), split_axis=1, concat_axis=1, tile...  21.7 us
    all_to_all x2, waiting for transfers between devices, to_pixels(): lax.all_to_all(strided, ('seg', 'grp'), split_axis=1, concat_axis=1, tile...  14.5 us
    pallas_call x2, Pallas kernels, temporal_backward_k(): pl.pallas_call(functools.partial(tbwd_kernel, with_pre), grid_spec=pltpu....  13.7 us
    all_to_all x2, starting transfers between devices, to_frames(): lax.all_to_all(blocks, ('seg', 'grp'), split_axis=1, concat_axis=1, tiled...  11.4 us
    pallas_call x2, Pallas kernels, temporal_forward_k(): pl.pallas_call(tfwd_kernel, grid_spec=pltpu.PrefetchScalarGridSpec(num_sc...  11.4 us
    all_to_all x1, waiting for transfers between devices, all_sum(): lax.all_to_all(flat.reshape(count, chunk), ('seg', 'grp'), split_axis=0,...  11 us
  transfers between devices with their start and end apart: 7, of which 5 were waited for; matrix products, arithmetic and copies ran while one was open for 19% of the time, Pallas kernels for 0%

profile of v1, /device:TPU:1, one launch (start us, length us, event | category | flops | bytes accessed | tf_op | source)
XLA Modules:
  0.0 358.7 jit_solution(2727249399601883369)
XLA Ops:
  7.2 2.9 copy.69
  10.1 11.5 %all-to-all-start.2 = ((bf16[30,128,128]{2,0,1:T(8,128)(2,1)}), bf16[30,128,128]{2,0,1:T(8,128)(2,1)S(1)}, u32[]{:S(2)}, u32[]{:S(2)}) async-start(bf16[30,128,128]{2,0,1:T(8,128)(2,1)} %copy.69), calls=%async_computation.2 | async-start | bytes 2097152 | tf_op jit(solution)/shard_map/all_to_all | solution.py:113
  21.6 2.5 pad_slice_fusion.8
  41.0 2.8 copy.65
  55.3 10.2 %all-to-all-start = ((bf16[30,128,128]{2,0,1:T(8,128)(2,1)}), bf16[30,128,128]{2,0,1:T(8,128)(2,1)}, u32[]{:S(2)}, u32[]{:S(2)}) async-start(bf16[30,128,128]{2,0,1:T(8,128)(2,1)} %copy.65), calls=%async_computation | async-start | bytes 2097152 | tf_op jit(solution)/shard_map/all_to_all | solution.py:113
  67.5 1.9 convert_reduce_fusion
  69.7 14.5 %all-to-all-done = bf16[30,128,128]{2,0,1:T(8,128)(2,1)} async-done(((bf16[30,128,128]{2,0,1:T(8,128)(2,1)}), bf16[30,128,128]{2,0,1:T(8,128)(2,1)}, u32[]{:S(2)}, u32[]{:S(2)}) %all-to-all-start) | async-done | bytes 983072 | tf_op jit(solution)/shard_map/all_to_all | solution.py:113
  84.2 2.6 copy.66.act_ref
  86.7 5.8 %shard_map.110 = (f32[30,128,128]{2,1,0:T(8,128)}, bf16[30,128,128]{2,1,0:T(8,128)(2,1)}) custom-call(s32[1]{0:T(128)} %get-tuple-element.70.dil_ref, bf16[30,128,128]{2,1,0:T(8,128)(2,1)} %copy.66.act_ref, bf16[640,128]{1,0:T(8,128)(2,1)} %bitcast.320), custom_call_target="tpu_custom_call" | custom-call | tf_op jit(solution)/shard_map/pallas_call | solution.py:201
  92.5 5.7 %shard_map.111 = (f32[30,128,128]{2,1,0:T(8,128)}, bf16[30,128,128]{2,1,0:T(8,128)(2,1)}) custom-call(s32[1]{0:T(128)} %get-tuple-element.71.dil_ref, bf16[30,128,128]{2,1,0:T(8,128)(2,1)} %get-tuple-element.13.act_ref, bf16[640,128]{1,0:T(8,128)(2,1)} %bitcast.319), custom_call_target="tpu_custom_call" | custom-call | tf_op jit(solution)/shard_map/pallas_call | solution.py:201
  101.4 7.3 %shard_map.112 = (bf16[30,128,128]{2,1,0:T(8,128)(2,1)}, f32[128,640]{1,0:T(8,128)}) custom-call(s32[1]{0:T(128)} %get-tuple-element.71.dil_ref, bf16[30,128,128]{2,1,0:T(8,128)(2,1)} %get-tuple-element.13.act_ref, bf16[30,128,128]{2,1,0:T(8,128)(2,1)} %fusion.2.grad_ref, bf16[640,128]{1,0:T(8,128)(2,1)} %copy-done.15, f32[30,128,128]{2,1,0:T(8,128)} %get-tuple-element.16.rest_0_), custom_call_target="tpu_custom_call" | custom-call | tf_op jit(solution)/shard_map/pallas_call | solution.py:251
  108.6 6.5 %shard_map.113 = (bf16[30,128,128]{2,1,0:T(8,128)(2,1)}, f32[128,640]{1,0:T(8,128)}) custom-call(s32[1]{0:T(128)} %get-tuple-element.70.dil_ref, bf16[30,128,128]{2,1,0:T(8,128)(2,1)} %copy.66.act_ref, bf16[30,128,128]{2,1,0:T(8,128)(2,1)} %get-tuple-element.17.grad_ref, bf16[640,128]{1,0:T(8,128)(2,1)} %constant_dynamic-update-slice_fusion.5.wt_ref), custom_call_target="tpu_custom_call" | custom-call | tf_op jit(solution)/shard_map/pallas_call | solution.py:251
  116.3 1.9 copy.87
  121.9 4.8 %all-to-all-start.3 = ((bf16[30,128,128]{2,0,1:T(8,128)(2,1)}), bf16[30,128,128]{2,0,1:T(8,128)(2,1)}, u32[]{:S(2)}, u32[]{:S(2)}) async-start(bf16[30,128,128]{2,0,1:T(8,128)(2,1)} %copy.82), calls=%async_computation.3 | async-start | bytes 2097152 | tf_op jit(solution)/shard_map/all_to_all | solution.py:117
  133.4 147.7 %all-reduce.5.cloned.1.call-done = (f32[2,5,128,128]{2,3,1,0:T(8,128)}, f32[2,128,128]{2,1,0:T(8,128)}) async-done(((f32[2,5,128,128]{2,3,1,0:T(8,128)}, f32[2,128,128]{2,1,0:T(8,128)}), (f32[2,5,128,128]{2,3,1,0:T(8,128)}, f32[2,128,128]{2,1,0:T(8,128)})) %all-reduce.5.cloned.1.call-update) | async-done | bytes 786448 | tf_op jit(solution)/shard_map/psum | solution.py:344
  284.0 6.6 %all-to-all-start.1 = ((bf16[30,128,128]{2,0,1:T(8,128)(2,1)}), bf16[30,128,128]{2,0,1:T(8,128)(2,1)S(1)}, u32[]{:S(2)}, u32[]{:S(2)}) async-start(bf16[30,128,128]{2,0,1:T(8,128)(2,1)} %copy.67), calls=%async_computation.1 | async-start | bytes 2097152 | tf_op jit(solution)/shard_map/all_to_all | solution.py:117
  290.6 2.1 multiply_convert_fusion
  299.1 3.3 pad_slice_fusion
  305.9 3.7 %all-to-all-done.1 = bf16[30,128,128]{2,0,1:T(8,128)(2,1)S(1)} async-done(((bf16[30,128,128]{2,0,1:T(8,128)(2,1)}), bf16[30,128,128]{2,0,1:T(8,128)(2,1)S(1)}, u32[]{:S(2)}, u32[]{:S(2)}) %all-to-all-start.1) | async-done | bytes 983072 | tf_op jit(solution)/shard_map/all_to_all | solution.py:117
  309.6 6.5 %all-to-all-start.4 = ((f32[128,1,1152]{2,1,0:T(1,128)}), f32[128,1,1152]{2,1,0:T(1,128)}, u32[]{:S(2)}, u32[]{:S(2)}) async-start(f32[128,1,1152]{2,1,0:T(1,128)} %bitcast.321), calls=%async_computation.4 | async-start | bytes 1179648 | tf_op jit(solution)/shard_map/all_to_all | solution.py:273
  319.0 11.0 %all-to-all-done.4 = f32[128,1,1152]{2,1,0:T(1,128)} async-done(((f32[128,1,1152]{2,1,0:T(1,128)}), f32[128,1,1152]{2,1,0:T(1,128)}, u32[]{:S(2)}, u32[]{:S(2)}) %all-to-all-start.4) | async-done | bytes 589856 | tf_op jit(solution)/shard_map/all_to_all | solution.py:273
  332.6 4.2 %all-to-all-start.5 = ((f32[128,1,1152]{2,1,0:T(1,128)}), f32[128,1,1152]{2,1,0:T(1,128)S(1)}, u32[]{:S(2)}, u32[]{:S(2)}) async-start(f32[128,1,1152]{2,1,0:T(1,128)} %broadcast_in_dim.4), calls=%async_computation.5 | async-start | bytes 1179648 | tf_op jit(solution)/shard_map/all_to_all | solution.py:278
  338.1 2.1 fusion
  340.2 10.8 %all-to-all-done.5 = f32[128,1,1152]{2,1,0:T(1,128)S(1)} async-done(((f32[128,1,1152]{2,1,0:T(1,128)}), f32[128,1,1152]{2,1,0:T(1,128)S(1)}, u32[]{:S(2)}, u32[]{:S(2)}) %all-to-all-start.5) | async-done | bytes 589856 | tf_op jit(solution)/shard_map/all_to_all | solution.py:278
  (121 shorter events, 65.3 us)
Async XLA Ops:
  7.2 14.4 %copy-start = (bf16[1,32,120,128]{3,2,1,0:T(8,128)(2,1)S(1)}, bf16[1,32,120,128]{3,2,1,0:T(8,128)(2,1)}, u32[]{:S(2)}) copy-start(bf16[1,32,120,128]{3,2,1,0:T(8,128)(2,1)} %param.7) | copy-start | bytes 2949124
  10.1 45.2 %all-to-all-start.2 = ((bf16[30,128,128]{2,0,1:T(8,128)(2,1)}), bf16[30,128,128]{2,0,1:T(8,128)(2,1)S(1)}, u32[]{:S(2)}, u32[]{:S(2)}) async-start(bf16[30,128,128]{2,0,1:T(8,128)(2,1)} %copy.69), calls=%async_computation.2 | async-start | bytes 2097152 | tf_op jit(solution)/shard_map/all_to_all | solution.py:113
  21.6 2.5 copy-start.10
  27.8 1.5 copy-start.9
  27.8 13.2 %copy-start.19 = (s32[8]{0:T(128)S(1)}, s32[8]{0:T(128)}, u32[]{:S(2)}) copy-start(s32[8]{0:T(128)} %param.11) | copy-start | bytes 100
  41.0 24.6 %copy-start.18 = (s32[2]{0:T(128)S(1)}, s32[2]{0:T(128)}, u32[]{:S(2)}) copy-start(s32[2]{0:T(128)} %param.12) | copy-start | bytes 28
  50.5 15.7 %copy-start.17 = (bf16[1,1,128,128]{2,3,1,0:T(8,128)(2,1)S(1)}, bf16[1,1,128,128]{2,3,1,0:T(8,128)(2,1)}, u32[]{:S(2)}) copy-start(bf16[1,1,128,128]{2,3,1,0:T(8,128)(2,1)} %copy.108) | copy-start | bytes 98308
  51.2 2.7 copy-start.15
  55.3 14.1 %copy-start.14 = (bf16[2,128,128]{2,1,0:T(8,128)(2,1)S(1)}, bf16[2,128,128]{2,1,0:T(8,128)(2,1)}, u32[]{:S(2)}) copy-start(bf16[2,128,128]{2,1,0:T(8,128)(2,1)} %param.10) | copy-start | bytes 196612
  55.3 11.5 %copy-start.2 = (bf16[30,128,128]{2,0,1:T(8,128)(2,1)}, bf16[30,128,128]{2,0,1:T(8,128)(2,1)S(1)}, u32[]{:S(2)}) copy-start(bf16[30,128,128]{2,0,1:T(8,128)(2,1)S(1)} %all-to-all-done.2) | copy-start | bytes 2949124
  55.3 28.9 %all-to-all-start = ((bf16[30,128,128]{2,0,1:T(8,128)(2,1)}), bf16[30,128,128]{2,0,1:T(8,128)(2,1)}, u32[]{:S(2)}, u32[]{:S(2)}) async-start(bf16[30,128,128]{2,0,1:T(8,128)(2,1)} %copy.65), calls=%async_computation | async-start | bytes 2097152 | tf_op jit(solution)/shard_map/all_to_all | solution.py:113
  98.2 1.5 copy-start.8
  118.1 1.8 copy-start.6
  118.1 2.1 copy-start.12
  121.9 162.1 %all-to-all-start.3 = ((bf16[30,128,128]{2,0,1:T(8,128)(2,1)}), bf16[30,128,128]{2,0,1:T(8,128)(2,1)}, u32[]{:S(2)}, u32[]{:S(2)}) async-start(bf16[30,128,128]{2,0,1:T(8,128)(2,1)} %copy.82), calls=%async_computation.3 | async-start | bytes 2097152 | tf_op jit(solution)/shard_map/all_to_all | solution.py:117
  126.8 154.3 %all-reduce.5.cloned.1.call-start = ((), (), s32[]{:S(2)}) async-start(), calls=%async_computation.6 | async-start | bytes 1572864 | tf_op jit(solution)/shard_map/psum | solution.py:344
  281.1 2.3 copy-start.16
  284.0 25.6 %all-to-all-start.1 = ((bf16[30,128,128]{2,0,1:T(8,128)(2,1)}), bf16[30,128,128]{2,0,1:T(8,128)(2,1)S(1)}, u32[]{:S(2)}, u32[]{:S(2)}) async-start(bf16[30,128,128]{2,0,1:T(8,128)(2,1)} %copy.67), calls=%async_computation.1 | async-start | bytes 2097152 | tf_op jit(solution)/shard_map/all_to_all | solution.py:117
  290.6 2.1 copy-start.1
  299.1 3.4 copy-start.11
  309.6 20.5 %all-to-all-start.4 = ((f32[128,1,1152]{2,1,0:T(1,128)}), f32[128,1,1152]{2,1,0:T(1,128)}, u32[]{:S(2)}, u32[]{:S(2)}) async-start(f32[128,1,1152]{2,1,0:T(1,128)} %bitcast.321), calls=%async_computation.4 | async-start | bytes 1179648 | tf_op jit(solution)/shard_map/all_to_all | solution.py:273
  316.1 1.3 copy-start.5
  319.0 17.8 %copy-start.3 = (bf16[1,32,120,128]{3,2,1,0:T(8,128)(2,1)S(1)}, bf16[1,32,120,128]{3,2,1,0:T(8,128)(2,1)}, u32[]{:S(2)}) copy-start(bf16[1,32,120,128]{3,2,1,0:T(8,128)(2,1)} %get-tuple-element.46) | copy-start | bytes 2949124
  332.6 18.5 %all-to-all-start.5 = ((f32[128,1,1152]{2,1,0:T(1,128)}), f32[128,1,1152]{2,1,0:T(1,128)S(1)}, u32[]{:S(2)}, u32[]{:S(2)}) async-start(f32[128,1,1152]{2,1,0:T(1,128)} %broadcast_in_dim.4), calls=%async_computation.5 | async-start | bytes 1179648 | tf_op jit(solution)/shard_map/all_to_all | solution.py:278
  (3 other events, 3.3 us)
Sparse Core Ops, SparseCore 0:
  132.9 148.0 all-reduce.4

commit v2 on v0

--- a/solution.py
+++ b/solution.py
@@ -220,7 +220,15 @@
         out_ref, tg_ref = rest
     blocks, frames, chans = act_ref.shape
     stacked = shifted_taps(grad_ref, dil_ref[0], -1)
-    grad_act = jnp.dot(stacked, wt_ref[...], preferred_element_type=jnp.float32)
+    grad_act = None
+    for tap in range(5):
+        term = lax.dot_general(
+            stacked[:, tap * chans : (tap + 1) * chans],
+            wt_ref[tap * chans : (tap + 1) * chans, :],
+            (((1,), (1,)), ((), ())),
+            preferred_element_type=jnp.float32,
+        )
+        grad_act = term if grad_act is None else grad_act + term
     flat_act = act_ref[...].reshape(blocks * frames, chans)
     part = lax.dot_general(
         flat_act, stacked, (((0,), (0,)), ((), ())), preferred_element_type=jnp.float32
@@ -230,7 +238,8 @@
     def _():
         tg_ref[...] = jnp.zeros_like(tg_ref)
 
-    tg_ref[...] += part
+    for tap in range(5):
+        tg_ref[tap] += part[:, tap * chans : (tap + 1) * chans]
     if with_pre:
         pre = pre_ref[...].reshape(blocks * frames, chans)
         sigma = 1.0 / (1.0 + jnp.exp(-pre))
@@ -241,7 +250,7 @@
 def temporal_backward_k(acts, grads, kernel, step_size, pre_below):
     count, frames, chans = acts.shape
     spec = pl.BlockSpec((JB, frames, chans), lambda j, d: (j, 0, 0))
-    wt = jnp.concatenate([kernel[tap].T for tap in range(5)], axis=0)
+    wt = kernel.reshape(5 * chans, chans)
     with_pre = pre_below is not None
     in_specs = [spec, spec, pl.BlockSpec((5 * chans, chans), lambda j, d: (0, 0))]
     operands = [step_size.reshape(1), acts, grads, wt]
@@ -254,34 +263,36 @@
             num_scalar_prefetch=1,
             grid=(count // JB,),
             in_specs=in_specs,
-            out_specs=[spec, pl.BlockSpec((chans, 5 * chans), lambda j, d: (0, 0))],
+            out_specs=[spec, pl.BlockSpec((5, chans, chans), lambda j, d: (0, 0, 0))],
         ),
         out_shape=[
             jax.ShapeDtypeStruct(acts.shape, jnp.bfloat16),
-            jax.ShapeDtypeStruct((chans, 5 * chans), jnp.float32),
+            jax.ShapeDtypeStruct((5, chans, chans), jnp.float32),
         ],
         compiler_params=pltpu.CompilerParams(dimension_semantics=("arbitrary",)),
     )(*operands)
-    tgrad = tg.reshape(chans, 5, chans).transpose(1, 0, 2)
-    return out, tgrad
+    return out, tg
 
 
 def all_sum(parts, scale):
-    flat = jnp.concatenate([p.reshape(-1) for p in parts])
+    chans = parts[0].shape[-1]
     count = lax.axis_size(("seg", "grp"))
-    chunk = flat.shape[0] // count
-    pieces = lax.all_to_all(
-        flat.reshape(count, chunk), ("seg", "grp"), split_axis=0, concat_axis=0, tiled=True
-    )
-    mine = jnp.sum(pieces, axis=0) * scale
-    spread = jnp.broadcast_to(mine[None], (count, chunk))
+    rows = [p.reshape(-1, chans) for p in parts]
+    used = sum(r.shape[0] for r in rows)
+    per = -(-used // (count * 8)) * 8
+    rows.append(jnp.zeros((per * count - used, chans), jnp.float32))
+    stack = jnp.concatenate(rows, axis=0).reshape(count, per, chans)
+    pieces = lax.all_to_all(stack, ("seg", "grp"), split_axis=0, concat_axis=0, tiled=True)
+    mine = jnp.sum(pieces, axis=0, keepdims=True) * scale
+    spread = jnp.broadcast_to(mine, stack.shape)
     whole = lax.all_to_all(spread, ("seg", "grp"), split_axis=0, concat_axis=0, tiled=True)
-    whole = whole.reshape(-1)
+    whole = whole.reshape(-1, chans)
     out = []
     offset = 0
     for p in parts:
-        out.append(whole[offset : offset + p.size].reshape(p.shape))
-        offset += p.size
+        size = p.size // chans
+        out.append(whole[offset : offset + size].reshape(p.shape))
+        offset += size
     return out
 
 

time: 228 us -> 206 us (0.904)
  local copies, waits for them, and re-layouts: 61 us -> 28.2 us
  waiting for transfers between devices: 53.6 us -> 70.3 us
  starting transfers between devices: 45 us -> 39.2 us
    unnamed x60 -> x38, local copies, waits for them, and re-layouts: 26.6 us -> 1.47 us
    all_to_all x2, waiting for transfers between devices: 5.95 us -> 14.6 us  [to_frames(): lax.all_to_all(blocks, ('seg', 'grp'), split_axis=1, concat_axis=1, tiled...]
    all_to_all x2, waiting for transfers between devices: 14.4 us -> 22.9 us  [to_pixels(): lax.all_to_all(strided, ('seg', 'grp'), split_axis=1, concat_axis=1, tile...]
    all_to_all x2, starting transfers between devices: 21.7 us -> 16.4 us  [to_pixels(): lax.all_to_all(strided, ('seg', 'grp'), split_axis=1, concat_axis=1, tile...]
    pallas_call x3 -> x1, local copies, waits for them, and re-layouts: 5.83 us -> 2.81 us  [temporal_backward_k(): pl.pallas_call(functools.partial(tbwd_kernel, with_pre), grid_spec=pltpu....]
  transfers between devices with their start and end apart: 6 -> 6, of which waited for: 4 -> 6; matrix products, arithmetic and copies ran while one was open for 36% -> 25% of each run, Pallas kernels for 0% -> 0%
where the time goes in v2:
time: 206 us; the launch traced here: 205 us
  waiting for transfers between devices  70.3 us (34%)
  starting transfers between devices  39.2 us (19%)
  local copies, waits for them, and re-layouts  28.2 us (14%)
  matrix products  26.7 us (13%)
  Pallas kernels  25 us (12%)
  other arithmetic  14.4 us (7%)
    all_to_all x2, waiting for transfers between devices, to_pixels(): lax.all_to_all(strided, ('seg', 'grp'), split_axis=1, concat_axis=1, tile...  22.9 us
    all_to_all x1, waiting for transfers between devices, all_sum(): lax.all_to_all(spread, ('seg', 'grp'), split_axis=0, concat_axis=0, tiled...  16.9 us
    all_to_all x2, starting transfers between devices, to_pixels(): lax.all_to_all(strided, ('seg', 'grp'), split_axis=1, concat_axis=1, tile...  16.4 us
    all_to_all x1, waiting for transfers between devices, all_sum(): lax.all_to_all(stack, ('seg', 'grp'), split_axis=0, concat_axis=0, tiled=...  15.9 us
    all_to_all x2, waiting for transfers between devices, to_frames(): lax.all_to_all(blocks, ('seg', 'grp'), split_axis=1, concat_axis=1, tiled...  14.6 us
    dot_general x9, matrix products, spatial_back(): jnp.dot(piece, kernel[3 * row_tap + col_tap].T, preferred_element_type=jn...  14 us
    pallas_call x2, Pallas kernels, temporal_backward_k(): pl.pallas_call(functools.partial(tbwd_kernel, with_pre), grid_spec=pltpu....  13.5 us
    pallas_call x2, Pallas kernels, temporal_forward_k(): pl.pallas_call(tfwd_kernel, grid_spec=pltpu.PrefetchScalarGridSpec(num_sc...  11.4 us
  transfers between devices with their start and end apart: 6, of which 6 were waited for; matrix products, arithmetic and copies ran while one was open for 25% of the time, Pallas kernels for 0%

profile of v2, /device:TPU:1, one launch (start us, length us, event | category | flops | bytes accessed | tf_op | source)
XLA Modules:
  0.0 204.8 jit_solution(11830003142770149219)
XLA Ops:
  0.6 2.9 %copy.26 = bf16[30,128,128]{2,0,1:T(8,128)(2,1)} copy(bf16[30,128,128]{2,1,0:T(8,128)(2,1)} %bitcast.278) | data formatting | bytes 1966080 | tf_op jit(solution)/shard_map/reshape;reshape | solution.py:112
  3.5 11.5 %all-to-all-start.2 = ((bf16[30,128,128]{2,0,1:T(8,128)(2,1)}), bf16[30,128,128]{2,0,1:T(8,128)(2,1)S(1)}, u32[]{:S(2)}, u32[]{:S(2)}) async-start(bf16[30,128,128]{2,0,1:T(8,128)(2,1)} %copy.26), calls=%async_computation.2 | async-start | bytes 2097152 | tf_op jit(solution)/shard_map/all_to_all | solution.py:113
  15.1 2.5 %pad_slice_fusion.8 = (bf16[1,32,120,128]{3,2,1,0:T(8,128)(2,1)S(1)}, bf16[1,32,120,128]{3,2,1,0:T(8,128)(2,1)S(1)}, bf16[1,32,120,128]{3,2,1,0:T(8,128)(2,1)S(1...) fusion(bf16[1,32,120,128]{3,2,1,0:T(8,128)(2,1)S(1)} %copy-done.2), kind=kLoop, calls=%fused_computation.70 | loop fusion | bytes 8847360 | tf_op jit(solution)/shard_map/slice | solution.py:36
  23.5 10.5 %all-to-all-done.2 = bf16[30,128,128]{2,0,1:T(8,128)(2,1)S(1)} async-done(((bf16[30,128,128]{2,0,1:T(8,128)(2,1)}), bf16[30,128,128]{2,0,1:T(8,128)(2,1)S(1)}, u32[]{:S(2)}, u32[]{:S(2)}) %all-to-all-start.2) | async-done | bytes 983072 | tf_op jit(solution)/shard_map/all_to_all | solution.py:113
  34.0 4.9 %all-to-all-start = ((bf16[30,128,128]{2,0,1:T(8,128)(2,1)}), bf16[30,128,128]{2,0,1:T(8,128)(2,1)}, u32[]{:S(2)}, u32[]{:S(2)}) async-start(bf16[30,128,128]{2,0,1:T(8,128)(2,1)} %copy.22), calls=%async_computation | async-start | bytes 2097152 | tf_op jit(solution)/shard_map/all_to_all | solution.py:113
  45.1 12.4 %all-to-all-done = bf16[30,128,128]{2,0,1:T(8,128)(2,1)} async-done(((bf16[30,128,128]{2,0,1:T(8,128)(2,1)}), bf16[30,128,128]{2,0,1:T(8,128)(2,1)}, u32[]{:S(2)}, u32[]{:S(2)}) %all-to-all-start) | async-done | bytes 983072 | tf_op jit(solution)/shard_map/all_to_all | solution.py:113
  57.5 2.6 %copy.23.act_ref = bf16[30,128,128]{2,1,0:T(8,128)(2,1)} copy(bf16[30,128,128]{2,0,1:T(8,128)(2,1)} %all-to-all-done) | data formatting | bytes 1966080 | tf_op jit(solution)/shard_map/all_to_all | solution.py:113
  60.1 5.7 %shard_map.110 = (f32[30,128,128]{2,1,0:T(8,128)}, bf16[30,128,128]{2,1,0:T(8,128)(2,1)}) custom-call(s32[1]{0:T(128)} %get-tuple-element.43.dil_ref, bf16[30,128,128]{2,1,0:T(8,128)(2,1)} %copy.23.act_ref, bf16[640,128]{1,0:T(8,128)(2,1)} %bitcast.274), custom_call_target="tpu_custom_call" | custom-call | tf_op jit(solution)/shard_map/pallas_call | solution.py:201
  65.8 5.7 %shard_map.111 = (f32[30,128,128]{2,1,0:T(8,128)}, bf16[30,128,128]{2,1,0:T(8,128)(2,1)}) custom-call(s32[1]{0:T(128)} %get-tuple-element.44.dil_ref, bf16[30,128,128]{2,1,0:T(8,128)(2,1)} %get-tuple-element.13.act_ref, bf16[640,128]{1,0:T(8,128)(2,1)} %bitcast.276), custom_call_target="tpu_custom_call" | custom-call | tf_op jit(solution)/shard_map/pallas_call | solution.py:201
  71.5 3.9 %fusion.2.grad_ref = bf16[30,128,128]{2,1,0:T(8,128)(2,1)} fusion(f32[30,8,16,128]{3,2,1,0:T(8,128)} %multiply_add_fusion, f32[30,128,128]{2,1,0:T(8,128)} %get-tuple-element.15), kind=kLoop, calls=%fused_computation.20 | loop fusion | flops 4423680 | bytes 4915200 | tf_op jit(solution)/shard_map/convert_element_type | solution.py:346
  75.3 7.2 %shard_map.112 = (bf16[30,128,128]{2,1,0:T(8,128)(2,1)}, f32[5,128,128]{2,1,0:T(8,128)}) custom-call(s32[1]{0:T(128)} %get-tuple-element.44.dil_ref, bf16[30,128,128]{2,1,0:T(8,128)(2,1)} %get-tuple-element.13.act_ref, bf16[30,128,128]{2,1,0:T(8,128)(2,1)} %fusion.2.grad_ref, bf16[640,128]{1,0:T(8,128)(2,1)} %bitcast.277, ...), custom_call_target="tpu_custom_call" | custom-call | tf_op jit(solution)/shard_map/pallas_call | solution.py:260
  82.5 6.3 %shard_map.113 = (bf16[30,128,128]{2,1,0:T(8,128)(2,1)}, f32[5,128,128]{2,1,0:T(8,128)}) custom-call(s32[1]{0:T(128)} %get-tuple-element.43.dil_ref, bf16[30,128,128]{2,1,0:T(8,128)(2,1)} %copy.23.act_ref, bf16[30,128,128]{2,1,0:T(8,128)(2,1)} %get-tuple-element.17.grad_ref, bf16[640,128]{1,0:T(8,128)(2,1)} %bitcast.275), custom_call_target="tpu_custom_call" | custom-call | tf_op jit(solution)/shard_map/pallas_call | solution.py:260
  88.9 2.8 %copy.29 = bf16[30,128,128]{2,0,1:T(8,128)(2,1)} copy(bf16[30,128,128]{2,1,0:T(8,128)(2,1)} %get-tuple-element.18) | data formatting | bytes 1966080 | tf_op jit(solution)/shard_map/pallas_call | solution.py:260
  91.7 4.9 %all-to-all-start.3 = ((bf16[30,128,128]{2,0,1:T(8,128)(2,1)}), bf16[30,128,128]{2,0,1:T(8,128)(2,1)}, u32[]{:S(2)}, u32[]{:S(2)}) async-start(bf16[30,128,128]{2,0,1:T(8,128)(2,1)} %copy.29), calls=%async_computation.3 | async-start | bytes 2097152 | tf_op jit(solution)/shard_map/all_to_all | solution.py:117
  101.6 13.6 %all-to-all-done.3 = bf16[30,128,128]{2,0,1:T(8,128)(2,1)} async-done(((bf16[30,128,128]{2,0,1:T(8,128)(2,1)}), bf16[30,128,128]{2,0,1:T(8,128)(2,1)}, u32[]{:S(2)}, u32[]{:S(2)}) %all-to-all-start.3) | async-done | bytes 983072 | tf_op jit(solution)/shard_map/all_to_all | solution.py:117
  115.2 4.9 %all-to-all-start.1 = ((bf16[30,128,128]{2,0,1:T(8,128)(2,1)}), bf16[30,128,128]{2,0,1:T(8,128)(2,1)}, u32[]{:S(2)}, u32[]{:S(2)}) async-start(bf16[30,128,128]{2,0,1:T(8,128)(2,1)} %copy.24), calls=%async_computation.1 | async-start | bytes 2097152 | tf_op jit(solution)/shard_map/all_to_all | solution.py:117
  120.1 2.1 %multiply_convert_fusion = bf16[30,128,128]{2,1,0:T(8,128)(2,1)S(1)} fusion(f32[30,128,128]{2,1,0:T(8,128)S(1)} %bitcast.236, bf16[30,128,128]{2,0,1:T(8,128)(2,1)} %all-to-all-done.3), kind=kLoop, calls=%fused_computation.21 | loop fusion | flops 4915200 | bytes 3932160 | tf_op jit(solution)/shard_map/convert_element_type | solution.py:355
  129.1 3.8 %pad_slice_fusion = (bf16[1,32,120,128]{3,2,1,0:T(8,128)(2,1)}, bf16[1,32,120,128]{3,2,1,0:T(8,128)(2,1)S(1)}, bf16[1,32,120,128]{3,2,1,0:T(8,128)(2,1)}, bf16[1...) fusion(bf16[1,32,120,128]{3,2,1,0:T(8,128)(2,1)S(1)} %multiply_, ...), kind=kLoop, calls=%fused_computation.62 | loop fusion | bytes 8847360 | tf_op jit(solution)/shard_map/slice | solution.py:51
  138.7 8.7 %all-to-all-start.4 = ((f32[128,24,128]{2,1,0:T(8,128)}), f32[128,24,128]{2,1,0:T(8,128)S(1)}, u32[]{:S(2)}, u32[]{:S(2)}) async-start(f32[128,24,128]{2,1,0:T(8,128)} %bitcast.88), calls=%async_computation.4 | async-start | bytes 3145728 | tf_op jit(solution)/shard_map/all_to_all | solution.py:285
  147.4 2.7 %copy.25 = bf16[30,128,128]{2,1,0:T(8,128)(2,1)} copy(bf16[30,128,128]{2,0,1:T(8,128)(2,1)} %all-to-all-done.1) | data formatting | bytes 1966080 | tf_op jit(solution)/shard_map/all_to_all | solution.py:117
  151.9 2.6 %convolution_add_fusion.5 = f32[3840,128]{1,0:T(8,128)} fusion(f32[3840,128]{1,0:T(8,128)S(1)} %convolution_add_fusion.6, bf16[3840,128]{1,0:T(8,128)(2,1)S(1)} %bitcast.247, bf16[9,128,128]{2,1,0:T(8,128)(2,1)} %param.8), kind=kOutput, calls=%fused_computation.5 | convolution fusion | flops 126320640 | bytes 4947968 | tf_op jit(solution)/shard_map/dot_general | solution.py:54
  156.2 15.9 %all-to-all-done.4 = f32[128,24,128]{2,1,0:T(8,128)S(1)} async-done(((f32[128,24,128]{2,1,0:T(8,128)}), f32[128,24,128]{2,1,0:T(8,128)S(1)}, u32[]{:S(2)}, u32[]{:S(2)}) %all-to-all-start.4) | async-done | bytes 1572896 | tf_op jit(solution)/shard_map/all_to_all | solution.py:285
  173.5 4.4 %all-to-all-start.5 = ((f32[128,24,128]{2,1,0:T(8,128)}), f32[128,24,128]{2,1,0:T(8,128)S(1)}, u32[]{:S(2)}, u32[]{:S(2)}) async-start(f32[128,24,128]{2,1,0:T(8,128)} %broadcast_in_dim.8), calls=%async_computation.5 | async-start | bytes 3145728 | tf_op jit(solution)/shard_map/all_to_all | solution.py:288
  185.5 16.9 %all-to-all-done.5 = f32[128,24,128]{2,1,0:T(8,128)S(1)} async-done(((f32[128,24,128]{2,1,0:T(8,128)}), f32[128,24,128]{2,1,0:T(8,128)S(1)}, u32[]{:S(2)}, u32[]{:S(2)}) %all-to-all-start.5) | async-done | bytes 1572896 | tf_op jit(solution)/shard_map/all_to_all | solution.py:288
  (95 shorter events, 44.5 us)
Async XLA Ops:
  0.6 14.4 %copy-start.2 = (bf16[1,32,120,128]{3,2,1,0:T(8,128)(2,1)S(1)}, bf16[1,32,120,128]{3,2,1,0:T(8,128)(2,1)}, u32[]{:S(2)}) copy-start(bf16[1,32,120,128]{3,2,1,0:T(8,128)(2,1)} %param.7) | copy-start | bytes 2949124
  3.5 30.5 %all-to-all-start.2 = ((bf16[30,128,128]{2,0,1:T(8,128)(2,1)}), bf16[30,128,128]{2,0,1:T(8,128)(2,1)S(1)}, u32[]{:S(2)}, u32[]{:S(2)}) async-start(bf16[30,128,128]{2,0,1:T(8,128)(2,1)} %copy.26), calls=%async_computation.2 | async-start | bytes 2097152 | tf_op jit(solution)/shard_map/all_to_all | solution.py:113
  15.1 2.5 %copy-start.13 = (bf16[9,128,128]{2,1,0:T(8,128)(2,1)S(1)}, bf16[9,128,128]{2,1,0:T(8,128)(2,1)}, u32[]{:S(2)}) copy-start(bf16[9,128,128]{2,1,0:T(8,128)(2,1)} %param.8) | copy-start | bytes 884740
  21.2 2.2 %copy-start.18 = (s32[8]{0:T(128)S(1)}, s32[8]{0:T(128)}, u32[]{:S(2)}) copy-start(s32[8]{0:T(128)} %param.11) | copy-start | bytes 100
  21.8 17.1 %copy-start.17 = (s32[2]{0:T(128)S(1)}, s32[2]{0:T(128)}, u32[]{:S(2)}) copy-start(s32[2]{0:T(128)} %param.12) | copy-start | bytes 28
  23.5 19.7 %copy-start.16 = (bf16[2,128,128]{2,1,0:T(8,128)(2,1)S(1)}, bf16[2,128,128]{2,1,0:T(8,128)(2,1)}, u32[]{:S(2)}) copy-start(bf16[2,128,128]{2,1,0:T(8,128)(2,1)} %param.10) | copy-start | bytes 196612
  34.0 5.6 %copy-start.6 = (bf16[30,128,128]{2,0,1:T(8,128)(2,1)}, bf16[30,128,128]{2,0,1:T(8,128)(2,1)S(1)}, u32[]{:S(2)}) copy-start(bf16[30,128,128]{2,0,1:T(8,128)(2,1)S(1)} %all-to-all-done.2) | copy-start | bytes 2949124
  34.0 23.5 %all-to-all-start = ((bf16[30,128,128]{2,0,1:T(8,128)(2,1)}), bf16[30,128,128]{2,0,1:T(8,128)(2,1)}, u32[]{:S(2)}, u32[]{:S(2)}) async-start(bf16[30,128,128]{2,0,1:T(8,128)(2,1)} %copy.22), calls=%async_computation | async-start | bytes 2097152 | tf_op jit(solution)/shard_map/all_to_all | solution.py:113
  91.7 23.5 %all-to-all-start.3 = ((bf16[30,128,128]{2,0,1:T(8,128)(2,1)}), bf16[30,128,128]{2,0,1:T(8,128)(2,1)}, u32[]{:S(2)}, u32[]{:S(2)}) async-start(bf16[30,128,128]{2,0,1:T(8,128)(2,1)} %copy.29), calls=%async_computation.3 | async-start | bytes 2097152 | tf_op jit(solution)/shard_map/all_to_all | solution.py:117
  96.6 1.8 copy-start.11
  100.5 1.1 copy-start.15
  115.2 23.5 %all-to-all-start.1 = ((bf16[30,128,128]{2,0,1:T(8,128)(2,1)}), bf16[30,128,128]{2,0,1:T(8,128)(2,1)}, u32[]{:S(2)}, u32[]{:S(2)}) async-start(bf16[30,128,128]{2,0,1:T(8,128)(2,1)} %copy.24), calls=%async_computation.1 | async-start | bytes 2097152 | tf_op jit(solution)/shard_map/all_to_all | solution.py:117
  120.1 2.1 %copy-start.3 = (bf16[1,32,120,128]{3,2,1,0:T(8,128)(2,1)S(1)}, bf16[1,32,120,128]{3,2,1,0:T(8,128)(2,1)}, u32[]{:S(2)}) copy-start(bf16[1,32,120,128]{3,2,1,0:T(8,128)(2,1)} %param.7) | copy-start | bytes 2949124
  127.1 1.3 copy-start
  138.7 33.3 %all-to-all-start.4 = ((f32[128,24,128]{2,1,0:T(8,128)}), f32[128,24,128]{2,1,0:T(8,128)S(1)}, u32[]{:S(2)}, u32[]{:S(2)}) async-start(f32[128,24,128]{2,1,0:T(8,128)} %bitcast.88), calls=%async_computation.4 | async-start | bytes 3145728 | tf_op jit(solution)/shard_map/all_to_all | solution.py:285
  147.4 2.7 %copy-start.4 = (f32[3840,128]{1,0:T(8,128)S(1)}, f32[3840,128]{1,0:T(8,128)}, u32[]{:S(2)}) copy-start(f32[3840,128]{1,0:T(8,128)} %convolution_add_fusion.7) | copy-start | bytes 5898244
  150.1 1.7 copy-start.10
  151.9 2.6 %copy-start.1 = (f32[30,128,128]{2,1,0:T(8,128)S(1)}, f32[30,128,128]{2,1,0:T(8,128)}, u32[]{:S(2)}) copy-start(f32[30,128,128]{2,1,0:T(8,128)} %copy-done) | copy-start | bytes 5898244
  173.5 4.4 %copy-start.5 = (f32[3840,128]{1,0:T(8,128)S(1)}, f32[3840,128]{1,0:T(8,128)}, u32[]{:S(2)}) copy-start(f32[3840,128]{1,0:T(8,128)} %convolution_add_fusion.5) | copy-start | bytes 5898244
  173.5 29.0 %all-to-all-start.5 = ((f32[128,24,128]{2,1,0:T(8,128)}), f32[128,24,128]{2,1,0:T(8,128)S(1)}, u32[]{:S(2)}, u32[]{:S(2)}) async-start(f32[128,24,128]{2,1,0:T(8,128)} %broadcast_in_dim.8), calls=%async_computation.5 | async-start | bytes 3145728 | tf_op jit(solution)/shard_map/all_to_all | solution.py:288
  177.9 1.7 copy-start.9
  179.6 1.3 copy-start.8
  180.9 1.3 copy-start.7
  182.1 1.3 copy-start.12
  (1 other events, 1.0 us)

commit v3 on v2

--- a/solution.py
+++ b/solution.py
@@ -210,6 +210,11 @@
             jax.ShapeDtypeStruct(acts.shape, jnp.float32),
             jax.ShapeDtypeStruct(acts.shape, jnp.bfloat16),
         ],
+        cost_estimate=pl.CostEstimate(
+            flops=2 * count * frames * chans * chans * 9,
+            transcendentals=count * frames * chans,
+            bytes_accessed=count * frames * chans * 8,
+        ),
     )(step_size.reshape(1), acts, kernel.reshape(5 * chans, chans))
 
 
@@ -270,6 +275,11 @@
             jax.ShapeDtypeStruct((5, chans, chans), jnp.float32),
         ],
         compiler_params=pltpu.CompilerParams(dimension_semantics=("arbitrary",)),
+        cost_estimate=pl.CostEstimate(
+            flops=2 * count * frames * chans * chans * 14,
+            transcendentals=count * frames * chans,
+            bytes_accessed=count * frames * chans * 10,
+        ),
     )(*operands)
     return out, tg
 
@@ -306,6 +316,7 @@
     act_zero = jax.nn.silu(pre_spatial).astype(jnp.bfloat16).reshape(local_frames, pixels, chans)
     cot_local = cotangent.reshape(local_frames, pixels, chans)
     act_blocks = to_pixels(act_zero)
+    act_blocks, cot_local = lax.optimization_barrier((act_blocks, cot_local))
     cot_blocks = to_pixels(cot_local)
     acts = [act_blocks]
     block, total_frames = act_blocks.shape[0], act_blocks.shape[1]

time: 206 us -> 204 us (level)
  waiting for transfers between devices: 70.3 us -> 60.1 us
  starting transfers between devices: 39.2 us -> 44.7 us
  local copies, waits for them, and re-layouts: 28.2 us -> 33.1 us
    all_to_all x2, starting transfers between devices: 9.75 us -> 20.1 us  [to_frames(): lax.all_to_all(blocks, ('seg', 'grp'), split_axis=1, concat_axis=1, tiled...]
    all_to_all x1, waiting for transfers between devices: 15.9 us -> 11.2 us  [all_sum(): lax.all_to_all(stack, ('seg', 'grp'), split_axis=0, concat_axis=0, tiled=...]
    all_to_all x2, waiting for transfers between devices: 22.9 us -> 18.5 us  [to_pixels(): lax.all_to_all(strided, ('seg', 'grp'), split_axis=1, concat_axis=1, tile...]
    all_to_all x1, starting transfers between devices: 8.7 us -> 4.39 us  [all_sum(): lax.all_to_all(stack, ('seg', 'grp'), split_axis=0, concat_axis=0, tiled=...]
    slice x1, local copies, waits for them, and re-layouts: 2.52 us -> 6.74 us  [spatial_forward(): padded[:, row_tap:row_tap + rows, col_tap:col_tap + cols, :]]
    reshape x0 -> x1, local copies, waits for them, and re-layouts: none -> 3.24 us  [to_pixels(): strided = flat.reshape(-1, count, chans)]
    another operation x1 -> x0, local copies, waits for them, and re-layouts: 2.89 us -> none  [to_pixels(): strided = flat.reshape(-1, count, chans)]
    all_to_all x1 -> x0, local copies, waits for them, and re-layouts: 2.55 us -> none  [to_pixels(): lax.all_to_all(strided, ('seg', 'grp'), split_axis=1, concat_axis=1, tile...]
  transfers between devices with their start and end apart: 6 -> 6, of which waited for: 6 -> 5; matrix products, arithmetic and copies ran while one was open for 25% -> 20% of each run, Pallas kernels for 0% -> 12%
where the time goes in v3:
time: 204 us; the launch traced here: 202 us
  waiting for transfers between devices  60.1 us (29%)
  starting transfers between devices  44.7 us (22%)
  local copies, waits for them, and re-layouts  33.1 us (16%)
  Pallas kernels  25.2 us (12%)
  matrix products  25.1 us (12%)
  other arithmetic  12.9 us (6%)
    all_to_all x2, starting transfers between devices, to_frames(): lax.all_to_all(blocks, ('seg', 'grp'), split_axis=1, concat_axis=1, tiled...  20.1 us
    all_to_all x2, waiting for transfers between devices, to_pixels(): lax.all_to_all(strided, ('seg', 'grp'), split_axis=1, concat_axis=1, tile...  18.5 us
    all_to_all x1, waiting for transfers between devices, all_sum(): lax.all_to_all(spread, ('seg', 'grp'), split_axis=0, concat_axis=0, tiled...  16.9 us
    all_to_all x2, starting transfers between devices, to_pixels(): lax.all_to_all(strided, ('seg', 'grp'), split_axis=1, concat_axis=1, tile...  15.9 us
    pallas_call x2, Pallas kernels, temporal_backward_k(): pl.pallas_call(functools.partial(tbwd_kernel, with_pre), grid_spec=pltpu....  13.6 us
    dot_general x9, matrix products, spatial_back(): jnp.dot(piece, kernel[3 * row_tap + col_tap].T, preferred_element_type=jn...  13.6 us
    all_to_all x2, waiting for transfers between devices, to_frames(): lax.all_to_all(blocks, ('seg', 'grp'), split_axis=1, concat_axis=1, tiled...  13.4 us
    pallas_call x2, Pallas kernels, temporal_forward_k(): pl.pallas_call(tfwd_kernel, grid_spec=pltpu.PrefetchScalarGridSpec(num_sc...  11.6 us
  transfers between devices with their start and end apart: 6, of which 5 were waited for; matrix products, arithmetic and copies ran while one was open for 20% of the time, Pallas kernels for 12%

profile of v3, /device:TPU:1, one launch (start us, length us, event | category | flops | bytes accessed | tf_op | source)
XLA Modules:
  0.0 202.3 jit_solution(6664620345462203745)
XLA Ops:
  0.6 6.7 %pad_slice_fusion.8 = (bf16[1,32,120,128]{3,2,1,0:T(8,128)(2,1)S(1)}, bf16[1,32,120,128]{3,2,1,0:T(8,128)(2,1)S(1)}, bf16[1,32,120,128]{3,2,1,0:T(8,128)(2,1)S(1...) fusion(bf16[1,32,120,128]{3,2,1,0:T(8,128)(2,1)} %param.7), kind=kLoop, calls=%fused_computation.70 | loop fusion | bytes 8847360 | tf_op jit(solution)/shard_map/slice | solution.py:36
  14.0 11.5 %all-to-all-start = ((bf16[30,128,128]{2,0,1:T(8,128)(2,1)}), bf16[30,128,128]{2,0,1:T(8,128)(2,1)S(1)}, u32[]{:S(2)}, u32[]{:S(2)}) async-start(bf16[30,128,128]{2,0,1:T(8,128)(2,1)} %copy.22), calls=%async_computation | async-start | bytes 2097152 | tf_op jit(solution)/shard_map/all_to_all | solution.py:113
  26.3 18.1 %all-to-all-done = bf16[30,128,128]{2,0,1:T(8,128)(2,1)S(1)} async-done(((bf16[30,128,128]{2,0,1:T(8,128)(2,1)}), bf16[30,128,128]{2,0,1:T(8,128)(2,1)S(1)}, u32[]{:S(2)}, u32[]{:S(2)}) %all-to-all-start) | async-done | bytes 983072 | tf_op jit(solution)/shard_map/all_to_all | solution.py:113
  44.5 3.2 %copy.26 = bf16[30,128,128]{2,0,1:T(8,128)(2,1)} copy(bf16[30,128,128]{2,1,0:T(8,128)(2,1)} %bitcast.276) | data formatting | bytes 1966080 | tf_op jit(solution)/shard_map/reshape | solution.py:112
  47.7 4.4 %all-to-all-start.2 = ((bf16[30,128,128]{2,0,1:T(8,128)(2,1)}), bf16[30,128,128]{2,0,1:T(8,128)(2,1)S(1)}, u32[]{:S(2)}, u32[]{:S(2)}) async-start(bf16[30,128,128]{2,0,1:T(8,128)(2,1)} %copy.26), calls=%async_computation.2 | async-start | bytes 2097152 | tf_op jit(solution)/shard_map/all_to_all | solution.py:113
  52.8 2.5 %copy.23.act_ref = bf16[30,128,128]{2,1,0:T(8,128)(2,1)} copy(bf16[30,128,128]{2,0,1:T(8,128)(2,1)} %copy-done.4) | data formatting | bytes 1966080 | tf_op jit(solution)/shard_map/optimization_barrier | solution.py:319
  55.4 5.7 %shard_map.110 = (f32[30,128,128]{2,1,0:T(8,128)}, bf16[30,128,128]{2,1,0:T(8,128)(2,1)}) custom-call(s32[1]{0:T(128)} %get-tuple-element.47.dil_ref, bf16[30,128,128]{2,1,0:T(8,128)(2,1)} %copy.23.act_ref, bf16[640,128]{1,0:T(8,128)(2,1)} %bitcast.287), custom_call_target="tpu_custom_call" | custom-call | flops 1132462080 | bytes 3932160 | tf_op jit(solution)/shard_map/pallas_call | solution.py:201
  61.1 5.9 %shard_map.111 = (f32[30,128,128]{2,1,0:T(8,128)}, bf16[30,128,128]{2,1,0:T(8,128)(2,1)}) custom-call(s32[1]{0:T(128)} %get-tuple-element.48.dil_ref, bf16[30,128,128]{2,1,0:T(8,128)(2,1)} %get-tuple-element.16.act_ref, bf16[640,128]{1,0:T(8,128)(2,1)} %bitcast.289), custom_call_target="tpu_custom_call" | custom-call | flops 1132462080 | bytes 3932160 | tf_op jit(solution)/shard_map/pallas_call | solution.py:201
  72.1 9.9 %all-to-all-start.1 = ((bf16[30,128,128]{2,0,1:T(8,128)(2,1)}), bf16[30,128,128]{2,0,1:T(8,128)(2,1)}, u32[]{:S(2)}, u32[]{:S(2)}) async-start(bf16[30,128,128]{2,0,1:T(8,128)(2,1)} %copy.24), calls=%async_computation.1 | async-start | bytes 2097152 | tf_op jit(solution)/shard_map/all_to_all | solution.py:117
  81.9 1.9 convert_reduce_fusion
  87.1 7.3 %shard_map.112 = (bf16[30,128,128]{2,1,0:T(8,128)(2,1)}, f32[5,128,128]{2,1,0:T(8,128)}) custom-call(s32[1]{0:T(128)} %get-tuple-element.48.dil_ref, bf16[30,128,128]{2,1,0:T(8,128)(2,1)} %get-tuple-element.16.act_ref, bf16[30,128,128]{2,1,0:T(8,128)(2,1)} %fusion.2.grad_ref, bf16[640,128]{1,0:T(8,128)(2,1)} %bitcast.290, ...), custom_call_target="tpu_custom_call" | custom-call | flops 1761607680 | bytes 4915200 | tf_op jit(solution)/shard_map/pallas_call | solution.py:265
  94.4 6.3 %shard_map.113 = (bf16[30,128,128]{2,1,0:T(8,128)(2,1)}, f32[5,128,128]{2,1,0:T(8,128)}) custom-call(s32[1]{0:T(128)} %get-tuple-element.47.dil_ref, bf16[30,128,128]{2,1,0:T(8,128)(2,1)} %copy.23.act_ref, bf16[30,128,128]{2,1,0:T(8,128)(2,1)} %get-tuple-element.21.grad_ref, bf16[640,128]{1,0:T(8,128)(2,1)} %bitcast.288), custom_call_target="tpu_custom_call" | custom-call | flops 1761607680 | bytes 4915200 | tf_op jit(solution)/shard_map/pallas_call | solution.py:265
  100.7 2.8 %copy.29 = bf16[30,128,128]{2,0,1:T(8,128)(2,1)} copy(bf16[30,128,128]{2,1,0:T(8,128)(2,1)} %get-tuple-element.22) | data formatting | bytes 1966080 | tf_op jit(solution)/shard_map/pallas_call | solution.py:265
  103.6 10.2 %all-to-all-start.3 = ((bf16[30,128,128]{2,0,1:T(8,128)(2,1)}), bf16[30,128,128]{2,0,1:T(8,128)(2,1)}, u32[]{:S(2)}, u32[]{:S(2)}) async-start(bf16[30,128,128]{2,0,1:T(8,128)(2,1)} %copy.29), calls=%async_computation.3 | async-start | bytes 2097152 | tf_op jit(solution)/shard_map/all_to_all | solution.py:117
  113.8 2.6 %copy.25 = bf16[30,128,128]{2,1,0:T(8,128)(2,1)} copy(bf16[30,128,128]{2,0,1:T(8,128)(2,1)} %all-to-all-done.1) | data formatting | bytes 1966080 | tf_op jit(solution)/shard_map/all_to_all | solution.py:117
  119.0 13.4 %all-to-all-done.3 = bf16[30,128,128]{2,0,1:T(8,128)(2,1)} async-done(((bf16[30,128,128]{2,0,1:T(8,128)(2,1)}), bf16[30,128,128]{2,0,1:T(8,128)(2,1)}, u32[]{:S(2)}, u32[]{:S(2)}) %all-to-all-start.3) | async-done | bytes 983072 | tf_op jit(solution)/shard_map/all_to_all | solution.py:117
  132.4 2.0 %multiply_convert_fusion = bf16[30,128,128]{2,1,0:T(8,128)(2,1)S(1)} fusion(f32[30,128,128]{2,1,0:T(8,128)S(1)} %bitcast.237, bf16[30,128,128]{2,0,1:T(8,128)(2,1)} %all-to-all-done.3), kind=kLoop, calls=%fused_computation.21 | loop fusion | flops 4915200 | bytes 3932160 | tf_op jit(solution)/shard_map/convert_element_type | solution.py:366
  140.5 4.4 %all-to-all-start.4 = ((f32[128,24,128]{2,1,0:T(8,128)}), f32[128,24,128]{2,1,0:T(8,128)S(1)}, u32[]{:S(2)}, u32[]{:S(2)}) async-start(f32[128,24,128]{2,1,0:T(8,128)} %bitcast.243), calls=%async_computation.4 | async-start | bytes 3145728 | tf_op jit(solution)/shard_map/all_to_all | solution.py:295
  147.2 3.3 %pad_slice_fusion = (bf16[1,32,120,128]{3,2,1,0:T(8,128)(2,1)}, bf16[1,32,120,128]{3,2,1,0:T(8,128)(2,1)S(1)}, bf16[1,32,120,128]{3,2,1,0:T(8,128)(2,1)S(1)}, bf...) fusion(bf16[1,32,120,128]{3,2,1,0:T(8,128)(2,1)S(1)} %multiply_, ...), kind=kLoop, calls=%fused_computation.62 | loop fusion | bytes 8847360 | tf_op jit(solution)/shard_map/slice | solution.py:51
  154.1 2.5 %convolution_add_fusion.5 = f32[3840,128]{1,0:T(8,128)} fusion(f32[3840,128]{1,0:T(8,128)S(1)} %convolution_add_fusion.6, bf16[3840,128]{1,0:T(8,128)(2,1)S(1)} %bitcast.253, bf16[9,128,128]{2,1,0:T(8,128)(2,1)} %param.8), kind=kOutput, calls=%fused_computation.5 | convolution fusion | flops 126320640 | bytes 4947968 | tf_op jit(solution)/shard_map/dot_general | solution.py:54
  158.3 11.2 %all-to-all-done.4 = f32[128,24,128]{2,1,0:T(8,128)S(1)} async-done(((f32[128,24,128]{2,1,0:T(8,128)}), f32[128,24,128]{2,1,0:T(8,128)S(1)}, u32[]{:S(2)}, u32[]{:S(2)}) %all-to-all-start.4) | async-done | bytes 1572896 | tf_op jit(solution)/shard_map/all_to_all | solution.py:295
  170.9 4.4 %all-to-all-start.5 = ((f32[128,24,128]{2,1,0:T(8,128)}), f32[128,24,128]{2,1,0:T(8,128)S(1)}, u32[]{:S(2)}, u32[]{:S(2)}) async-start(f32[128,24,128]{2,1,0:T(8,128)} %broadcast_in_dim.8), calls=%async_computation.5 | async-start | bytes 3145728 | tf_op jit(solution)/shard_map/all_to_all | solution.py:298
  180.9 2.1 %fusion = bf16[3840,128]{1,0:T(8,128)(2,1)} fusion(f32[3840,128]{1,0:T(8,128)S(1)} %convolution_add_fusion.1, bf16[3840,128]{1,0:T(8,128)(2,1)S(1)} %bitcast.265, bf16[9,128,128]{2,1,0:T(8,128)(2,1)} %param.8), kind=kOutput, calls=%fused_computation.16 | convolution fusion | flops 126812160 | bytes 3964928 | tf_op jit(solution)/shard_map/dot_general | solution.py:54
  183.0 16.9 %all-to-all-done.5 = f32[128,24,128]{2,1,0:T(8,128)S(1)} async-done(((f32[128,24,128]{2,1,0:T(8,128)}), f32[128,24,128]{2,1,0:T(8,128)S(1)}, u32[]{:S(2)}, u32[]{:S(2)}) %all-to-all-start.5) | async-done | bytes 1572896 | tf_op jit(solution)/shard_map/all_to_all | solution.py:298
  (97 shorter events, 41.7 us)
Async XLA Ops:
  0.6 6.8 %copy-start.13 = (bf16[9,128,128]{2,1,0:T(8,128)(2,1)S(1)}, bf16[9,128,128]{2,1,0:T(8,128)(2,1)}, u32[]{:S(2)}) copy-start(bf16[9,128,128]{2,1,0:T(8,128)(2,1)} %param.8) | copy-start | bytes 884740
  8.6 1.2 copy-start
  12.4 13.1 %copy-start.19 = (s32[8]{0:T(128)S(1)}, s32[8]{0:T(128)}, u32[]{:S(2)}) copy-start(s32[8]{0:T(128)} %param.11) | copy-start | bytes 100
  12.4 13.2 %copy-start.16 = (bf16[2,5,128,128]{3,2,1,0:T(8,128)(2,1)S(1)}, bf16[2,5,128,128]{3,2,1,0:T(8,128)(2,1)}, u32[]{:S(2)}) copy-start(bf16[2,5,128,128]{3,2,1,0:T(8,128)(2,1)} %param.9) | copy-start | bytes 983044
  14.0 30.5 %all-to-all-start = ((bf16[30,128,128]{2,0,1:T(8,128)(2,1)}), bf16[30,128,128]{2,0,1:T(8,128)(2,1)S(1)}, u32[]{:S(2)}, u32[]{:S(2)}) async-start(bf16[30,128,128]{2,0,1:T(8,128)(2,1)} %copy.22), calls=%async_computation | async-start | bytes 2097152 | tf_op jit(solution)/shard_map/all_to_all | solution.py:113
  44.5 3.2 %copy-start.4 = (bf16[30,128,128]{2,0,1:T(8,128)(2,1)}, bf16[30,128,128]{2,0,1:T(8,128)(2,1)S(1)}, u32[]{:S(2)}) copy-start(bf16[30,128,128]{2,0,1:T(8,128)(2,1)S(1)} %all-to-all-done) | copy-start | bytes 2949124
  44.5 7.6 %copy-start.18 = (s32[2]{0:T(128)S(1)}, s32[2]{0:T(128)}, u32[]{:S(2)}) copy-start(s32[2]{0:T(128)} %param.12) | copy-start | bytes 28
  47.7 23.4 %all-to-all-start.2 = ((bf16[30,128,128]{2,0,1:T(8,128)(2,1)}), bf16[30,128,128]{2,0,1:T(8,128)(2,1)S(1)}, u32[]{:S(2)}, u32[]{:S(2)}) async-start(bf16[30,128,128]{2,0,1:T(8,128)(2,1)} %copy.26), calls=%async_computation.2 | async-start | bytes 2097152 | tf_op jit(solution)/shard_map/all_to_all | solution.py:113
  61.1 7.5 %copy-start.17 = (bf16[2,128,128]{2,1,0:T(8,128)(2,1)S(1)}, bf16[2,128,128]{2,1,0:T(8,128)(2,1)}, u32[]{:S(2)}) copy-start(bf16[2,128,128]{2,1,0:T(8,128)(2,1)} %param.10) | copy-start | bytes 196612
  66.9 1.8 copy-start.8
  72.1 31.5 %all-to-all-start.1 = ((bf16[30,128,128]{2,0,1:T(8,128)(2,1)}), bf16[30,128,128]{2,0,1:T(8,128)(2,1)}, u32[]{:S(2)}, u32[]{:S(2)}) async-start(bf16[30,128,128]{2,0,1:T(8,128)(2,1)} %copy.24), calls=%async_computation.1 | async-start | bytes 2097152 | tf_op jit(solution)/shard_map/all_to_all | solution.py:117
  83.8 1.5 copy-start.12
  103.6 28.8 %all-to-all-start.3 = ((bf16[30,128,128]{2,0,1:T(8,128)(2,1)}), bf16[30,128,128]{2,0,1:T(8,128)(2,1)}, u32[]{:S(2)}, u32[]{:S(2)}) async-start(bf16[30,128,128]{2,0,1:T(8,128)(2,1)} %copy.29), calls=%async_computation.3 | async-start | bytes 2097152 | tf_op jit(solution)/shard_map/all_to_all | solution.py:117
  116.4 1.2 copy-start.9
  116.5 1.5 copy-start.14
  116.5 1.5 copy-start.15
  119.0 15.5 %copy-start.1 = (bf16[1,32,120,128]{3,2,1,0:T(8,128)(2,1)S(1)}, bf16[1,32,120,128]{3,2,1,0:T(8,128)(2,1)}, u32[]{:S(2)}) copy-start(bf16[1,32,120,128]{3,2,1,0:T(8,128)(2,1)} %param.7) | copy-start | bytes 2949124
  140.5 29.0 %all-to-all-start.4 = ((f32[128,24,128]{2,1,0:T(8,128)}), f32[128,24,128]{2,1,0:T(8,128)S(1)}, u32[]{:S(2)}, u32[]{:S(2)}) async-start(f32[128,24,128]{2,1,0:T(8,128)} %bitcast.243), calls=%async_computation.4 | async-start | bytes 3145728 | tf_op jit(solution)/shard_map/all_to_all | solution.py:295
  170.9 4.4 %copy-start.2 = (f32[3840,128]{1,0:T(8,128)S(1)}, f32[3840,128]{1,0:T(8,128)}, u32[]{:S(2)}) copy-start(f32[3840,128]{1,0:T(8,128)} %convolution_add_fusion.5) | copy-start | bytes 5898244
  170.9 29.0 %all-to-all-start.5 = ((f32[128,24,128]{2,1,0:T(8,128)}), f32[128,24,128]{2,1,0:T(8,128)S(1)}, u32[]{:S(2)}, u32[]{:S(2)}) async-start(f32[128,24,128]{2,1,0:T(8,128)} %broadcast_in_dim.8), calls=%async_computation.5 | async-start | bytes 3145728 | tf_op jit(solution)/shard_map/all_to_all | solution.py:298
  175.3 1.7 copy-start.7
  177.0 1.3 copy-start.6
  178.3 1.3 copy-start.5
  179.6 1.3 copy-start.10
  (2 other events, 2.1 us)

commit v4 on v3

--- a/solution.py
+++ b/solution.py
@@ -164,17 +164,17 @@
 
 def shifted_taps(x_ref, step, sign):
     blocks, frames, chans = x_ref.shape
-    wide = jnp.concatenate([x_ref[j] for j in range(blocks)], axis=1)
+    wide = jnp.concatenate([x_ref[j] for j in range(blocks)], axis=1).astype(jnp.float32)
+    rows = lax.broadcasted_iota(jnp.int32, wide.shape, 0)
     taps = []
     for tap in range(5):
         if tap == 2:
             taps.append(None)
             continue
-        moved = jnp.dot(
-            shift_matrix(sign * (tap - 2) * step, frames), wide,
-            preferred_element_type=jnp.float32,
-        ).astype(jnp.bfloat16)
-        taps.append(moved)
+        offset = sign * (tap - 2) * step
+        rolled = pltpu.roll(wide, (frames - offset) % frames, 0)
+        inside = (rows + offset >= 0) & (rows + offset < frames)
+        taps.append(jnp.where(inside, rolled, 0.0).astype(jnp.bfloat16))
     rows = []
     for j in range(blocks):
         parts = []

time: 204 us -> 209 us (1.025)
  Pallas kernels: 25.2 us -> 30.5 us
    pallas_call x2, Pallas kernels: 11.6 us -> 14.4 us  [temporal_forward_k(): pl.pallas_call(tfwd_kernel, grid_spec=pltpu.PrefetchScalarGridSpec(num_sc...]
    pallas_call x2, Pallas kernels: 13.6 us -> 16.1 us  [temporal_backward_k(): pl.pallas_call(functools.partial(tbwd_kernel, with_pre), grid_spec=pltpu....]
  transfers between devices with their start and end apart: 6 -> 6, of which waited for: 5 -> 4; matrix products, arithmetic and copies ran while one was open for 20% -> 19% of each run, Pallas kernels for 12% -> 15%
where the time goes in v4:
time: 209 us; the launch traced here: 208 us
  waiting for transfers between devices  59.7 us (29%)
  starting transfers between devices  45.1 us (22%)
  local copies, waits for them, and re-layouts  33.1 us (16%)
  Pallas kernels  30.5 us (15%)
  matrix products  25.2 us (12%)
  other arithmetic  12.9 us (6%)
    all_to_all x2, starting transfers between devices, to_frames(): lax.all_to_all(blocks, ('seg', 'grp'), split_axis=1, concat_axis=1, tiled...  20.4 us
    all_to_all x2, waiting for transfers between devices, to_pixels(): lax.all_to_all(strided, ('seg', 'grp'), split_axis=1, concat_axis=1, tile...  18.1 us
    all_to_all x1, waiting for transfers between devices, all_sum(): lax.all_to_all(spread, ('seg', 'grp'), split_axis=0, concat_axis=0, tiled...  16.9 us
    pallas_call x2, Pallas kernels, temporal_backward_k(): pl.pallas_call(functools.partial(tbwd_kernel, with_pre), grid_spec=pltpu....  16.1 us
    all_to_all x2, starting transfers between devices, to_pixels(): lax.all_to_all(strided, ('seg', 'grp'), split_axis=1, concat_axis=1, tile...  15.9 us
    pallas_call x2, Pallas kernels, temporal_forward_k(): pl.pallas_call(tfwd_kernel, grid_spec=pltpu.PrefetchScalarGridSpec(num_sc...  14.4 us
    dot_general x9, matrix products, spatial_back(): jnp.dot(piece, kernel[3 * row_tap + col_tap].T, preferred_element_type=jn...  13.6 us
    all_to_all x2, waiting for transfers between devices, to_frames(): lax.all_to_all(blocks, ('seg', 'grp'), split_axis=1, concat_axis=1, tiled...  13.4 us
  transfers between devices with their start and end apart: 6, of which 4 were waited for; matrix products, arithmetic and copies ran while one was open for 19% of the time, Pallas kernels for 15%

profile of v4, /device:TPU:1, one launch (start us, length us, event | category | flops | bytes accessed | tf_op | source)
XLA Modules:
  0.0 207.6 jit_solution(4229003452700173113)
XLA Ops:
  0.6 6.7 %pad_slice_fusion.8 = (bf16[1,32,120,128]{3,2,1,0:T(8,128)(2,1)S(1)}, bf16[1,32,120,128]{3,2,1,0:T(8,128)(2,1)S(1)}, bf16[1,32,120,128]{3,2,1,0:T(8,128)(2,1)S(1...) fusion(bf16[1,32,120,128]{3,2,1,0:T(8,128)(2,1)} %param.7), kind=kLoop, calls=%fused_computation.70 | loop fusion | bytes 8847360 | tf_op jit(solution)/shard_map/slice | solution.py:36
  14.0 11.5 %all-to-all-start = ((bf16[30,128,128]{2,0,1:T(8,128)(2,1)}), bf16[30,128,128]{2,0,1:T(8,128)(2,1)S(1)}, u32[]{:S(2)}, u32[]{:S(2)}) async-start(bf16[30,128,128]{2,0,1:T(8,128)(2,1)} %copy.22), calls=%async_computation | async-start | bytes 2097152 | tf_op jit(solution)/shard_map/all_to_all | solution.py:113
  26.3 18.1 %all-to-all-done = bf16[30,128,128]{2,0,1:T(8,128)(2,1)S(1)} async-done(((bf16[30,128,128]{2,0,1:T(8,128)(2,1)}), bf16[30,128,128]{2,0,1:T(8,128)(2,1)S(1)}, u32[]{:S(2)}, u32[]{:S(2)}) %all-to-all-start) | async-done | bytes 983072 | tf_op jit(solution)/shard_map/all_to_all | solution.py:113
  44.5 3.2 %copy.26 = bf16[30,128,128]{2,0,1:T(8,128)(2,1)} copy(bf16[30,128,128]{2,1,0:T(8,128)(2,1)} %bitcast.276) | data formatting | bytes 1966080 | tf_op jit(solution)/shard_map/reshape | solution.py:112
  47.7 4.4 %all-to-all-start.2 = ((bf16[30,128,128]{2,0,1:T(8,128)(2,1)}), bf16[30,128,128]{2,0,1:T(8,128)(2,1)S(1)}, u32[]{:S(2)}, u32[]{:S(2)}) async-start(bf16[30,128,128]{2,0,1:T(8,128)(2,1)} %copy.26), calls=%async_computation.2 | async-start | bytes 2097152 | tf_op jit(solution)/shard_map/all_to_all | solution.py:113
  52.8 2.5 %copy.23.act_ref = bf16[30,128,128]{2,1,0:T(8,128)(2,1)} copy(bf16[30,128,128]{2,0,1:T(8,128)(2,1)} %copy-done.4) | data formatting | bytes 1966080 | tf_op jit(solution)/shard_map/optimization_barrier | solution.py:319
  55.4 7.1 %shard_map.110 = (f32[30,128,128]{2,1,0:T(8,128)}, bf16[30,128,128]{2,1,0:T(8,128)(2,1)}) custom-call(s32[1]{0:T(128)} %get-tuple-element.47.dil_ref, bf16[30,128,128]{2,1,0:T(8,128)(2,1)} %copy.23.act_ref, bf16[640,128]{1,0:T(8,128)(2,1)} %bitcast.287), custom_call_target="tpu_custom_call" | custom-call | flops 1132462080 | bytes 3932160 | tf_op jit(solution)/shard_map/pallas_call | solution.py:201
  62.5 7.3 %shard_map.111 = (f32[30,128,128]{2,1,0:T(8,128)}, bf16[30,128,128]{2,1,0:T(8,128)(2,1)}) custom-call(s32[1]{0:T(128)} %get-tuple-element.48.dil_ref, bf16[30,128,128]{2,1,0:T(8,128)(2,1)} %get-tuple-element.16.act_ref, bf16[640,128]{1,0:T(8,128)(2,1)} %bitcast.289), custom_call_target="tpu_custom_call" | custom-call | flops 1132462080 | bytes 3932160 | tf_op jit(solution)/shard_map/pallas_call | solution.py:201
  74.5 10.2 %all-to-all-start.1 = ((bf16[30,128,128]{2,0,1:T(8,128)(2,1)}), bf16[30,128,128]{2,0,1:T(8,128)(2,1)}, u32[]{:S(2)}, u32[]{:S(2)}) async-start(bf16[30,128,128]{2,0,1:T(8,128)(2,1)} %copy.24), calls=%async_computation.1 | async-start | bytes 2097152 | tf_op jit(solution)/shard_map/all_to_all | solution.py:117
  84.8 1.9 convert_reduce_fusion
  89.9 8.5 %shard_map.112 = (bf16[30,128,128]{2,1,0:T(8,128)(2,1)}, f32[5,128,128]{2,1,0:T(8,128)}) custom-call(s32[1]{0:T(128)} %get-tuple-element.48.dil_ref, bf16[30,128,128]{2,1,0:T(8,128)(2,1)} %get-tuple-element.16.act_ref, bf16[30,128,128]{2,1,0:T(8,128)(2,1)} %fusion.2.grad_ref, bf16[640,128]{1,0:T(8,128)(2,1)} %bitcast.290, ...), custom_call_target="tpu_custom_call" | custom-call | flops 1761607680 | bytes 4915200 | tf_op jit(solution)/shard_map/pallas_call | solution.py:265
  98.4 7.6 %shard_map.113 = (bf16[30,128,128]{2,1,0:T(8,128)(2,1)}, f32[5,128,128]{2,1,0:T(8,128)}) custom-call(s32[1]{0:T(128)} %get-tuple-element.47.dil_ref, bf16[30,128,128]{2,1,0:T(8,128)(2,1)} %copy.23.act_ref, bf16[30,128,128]{2,1,0:T(8,128)(2,1)} %get-tuple-element.21.grad_ref, bf16[640,128]{1,0:T(8,128)(2,1)} %bitcast.288), custom_call_target="tpu_custom_call" | custom-call | flops 1761607680 | bytes 4915200 | tf_op jit(solution)/shard_map/pallas_call | solution.py:265
  106.0 2.8 %copy.29 = bf16[30,128,128]{2,0,1:T(8,128)(2,1)} copy(bf16[30,128,128]{2,1,0:T(8,128)(2,1)} %get-tuple-element.22) | data formatting | bytes 1966080 | tf_op jit(solution)/shard_map/pallas_call | solution.py:265
  108.8 10.2 %all-to-all-start.3 = ((bf16[30,128,128]{2,0,1:T(8,128)(2,1)}), bf16[30,128,128]{2,0,1:T(8,128)(2,1)}, u32[]{:S(2)}, u32[]{:S(2)}) async-start(bf16[30,128,128]{2,0,1:T(8,128)(2,1)} %copy.29), calls=%async_computation.3 | async-start | bytes 2097152 | tf_op jit(solution)/shard_map/all_to_all | solution.py:117
  119.1 2.6 %copy.25 = bf16[30,128,128]{2,1,0:T(8,128)(2,1)} copy(bf16[30,128,128]{2,0,1:T(8,128)(2,1)} %all-to-all-done.1) | data formatting | bytes 1966080 | tf_op jit(solution)/shard_map/all_to_all | solution.py:117
  124.2 13.4 %all-to-all-done.3 = bf16[30,128,128]{2,0,1:T(8,128)(2,1)} async-done(((bf16[30,128,128]{2,0,1:T(8,128)(2,1)}), bf16[30,128,128]{2,0,1:T(8,128)(2,1)}, u32[]{:S(2)}, u32[]{:S(2)}) %all-to-all-start.3) | async-done | bytes 983072 | tf_op jit(solution)/shard_map/all_to_all | solution.py:117
  137.7 2.0 multiply_convert_fusion
  145.8 4.4 %all-to-all-start.4 = ((f32[128,24,128]{2,1,0:T(8,128)}), f32[128,24,128]{2,1,0:T(8,128)S(1)}, u32[]{:S(2)}, u32[]{:S(2)}) async-start(f32[128,24,128]{2,1,0:T(8,128)} %bitcast.243), calls=%async_computation.4 | async-start | bytes 3145728 | tf_op jit(solution)/shard_map/all_to_all | solution.py:295
  152.5 3.3 %pad_slice_fusion = (bf16[1,32,120,128]{3,2,1,0:T(8,128)(2,1)}, bf16[1,32,120,128]{3,2,1,0:T(8,128)(2,1)S(1)}, bf16[1,32,120,128]{3,2,1,0:T(8,128)(2,1)S(1)}, bf...) fusion(bf16[1,32,120,128]{3,2,1,0:T(8,128)(2,1)S(1)} %multiply_, ...), kind=kLoop, calls=%fused_computation.62 | loop fusion | bytes 8847360 | tf_op jit(solution)/shard_map/slice | solution.py:51
  159.4 2.5 %convolution_add_fusion.5 = f32[3840,128]{1,0:T(8,128)} fusion(f32[3840,128]{1,0:T(8,128)S(1)} %convolution_add_fusion.6, bf16[3840,128]{1,0:T(8,128)(2,1)S(1)} %bitcast.253, bf16[9,128,128]{2,1,0:T(8,128)(2,1)} %param.8), kind=kOutput, calls=%fused_computation.5 | convolution fusion | flops 126320640 | bytes 4947968 | tf_op jit(solution)/shard_map/dot_general | solution.py:54
  163.5 11.2 %all-to-all-done.4 = f32[128,24,128]{2,1,0:T(8,128)S(1)} async-done(((f32[128,24,128]{2,1,0:T(8,128)}), f32[128,24,128]{2,1,0:T(8,128)S(1)}, u32[]{:S(2)}, u32[]{:S(2)}) %all-to-all-start.4) | async-done | bytes 1572896 | tf_op jit(solution)/shard_map/all_to_all | solution.py:295
  176.2 4.4 %all-to-all-start.5 = ((f32[128,24,128]{2,1,0:T(8,128)}), f32[128,24,128]{2,1,0:T(8,128)S(1)}, u32[]{:S(2)}, u32[]{:S(2)}) async-start(f32[128,24,128]{2,1,0:T(8,128)} %broadcast_in_dim.8), calls=%async_computation.5 | async-start | bytes 3145728 | tf_op jit(solution)/shard_map/all_to_all | solution.py:298
  186.2 2.1 %fusion = bf16[3840,128]{1,0:T(8,128)(2,1)} fusion(f32[3840,128]{1,0:T(8,128)S(1)} %convolution_add_fusion.1, bf16[3840,128]{1,0:T(8,128)(2,1)S(1)} %bitcast.265, bf16[9,128,128]{2,1,0:T(8,128)(2,1)} %param.8), kind=kOutput, calls=%fused_computation.16 | convolution fusion | flops 126812160 | bytes 3964928 | tf_op jit(solution)/shard_map/dot_general | solution.py:54
  188.3 16.9 %all-to-all-done.5 = f32[128,24,128]{2,1,0:T(8,128)S(1)} async-done(((f32[128,24,128]{2,1,0:T(8,128)}), f32[128,24,128]{2,1,0:T(8,128)S(1)}, u32[]{:S(2)}, u32[]{:S(2)}) %all-to-all-start.5) | async-done | bytes 1572896 | tf_op jit(solution)/shard_map/all_to_all | solution.py:298
  (97 shorter events, 41.4 us)
Async XLA Ops:
  0.6 6.8 %copy-start.13 = (bf16[9,128,128]{2,1,0:T(8,128)(2,1)S(1)}, bf16[9,128,128]{2,1,0:T(8,128)(2,1)}, u32[]{:S(2)}) copy-start(bf16[9,128,128]{2,1,0:T(8,128)(2,1)} %param.8) | copy-start | bytes 884740
  8.6 1.2 copy-start
  12.4 13.1 %copy-start.19 = (s32[8]{0:T(128)S(1)}, s32[8]{0:T(128)}, u32[]{:S(2)}) copy-start(s32[8]{0:T(128)} %param.11) | copy-start | bytes 100
  12.4 13.2 %copy-start.16 = (bf16[2,5,128,128]{3,2,1,0:T(8,128)(2,1)S(1)}, bf16[2,5,128,128]{3,2,1,0:T(8,128)(2,1)}, u32[]{:S(2)}) copy-start(bf16[2,5,128,128]{3,2,1,0:T(8,128)(2,1)} %param.9) | copy-start | bytes 983044
  14.0 30.5 %all-to-all-start = ((bf16[30,128,128]{2,0,1:T(8,128)(2,1)}), bf16[30,128,128]{2,0,1:T(8,128)(2,1)S(1)}, u32[]{:S(2)}, u32[]{:S(2)}) async-start(bf16[30,128,128]{2,0,1:T(8,128)(2,1)} %copy.22), calls=%async_computation | async-start | bytes 2097152 | tf_op jit(solution)/shard_map/all_to_all | solution.py:113
  44.5 3.2 %copy-start.4 = (bf16[30,128,128]{2,0,1:T(8,128)(2,1)}, bf16[30,128,128]{2,0,1:T(8,128)(2,1)S(1)}, u32[]{:S(2)}) copy-start(bf16[30,128,128]{2,0,1:T(8,128)(2,1)S(1)} %all-to-all-done) | copy-start | bytes 2949124
  44.5 7.7 %copy-start.18 = (s32[2]{0:T(128)S(1)}, s32[2]{0:T(128)}, u32[]{:S(2)}) copy-start(s32[2]{0:T(128)} %param.12) | copy-start | bytes 28
  47.7 25.8 %all-to-all-start.2 = ((bf16[30,128,128]{2,0,1:T(8,128)(2,1)}), bf16[30,128,128]{2,0,1:T(8,128)(2,1)S(1)}, u32[]{:S(2)}, u32[]{:S(2)}) async-start(bf16[30,128,128]{2,0,1:T(8,128)(2,1)} %copy.26), calls=%async_computation.2 | async-start | bytes 2097152 | tf_op jit(solution)/shard_map/all_to_all | solution.py:113
  62.5 8.9 %copy-start.17 = (bf16[2,128,128]{2,1,0:T(8,128)(2,1)S(1)}, bf16[2,128,128]{2,1,0:T(8,128)(2,1)}, u32[]{:S(2)}) copy-start(bf16[2,128,128]{2,1,0:T(8,128)(2,1)} %param.10) | copy-start | bytes 196612
  69.8 1.8 copy-start.8
  74.5 34.3 %all-to-all-start.1 = ((bf16[30,128,128]{2,0,1:T(8,128)(2,1)}), bf16[30,128,128]{2,0,1:T(8,128)(2,1)}, u32[]{:S(2)}, u32[]{:S(2)}) async-start(bf16[30,128,128]{2,0,1:T(8,128)(2,1)} %copy.24), calls=%async_computation.1 | async-start | bytes 2097152 | tf_op jit(solution)/shard_map/all_to_all | solution.py:117
  86.7 1.5 copy-start.12
  108.8 28.8 %all-to-all-start.3 = ((bf16[30,128,128]{2,0,1:T(8,128)(2,1)}), bf16[30,128,128]{2,0,1:T(8,128)(2,1)}, u32[]{:S(2)}, u32[]{:S(2)}) async-start(bf16[30,128,128]{2,0,1:T(8,128)(2,1)} %copy.29), calls=%async_computation.3 | async-start | bytes 2097152 | tf_op jit(solution)/shard_map/all_to_all | solution.py:117
  121.6 1.2 copy-start.9
  121.8 1.5 copy-start.14
  121.8 1.5 copy-start.15
  124.2 15.5 %copy-start.1 = (bf16[1,32,120,128]{3,2,1,0:T(8,128)(2,1)S(1)}, bf16[1,32,120,128]{3,2,1,0:T(8,128)(2,1)}, u32[]{:S(2)}) copy-start(bf16[1,32,120,128]{3,2,1,0:T(8,128)(2,1)} %param.7) | copy-start | bytes 2949124
  145.8 29.0 %all-to-all-start.4 = ((f32[128,24,128]{2,1,0:T(8,128)}), f32[128,24,128]{2,1,0:T(8,128)S(1)}, u32[]{:S(2)}, u32[]{:S(2)}) async-start(f32[128,24,128]{2,1,0:T(8,128)} %bitcast.243), calls=%async_computation.4 | async-start | bytes 3145728 | tf_op jit(solution)/shard_map/all_to_all | solution.py:295
  176.2 4.4 %copy-start.2 = (f32[3840,128]{1,0:T(8,128)S(1)}, f32[3840,128]{1,0:T(8,128)}, u32[]{:S(2)}) copy-start(f32[3840,128]{1,0:T(8,128)} %convolution_add_fusion.5) | copy-start | bytes 5898244
  176.2 29.0 %all-to-all-start.5 = ((f32[128,24,128]{2,1,0:T(8,128)}), f32[128,24,128]{2,1,0:T(8,128)S(1)}, u32[]{:S(2)}, u32[]{:S(2)}) async-start(f32[128,24,128]{2,1,0:T(8,128)} %broadcast_in_dim.8), calls=%async_computation.5 | async-start | bytes 3145728 | tf_op jit(solution)/shard_map/all_to_all | solution.py:298
  180.6 1.7 copy-start.7
  182.3 1.3 copy-start.6
  183.6 1.3 copy-start.5
  184.9 1.3 copy-start.10
  (2 other events, 2.1 us)

commit v5 on v3

--- a/solution.py
+++ b/solution.py
@@ -293,10 +293,10 @@
     rows.append(jnp.zeros((per * count - used, chans), jnp.float32))
     stack = jnp.concatenate(rows, axis=0).reshape(count, per, chans)
     pieces = lax.all_to_all(stack, ("seg", "grp"), split_axis=0, concat_axis=0, tiled=True)
-    mine = jnp.sum(pieces, axis=0, keepdims=True) * scale
+    mine = (jnp.sum(pieces, axis=0, keepdims=True) * scale).astype(jnp.bfloat16)
     spread = jnp.broadcast_to(mine, stack.shape)
     whole = lax.all_to_all(spread, ("seg", "grp"), split_axis=0, concat_axis=0, tiled=True)
-    whole = whole.reshape(-1, chans)
+    whole = whole.astype(jnp.float32).reshape(-1, chans)
     out = []
     offset = 0
     for p in parts:

time: 204 us -> 195 us (0.956)
  matrix products: 25.1 us -> 19.1 us
    dot_general x9, matrix products: 13.6 us -> 7.56 us  [spatial_back(): jnp.dot(piece, kernel[3 * row_tap + col_tap].T, preferred_element_type=jn...]
    all_to_all x1, waiting for transfers between devices: 16.9 us -> 11.2 us  [all_sum(): lax.all_to_all(spread, ('seg', 'grp'), split_axis=0, concat_axis=0, tiled...]
    all_to_all x1, waiting for transfers between devices: 11.2 us -> 15.8 us  [all_sum(): lax.all_to_all(stack, ('seg', 'grp'), split_axis=0, concat_axis=0, tiled=...]
  transfers between devices with their start and end apart: 6 -> 6, of which waited for: 5 -> 5; matrix products, arithmetic and copies ran while one was open for 20% -> 17% of each run, Pallas kernels for 12% -> 13%
where the time goes in v5:
time: 195 us; the launch traced here: 194 us
  waiting for transfers between devices  59.2 us (30%)
  starting transfers between devices  44.5 us (23%)
  local copies, waits for them, and re-layouts  32.7 us (17%)
  Pallas kernels  24.9 us (13%)
  matrix products  19.1 us (10%)
  other arithmetic  12.1 us (6%)
    all_to_all x2, starting transfers between devices, to_frames(): lax.all_to_all(blocks, ('seg', 'grp'), split_axis=1, concat_axis=1, tiled...  19.8 us
    all_to_all x2, waiting for transfers between devices, to_pixels(): lax.all_to_all(strided, ('seg', 'grp'), split_axis=1, concat_axis=1, tile...  18.8 us
    all_to_all x2, starting transfers between devices, to_pixels(): lax.all_to_all(strided, ('seg', 'grp'), split_axis=1, concat_axis=1, tile...  15.9 us
    all_to_all x1, waiting for transfers between devices, all_sum(): lax.all_to_all(stack, ('seg', 'grp'), split_axis=0, concat_axis=0, tiled=...  15.8 us
    pallas_call x2, Pallas kernels, temporal_backward_k(): pl.pallas_call(functools.partial(tbwd_kernel, with_pre), grid_spec=pltpu....  13.5 us
    all_to_all x2, waiting for transfers between devices, to_frames(): lax.all_to_all(blocks, ('seg', 'grp'), split_axis=1, concat_axis=1, tiled...  13.4 us
    pallas_call x2, Pallas kernels, temporal_forward_k(): pl.pallas_call(tfwd_kernel, grid_spec=pltpu.PrefetchScalarGridSpec(num_sc...  11.4 us
    all_to_all x1, waiting for transfers between devices, all_sum(): lax.all_to_all(spread, ('seg', 'grp'), split_axis=0, concat_axis=0, tiled...  11.2 us
  transfers between devices with their start and end apart: 6, of which 5 were waited for; matrix products, arithmetic and copies ran while one was open for 17% of the time, Pallas kernels for 13%

profile of v5, /device:TPU:1, one launch (start us, length us, event | category | flops | bytes accessed | tf_op | source)
XLA Modules:
  0.0 193.6 jit_solution(3192086991222034412)
XLA Ops:
  0.6 6.7 %pad_slice_fusion.8 = (bf16[1,32,120,128]{3,2,1,0:T(8,128)(2,1)S(1)}, bf16[1,32,120,128]{3,2,1,0:T(8,128)(2,1)S(1)}, bf16[1,32,120,128]{3,2,1,0:T(8,128)(2,1)S(1...) fusion(bf16[1,32,120,128]{3,2,1,0:T(8,128)(2,1)} %param.7), kind=kLoop, calls=%fused_computation.70 | loop fusion | bytes 8847360 | tf_op jit(solution)/shard_map/slice | solution.py:36
  14.0 11.5 %all-to-all-start = ((bf16[30,128,128]{2,0,1:T(8,128)(2,1)}), bf16[30,128,128]{2,0,1:T(8,128)(2,1)S(1)}, u32[]{:S(2)}, u32[]{:S(2)}) async-start(bf16[30,128,128]{2,0,1:T(8,128)(2,1)} %copy.22), calls=%async_computation | async-start | bytes 2097152 | tf_op jit(solution)/shard_map/all_to_all | solution.py:113
  26.4 18.1 %all-to-all-done = bf16[30,128,128]{2,0,1:T(8,128)(2,1)S(1)} async-done(((bf16[30,128,128]{2,0,1:T(8,128)(2,1)}), bf16[30,128,128]{2,0,1:T(8,128)(2,1)S(1)}, u32[]{:S(2)}, u32[]{:S(2)}) %all-to-all-start) | async-done | bytes 983072 | tf_op jit(solution)/shard_map/all_to_all | solution.py:113
  44.5 3.3 %copy.26 = bf16[30,128,128]{2,0,1:T(8,128)(2,1)} copy(bf16[30,128,128]{2,1,0:T(8,128)(2,1)} %bitcast.276) | data formatting | bytes 1966080 | tf_op jit(solution)/shard_map/reshape | solution.py:112
  47.7 4.4 %all-to-all-start.2 = ((bf16[30,128,128]{2,0,1:T(8,128)(2,1)}), bf16[30,128,128]{2,0,1:T(8,128)(2,1)S(1)}, u32[]{:S(2)}, u32[]{:S(2)}) async-start(bf16[30,128,128]{2,0,1:T(8,128)(2,1)} %copy.26), calls=%async_computation.2 | async-start | bytes 2097152 | tf_op jit(solution)/shard_map/all_to_all | solution.py:113
  52.7 2.5 %copy.23.act_ref = bf16[30,128,128]{2,1,0:T(8,128)(2,1)} copy(bf16[30,128,128]{2,0,1:T(8,128)(2,1)} %copy-done.3) | data formatting | bytes 1966080 | tf_op jit(solution)/shard_map/optimization_barrier | solution.py:319
  55.3 5.7 %shard_map.110 = (f32[30,128,128]{2,1,0:T(8,128)}, bf16[30,128,128]{2,1,0:T(8,128)(2,1)}) custom-call(s32[1]{0:T(128)} %get-tuple-element.47.dil_ref, bf16[30,128,128]{2,1,0:T(8,128)(2,1)} %copy.23.act_ref, bf16[640,128]{1,0:T(8,128)(2,1)} %bitcast.287), custom_call_target="tpu_custom_call" | custom-call | flops 1132462080 | bytes 3932160 | tf_op jit(solution)/shard_map/pallas_call | solution.py:201
  61.0 5.7 %shard_map.111 = (f32[30,128,128]{2,1,0:T(8,128)}, bf16[30,128,128]{2,1,0:T(8,128)(2,1)}) custom-call(s32[1]{0:T(128)} %get-tuple-element.48.dil_ref, bf16[30,128,128]{2,1,0:T(8,128)(2,1)} %get-tuple-element.16.act_ref, bf16[640,128]{1,0:T(8,128)(2,1)} %bitcast.289), custom_call_target="tpu_custom_call" | custom-call | flops 1132462080 | bytes 3932160 | tf_op jit(solution)/shard_map/pallas_call | solution.py:201
  72.1 9.6 %all-to-all-start.1 = ((bf16[30,128,128]{2,0,1:T(8,128)(2,1)}), bf16[30,128,128]{2,0,1:T(8,128)(2,1)}, u32[]{:S(2)}, u32[]{:S(2)}) async-start(bf16[30,128,128]{2,0,1:T(8,128)(2,1)} %copy.24), calls=%async_computation.1 | async-start | bytes 2097152 | tf_op jit(solution)/shard_map/all_to_all | solution.py:117
  81.7 1.9 convert_reduce_fusion
  85.2 1.7 fusion.2.grad_ref
  86.9 7.2 %shard_map.112 = (bf16[30,128,128]{2,1,0:T(8,128)(2,1)}, f32[5,128,128]{2,1,0:T(8,128)}) custom-call(s32[1]{0:T(128)} %get-tuple-element.48.dil_ref, bf16[30,128,128]{2,1,0:T(8,128)(2,1)} %get-tuple-element.16.act_ref, bf16[30,128,128]{2,1,0:T(8,128)(2,1)} %fusion.2.grad_ref, bf16[640,128]{1,0:T(8,128)(2,1)} %bitcast.290, ...), custom_call_target="tpu_custom_call" | custom-call | flops 1761607680 | bytes 4915200 | tf_op jit(solution)/shard_map/pallas_call | solution.py:265
  94.0 6.4 %shard_map.113 = (bf16[30,128,128]{2,1,0:T(8,128)(2,1)}, f32[5,128,128]{2,1,0:T(8,128)}) custom-call(s32[1]{0:T(128)} %get-tuple-element.47.dil_ref, bf16[30,128,128]{2,1,0:T(8,128)(2,1)} %copy.23.act_ref, bf16[30,128,128]{2,1,0:T(8,128)(2,1)} %get-tuple-element.21.grad_ref, bf16[640,128]{1,0:T(8,128)(2,1)} %bitcast.288), custom_call_target="tpu_custom_call" | custom-call | flops 1761607680 | bytes 4915200 | tf_op jit(solution)/shard_map/pallas_call | solution.py:265
  100.4 2.8 %copy.29 = bf16[30,128,128]{2,0,1:T(8,128)(2,1)} copy(bf16[30,128,128]{2,1,0:T(8,128)(2,1)} %get-tuple-element.22) | data formatting | bytes 1966080 | tf_op jit(solution)/shard_map/pallas_call | solution.py:265
  103.2 10.2 %all-to-all-start.3 = ((bf16[30,128,128]{2,0,1:T(8,128)(2,1)}), bf16[30,128,128]{2,0,1:T(8,128)(2,1)}, u32[]{:S(2)}, u32[]{:S(2)}) async-start(bf16[30,128,128]{2,0,1:T(8,128)(2,1)} %copy.29), calls=%async_computation.3 | async-start | bytes 2097152 | tf_op jit(solution)/shard_map/all_to_all | solution.py:117
  113.4 2.6 %copy.25 = bf16[30,128,128]{2,1,0:T(8,128)(2,1)} copy(bf16[30,128,128]{2,0,1:T(8,128)(2,1)} %all-to-all-done.1) | data formatting | bytes 1966080 | tf_op jit(solution)/shard_map/all_to_all | solution.py:117
  118.6 13.4 %all-to-all-done.3 = bf16[30,128,128]{2,0,1:T(8,128)(2,1)} async-done(((bf16[30,128,128]{2,0,1:T(8,128)(2,1)}), bf16[30,128,128]{2,0,1:T(8,128)(2,1)}, u32[]{:S(2)}, u32[]{:S(2)}) %all-to-all-start.3) | async-done | bytes 983072 | tf_op jit(solution)/shard_map/all_to_all | solution.py:117
  132.0 2.0 %multiply_convert_fusion = bf16[30,128,128]{2,1,0:T(8,128)(2,1)S(1)} fusion(f32[30,128,128]{2,1,0:T(8,128)S(1)} %bitcast.237, bf16[30,128,128]{2,0,1:T(8,128)(2,1)} %all-to-all-done.3), kind=kLoop, calls=%fused_computation.21 | loop fusion | flops 4915200 | bytes 3932160 | tf_op jit(solution)/shard_map/convert_element_type | solution.py:366
  140.2 4.4 %all-to-all-start.4 = ((f32[128,24,128]{2,1,0:T(8,128)}), f32[128,24,128]{2,1,0:T(8,128)S(1)}, u32[]{:S(2)}, u32[]{:S(2)}) async-start(f32[128,24,128]{2,1,0:T(8,128)} %bitcast.243), calls=%async_computation.4 | async-start | bytes 3145728 | tf_op jit(solution)/shard_map/all_to_all | solution.py:295
  146.9 3.2 %pad_slice_fusion = (bf16[1,32,120,128]{3,2,1,0:T(8,128)(2,1)}, bf16[1,32,120,128]{3,2,1,0:T(8,128)(2,1)S(1)}, bf16[1,32,120,128]{3,2,1,0:T(8,128)(2,1)S(1)}, bf...) fusion(bf16[1,32,120,128]{3,2,1,0:T(8,128)(2,1)S(1)} %multiply_, ...), kind=kLoop, calls=%fused_computation.62 | loop fusion | bytes 8847360 | tf_op jit(solution)/shard_map/slice | solution.py:51
  153.4 15.8 %all-to-all-done.4 = f32[128,24,128]{2,1,0:T(8,128)S(1)} async-done(((f32[128,24,128]{2,1,0:T(8,128)}), f32[128,24,128]{2,1,0:T(8,128)S(1)}, u32[]{:S(2)}, u32[]{:S(2)}) %all-to-all-start.4) | async-done | bytes 1572896 | tf_op jit(solution)/shard_map/all_to_all | solution.py:295
  170.4 4.4 %all-to-all-start.5 = ((bf16[128,24,128]{2,1,0:T(8,128)(2,1)}), bf16[128,24,128]{2,1,0:T(8,128)(2,1)S(1)}, u32[]{:S(2)}, u32[]{:S(2)}) async-start(bf16[128,24,128]{2,1,0:T(8,128)(2,1)} %broadcast_in_dim.8), calls=%async_computation.5 | async-start | bytes 1572864 | tf_op jit(solution)/shard_map/all_to_all | solution.py:298
  177.8 2.1 %fusion = bf16[3840,128]{1,0:T(8,128)(2,1)} fusion(f32[3840,128]{1,0:T(8,128)S(1)} %convolution_add_fusion.1, bf16[3840,128]{1,0:T(8,128)(2,1)S(1)} %bitcast.263, bf16[9,128,128]{2,1,0:T(8,128)(2,1)} %param.8), kind=kOutput, calls=%fused_computation.16 | convolution fusion | flops 126812160 | bytes 3964928 | tf_op jit(solution)/shard_map/dot_general | solution.py:54
  179.9 11.2 %all-to-all-done.5 = bf16[128,24,128]{2,1,0:T(8,128)(2,1)S(1)} async-done(((bf16[128,24,128]{2,1,0:T(8,128)(2,1)}), bf16[128,24,128]{2,1,0:T(8,128)(2,1)S(1)}, u32[]{:S(2)}, u32[]{:S(2)}) %all-to-all-start.5) | async-done | bytes 786464 | tf_op jit(solution)/shard_map/all_to_all | solution.py:298
  (94 shorter events, 35.6 us)
Async XLA Ops:
  0.6 6.8 %copy-start.10 = (bf16[9,128,128]{2,1,0:T(8,128)(2,1)S(1)}, bf16[9,128,128]{2,1,0:T(8,128)(2,1)}, u32[]{:S(2)}) copy-start(bf16[9,128,128]{2,1,0:T(8,128)(2,1)} %param.8) | copy-start | bytes 884740
  8.6 1.2 copy-start
  12.4 13.2 %copy-start.17 = (s32[8]{0:T(128)S(1)}, s32[8]{0:T(128)}, u32[]{:S(2)}) copy-start(s32[8]{0:T(128)} %param.11) | copy-start | bytes 100
  12.4 13.2 %copy-start.14 = (bf16[2,5,128,128]{3,2,1,0:T(8,128)(2,1)S(1)}, bf16[2,5,128,128]{3,2,1,0:T(8,128)(2,1)}, u32[]{:S(2)}) copy-start(bf16[2,5,128,128]{3,2,1,0:T(8,128)(2,1)} %param.9) | copy-start | bytes 983044
  14.0 30.5 %all-to-all-start = ((bf16[30,128,128]{2,0,1:T(8,128)(2,1)}), bf16[30,128,128]{2,0,1:T(8,128)(2,1)S(1)}, u32[]{:S(2)}, u32[]{:S(2)}) async-start(bf16[30,128,128]{2,0,1:T(8,128)(2,1)} %copy.22), calls=%async_computation | async-start | bytes 2097152 | tf_op jit(solution)/shard_map/all_to_all | solution.py:113
  44.5 3.3 %copy-start.3 = (bf16[30,128,128]{2,0,1:T(8,128)(2,1)}, bf16[30,128,128]{2,0,1:T(8,128)(2,1)S(1)}, u32[]{:S(2)}) copy-start(bf16[30,128,128]{2,0,1:T(8,128)(2,1)S(1)} %all-to-all-done) | copy-start | bytes 2949124
  44.5 7.7 %copy-start.16 = (s32[2]{0:T(128)S(1)}, s32[2]{0:T(128)}, u32[]{:S(2)}) copy-start(s32[2]{0:T(128)} %param.12) | copy-start | bytes 28
  47.7 23.4 %all-to-all-start.2 = ((bf16[30,128,128]{2,0,1:T(8,128)(2,1)}), bf16[30,128,128]{2,0,1:T(8,128)(2,1)S(1)}, u32[]{:S(2)}, u32[]{:S(2)}) async-start(bf16[30,128,128]{2,0,1:T(8,128)(2,1)} %copy.26), calls=%async_computation.2 | async-start | bytes 2097152 | tf_op jit(solution)/shard_map/all_to_all | solution.py:113
  61.0 7.3 %copy-start.15 = (bf16[2,128,128]{2,1,0:T(8,128)(2,1)S(1)}, bf16[2,128,128]{2,1,0:T(8,128)(2,1)}, u32[]{:S(2)}) copy-start(bf16[2,128,128]{2,1,0:T(8,128)(2,1)} %param.10) | copy-start | bytes 196612
  66.7 1.8 copy-start.5
  71.1 1.0 copy-start.2
  72.1 31.1 %all-to-all-start.1 = ((bf16[30,128,128]{2,0,1:T(8,128)(2,1)}), bf16[30,128,128]{2,0,1:T(8,128)(2,1)}, u32[]{:S(2)}, u32[]{:S(2)}) async-start(bf16[30,128,128]{2,0,1:T(8,128)(2,1)} %copy.24), calls=%async_computation.1 | async-start | bytes 2097152 | tf_op jit(solution)/shard_map/all_to_all | solution.py:117
  83.6 1.5 copy-start.9
  103.2 28.8 %all-to-all-start.3 = ((bf16[30,128,128]{2,0,1:T(8,128)(2,1)}), bf16[30,128,128]{2,0,1:T(8,128)(2,1)}, u32[]{:S(2)}, u32[]{:S(2)}) async-start(bf16[30,128,128]{2,0,1:T(8,128)(2,1)} %copy.29), calls=%async_computation.3 | async-start | bytes 2097152 | tf_op jit(solution)/shard_map/all_to_all | solution.py:117
  116.0 1.2 copy-start.6
  116.2 1.5 copy-start.12
  116.2 1.5 copy-start.13
  118.6 15.5 %copy-start.1 = (bf16[1,32,120,128]{3,2,1,0:T(8,128)(2,1)S(1)}, bf16[1,32,120,128]{3,2,1,0:T(8,128)(2,1)}, u32[]{:S(2)}) copy-start(bf16[1,32,120,128]{3,2,1,0:T(8,128)(2,1)} %param.7) | copy-start | bytes 2949124
  137.5 1.1 copy-start.8
  140.2 29.0 %all-to-all-start.4 = ((f32[128,24,128]{2,1,0:T(8,128)}), f32[128,24,128]{2,1,0:T(8,128)S(1)}, u32[]{:S(2)}, u32[]{:S(2)}) async-start(f32[128,24,128]{2,1,0:T(8,128)} %bitcast.243), calls=%async_computation.4 | async-start | bytes 3145728 | tf_op jit(solution)/shard_map/all_to_all | solution.py:295
  146.9 3.2 %copy-start.11 = (bf16[9,128,128]{2,1,0:T(8,128)(2,1)S(1)}, bf16[9,128,128]{2,1,0:T(8,128)(2,1)}, u32[]{:S(2)}) copy-start(bf16[9,128,128]{2,1,0:T(8,128)(2,1)} %param.8) | copy-start | bytes 884740
  170.4 20.7 %all-to-all-start.5 = ((bf16[128,24,128]{2,1,0:T(8,128)(2,1)}), bf16[128,24,128]{2,1,0:T(8,128)(2,1)S(1)}, u32[]{:S(2)}, u32[]{:S(2)}) async-start(bf16[128,24,128]{2,1,0:T(8,128)(2,1)} %broadcast_in_dim.8), calls=%async_computation.5 | async-start | bytes 1572864 | tf_op jit(solution)/shard_map/all_to_all | solution.py:298
  174.8 1.7 copy-start.4
  176.5 1.3 copy-start.7

commit v6 on v5

--- a/solution.py
+++ b/solution.py
@@ -153,132 +153,150 @@
     )
 
 
-JB = 10
-
-
-def shift_matrix(offset, size):
-    rows = lax.broadcasted_iota(jnp.int32, (size, size), 0)
-    cols = lax.broadcasted_iota(jnp.int32, (size, size), 1)
-    return (cols == rows + offset).astype(jnp.bfloat16)
-
-
-def shifted_taps(x_ref, step, sign):
-    blocks, frames, chans = x_ref.shape
-    wide = jnp.concatenate([x_ref[j] for j in range(blocks)], axis=1)
-    taps = []
-    for tap in range(5):
-        if tap == 2:
-            taps.append(None)
-            continue
-        moved = jnp.dot(
-            shift_matrix(sign * (tap - 2) * step, frames), wide,
-            preferred_element_type=jnp.float32,
-        ).astype(jnp.bfloat16)
-        taps.append(moved)
-    rows = []
-    for j in range(blocks):
-        parts = []
-        for tap in range(5):
-            if tap == 2:
-                parts.append(x_ref[j])
-            else:
-                parts.append(taps[tap][:, j * chans : (j + 1) * chans])
-        rows.append(jnp.concatenate(parts, axis=1))
-    return jnp.concatenate(rows, axis=0)
-
-
-def tfwd_kernel(dil_ref, act_ref, w_ref, pre_ref, out_ref):
-    blocks, frames, chans = act_ref.shape
-    stacked = shifted_taps(act_ref, dil_ref[0], 1)
-    pre = jnp.dot(stacked, w_ref[...], preferred_element_type=jnp.float32)
-    pre_ref[...] = pre.reshape(blocks, frames, chans)
-    out_ref[...] = (pre / (1.0 + jnp.exp(-pre))).astype(jnp.bfloat16).reshape(blocks, frames, chans)
+HALO = 2 * DMAX
+FB = 16
+
+
+def fm_to_pixels(flat):
+    count = lax.axis_size(("seg", "grp"))
+    chans = flat.shape[-1]
+    strided = flat.reshape(-1, count, chans)
+    rows = -(-strided.shape[0] // 16) * 16
+    strided = jnp.pad(strided, ((0, rows - strided.shape[0]), (0, 0), (0, 0)))
+    out = lax.all_to_all(strided, ("seg", "grp"), split_axis=1, concat_axis=1, tiled=True)
+    return jnp.transpose(out, (1, 0, 2))
+
+
+def fm_to_frames(blocks, used):
+    moved = jnp.transpose(blocks, (1, 0, 2))
+    out = lax.all_to_all(moved, ("seg", "grp"), split_axis=1, concat_axis=1, tiled=True)
+    return out[:used].reshape(1, -1, blocks.shape[-1])
+
+
+def fill_halo(src_ref, pad_ref):
+    frames = src_ref.shape[0]
+    zeros = jnp.zeros((HALO,) + pad_ref.shape[1:], pad_ref.dtype)
+    pad_ref[0:HALO] = zeros
+    pad_ref[HALO + frames : 2 * HALO + frames] = zeros
+    pad_ref[HALO : HALO + frames] = src_ref[...]
+
+
+def tap_rows(pad_ref, start, rows):
+    return pad_ref[pl.ds(start, FB)].reshape(rows, pad_ref.shape[-1])
+
+
+def tfwd_kernel(dil_ref, act_ref, w_ref, pre_ref, out_ref, pad_ref):
+    frames, width, chans = act_ref.shape
+    fill_halo(act_ref, pad_ref)
+    step = dil_ref[0]
+    rows = FB * width
+    for block in range(frames // FB):
+        base = HALO + block * FB
+        stacked = jnp.concatenate(
+            [tap_rows(pad_ref, base + (tap - 2) * step, rows) for tap in range(5)], axis=1
+        )
+        pre = jnp.dot(stacked, w_ref[...], preferred_element_type=jnp.float32)
+        pre_ref[block * FB : (block + 1) * FB] = pre.reshape(FB, width, chans)
+        out_ref[block * FB : (block + 1) * FB] = (
+            (pre / (1.0 + jnp.exp(-pre))).astype(jnp.bfloat16).reshape(FB, width, chans)
+        )
 
 
 def temporal_forward_k(acts, kernel, step_size):
-    count, frames, chans = acts.shape
-    spec = pl.BlockSpec((JB, frames, chans), lambda j, d: (j, 0, 0))
+    frames, width, chans = acts.shape
     return pl.pallas_call(
         tfwd_kernel,
         grid_spec=pltpu.PrefetchScalarGridSpec(
             num_scalar_prefetch=1,
-            grid=(count // JB,),
-            in_specs=[spec, pl.BlockSpec((5 * chans, chans), lambda j, d: (0, 0))],
-            out_specs=[spec, spec],
+            grid=(1,),
+            in_specs=[
+                pl.BlockSpec(acts.shape, lambda i, d: (0, 0, 0)),
+                pl.BlockSpec((5 * chans, chans), lambda i, d: (0, 0)),
+            ],
+            out_specs=[
+                pl.BlockSpec(acts.shape, lambda i, d: (0, 0, 0)),
+                pl.BlockSpec(acts.shape, lambda i, d: (0, 0, 0)),
+            ],
+            scratch_shapes=[pltpu.VMEM((frames + 2 * HALO, width, chans), jnp.bfloat16)],
         ),
         out_shape=[
             jax.ShapeDtypeStruct(acts.shape, jnp.float32),
             jax.ShapeDtypeStruct(acts.shape, jnp.bfloat16),
         ],
         cost_estimate=pl.CostEstimate(
-            flops=2 * count * frames * chans * chans * 9,
-            transcendentals=count * frames * chans,
-            bytes_accessed=count * frames * chans * 8,
+            flops=2 * frames * width * chans * chans * 5,
+            transcendentals=frames * width * chans,
+            bytes_accessed=frames * width * chans * 8,
         ),
     )(step_size.reshape(1), acts, kernel.reshape(5 * chans, chans))
 
 
 def tbwd_kernel(with_pre, dil_ref, act_ref, grad_ref, wt_ref, *rest):
     if with_pre:
-        pre_ref, out_ref, tg_ref = rest
+        pre_ref, out_ref, tg_ref, pad_ref = rest
     else:
-        out_ref, tg_ref = rest
-    blocks, frames, chans = act_ref.shape
-    stacked = shifted_taps(grad_ref, dil_ref[0], -1)
-    grad_act = None
+        out_ref, tg_ref, pad_ref = rest
+    frames, width, chans = act_ref.shape
+    fill_halo(grad_ref, pad_ref)
+    step = dil_ref[0]
+    rows = FB * width
+    total = None
+    for block in range(frames // FB):
+        base = HALO + block * FB
+        stacked = jnp.concatenate(
+            [tap_rows(pad_ref, base - (tap - 2) * step, rows) for tap in range(5)], axis=1
+        )
+        grad_act = None
+        for tap in range(5):
+            term = lax.dot_general(
+                stacked[:, tap * chans : (tap + 1) * chans],
+                wt_ref[tap * chans : (tap + 1) * chans, :],
+                (((1,), (1,)), ((), ())),
+                preferred_element_type=jnp.float32,
+            )
+            grad_act = term if grad_act is None else grad_act + term
+        flat_act = act_ref[block * FB : (block + 1) * FB].reshape(rows, chans)
+        part = lax.dot_general(
+            flat_act, stacked, (((0,), (0,)), ((), ())), preferred_element_type=jnp.float32
+        )
+        total = part if total is None else total + part
+        if with_pre:
+            pre = pre_ref[block * FB : (block + 1) * FB].reshape(rows, chans)
+            sigma = 1.0 / (1.0 + jnp.exp(-pre))
+            grad_act = grad_act * (sigma * (1.0 + pre * (1.0 - sigma)))
+        out_ref[block * FB : (block + 1) * FB] = (
+            grad_act.astype(jnp.bfloat16).reshape(FB, width, chans)
+        )
     for tap in range(5):
-        term = lax.dot_general(
-            stacked[:, tap * chans : (tap + 1) * chans],
-            wt_ref[tap * chans : (tap + 1) * chans, :],
-            (((1,), (1,)), ((), ())),
-            preferred_element_type=jnp.float32,
-        )
-        grad_act = term if grad_act is None else grad_act + term
-    flat_act = act_ref[...].reshape(blocks * frames, chans)
-    part = lax.dot_general(
-        flat_act, stacked, (((0,), (0,)), ((), ())), preferred_element_type=jnp.float32
-    )
-
-    @pl.when(pl.program_id(0) == 0)
-    def _():
-        tg_ref[...] = jnp.zeros_like(tg_ref)
-
-    for tap in range(5):
-        tg_ref[tap] += part[:, tap * chans : (tap + 1) * chans]
+        tg_ref[tap] = total[:, tap * chans : (tap + 1) * chans]
+
+
+def temporal_backward_k(acts, grads, kernel, step_size, pre_below):
+    frames, width, chans = acts.shape
+    full = pl.BlockSpec(acts.shape, lambda i, d: (0, 0, 0))
+    with_pre = pre_below is not None
+    in_specs = [full, full, pl.BlockSpec((5 * chans, chans), lambda i, d: (0, 0))]
+    operands = [step_size.reshape(1), acts, grads, kernel.reshape(5 * chans, chans)]
     if with_pre:
-        pre = pre_ref[...].reshape(blocks * frames, chans)
-        sigma = 1.0 / (1.0 + jnp.exp(-pre))
-        grad_act = grad_act * (sigma * (1.0 + pre * (1.0 - sigma)))
-    out_ref[...] = grad_act.astype(jnp.bfloat16).reshape(blocks, frames, chans)
-
-
-def temporal_backward_k(acts, grads, kernel, step_size, pre_below):
-    count, frames, chans = acts.shape
-    spec = pl.BlockSpec((JB, frames, chans), lambda j, d: (j, 0, 0))
-    wt = kernel.reshape(5 * chans, chans)
-    with_pre = pre_below is not None
-    in_specs = [spec, spec, pl.BlockSpec((5 * chans, chans), lambda j, d: (0, 0))]
-    operands = [step_size.reshape(1), acts, grads, wt]
-    if with_pre:
-        in_specs.append(spec)
+        in_specs.append(full)
         operands.append(pre_below)
     out, tg = pl.pallas_call(
         functools.partial(tbwd_kernel, with_pre),
         grid_spec=pltpu.PrefetchScalarGridSpec(
             num_scalar_prefetch=1,
-            grid=(count // JB,),
+            grid=(1,),
             in_specs=in_specs,
-            out_specs=[spec, pl.BlockSpec((5, chans, chans), lambda j, d: (0, 0, 0))],
+            out_specs=[full, pl.BlockSpec((5, chans, chans), lambda i, d: (0, 0, 0))],
+            scratch_shapes=[pltpu.VMEM((frames + 2 * HALO, width, chans), jnp.bfloat16)],
         ),
         out_shape=[
             jax.ShapeDtypeStruct(acts.shape, jnp.bfloat16),
             jax.ShapeDtypeStruct((5, chans, chans), jnp.float32),
         ],
-        compiler_params=pltpu.CompilerParams(dimension_semantics=("arbitrary",)),
         cost_estimate=pl.CostEstimate(
-            flops=2 * count * frames * chans * chans * 14,
-            transcendentals=count * frames * chans,
-            bytes_accessed=count * frames * chans * 10,
+            flops=2 * frames * width * chans * chans * 10,
+            transcendentals=frames * width * chans,
+            bytes_accessed=frames * width * chans * 10,
         ),
     )(*operands)
     return out, tg
@@ -312,14 +330,16 @@
     local_frames, rows, cols, chans = frames_in.shape
     pixels = rows * cols
     seg_count = lax.axis_size("seg")
+    count = lax.axis_size(("seg", "grp"))
+    used = pixels // count
     pre_spatial = spatial_forward(frames_in, spatial_weight)
     act_zero = jax.nn.silu(pre_spatial).astype(jnp.bfloat16).reshape(local_frames, pixels, chans)
     cot_local = cotangent.reshape(local_frames, pixels, chans)
-    act_blocks = to_pixels(act_zero)
+    act_blocks = fm_to_pixels(act_zero)
     act_blocks, cot_local = lax.optimization_barrier((act_blocks, cot_local))
-    cot_blocks = to_pixels(cot_local)
+    cot_blocks = fm_to_pixels(cot_local)
     acts = [act_blocks]
-    block, total_frames = act_blocks.shape[0], act_blocks.shape[1]
+    total_frames, width = act_blocks.shape[0], act_blocks.shape[1]
     seg_frames = total_frames // seg_count
     pres = []
     for layer in range(LAYERS):
@@ -327,32 +347,32 @@
         pres.append(pre)
         acts.append(act)
     feat = acts[-1]
-    seg_shape = (block, seg_count, seg_frames, chans)
+    seg_shape = (seg_count, seg_frames, width, chans)
     feat_seg = feat.reshape(seg_shape)
     positions = jnp.arange(seg_frames, dtype=jnp.int32)
     onehot = positions[None, :] == key_index[:, None]
     keys = jnp.einsum(
-        "ns,jnsc->jnc", onehot.astype(jnp.bfloat16), feat_seg, preferred_element_type=jnp.float32
+        "ns,nsjc->njc", onehot.astype(jnp.bfloat16), feat_seg, preferred_element_type=jnp.float32
     ).astype(jnp.bfloat16)
-    key_full = jnp.broadcast_to(keys[:, :, None], seg_shape).reshape(-1, chans)
+    key_full = jnp.broadcast_to(keys[:, None], seg_shape).reshape(-1, chans)
     feat_flat = feat.reshape(-1, chans)
     key_part = jnp.dot(
         keys.reshape(-1, chans), uniting_weight[1], preferred_element_type=jnp.float32
-    ).reshape(block, seg_count, 1, chans)
+    ).reshape(seg_count, 1, width, chans)
     main_part = jnp.dot(feat_flat, uniting_weight[0], preferred_element_type=jnp.float32)
     united_blocks = (main_part.reshape(seg_shape) + key_part).astype(jnp.bfloat16)
-    united = to_frames(united_blocks.reshape(block, total_frames, chans))
+    united = fm_to_frames(united_blocks.reshape(total_frames, width, chans), used)
     cot_flat = cot_blocks.reshape(-1, chans)
     grad_feat = jnp.dot(cot_flat, uniting_weight[0].T, preferred_element_type=jnp.float32)
-    seg_cot = jnp.sum(cot_blocks.reshape(seg_shape).astype(jnp.float32), axis=2)
+    seg_cot = jnp.sum(cot_blocks.reshape(seg_shape).astype(jnp.float32), axis=1)
     key_term = jnp.dot(
         seg_cot.reshape(-1, chans),
         uniting_weight[1].T.astype(jnp.float32),
         precision=lax.Precision.HIGHEST,
-    ).reshape(block, seg_count, 1, chans)
-    placed = onehot.astype(jnp.float32)[None, :, :, None] * key_term
+    ).reshape(seg_count, 1, width, chans)
+    placed = onehot.astype(jnp.float32)[:, :, None, None] * key_term
     grad_feat = grad_feat.reshape(seg_shape) + placed
-    grad_feat = grad_feat.reshape(block, total_frames, chans)
+    grad_feat = grad_feat.reshape(total_frames, width, chans)
     grad_uniting = jnp.stack([inner(feat_flat, cot_flat), inner(key_full, cot_flat)])
     grad_pre = (grad_feat * silu_grad(pres[-1])).astype(jnp.bfloat16)
     tgrads = [None] * LAYERS
@@ -362,7 +382,7 @@
             acts[layer], grad_pre, temporal_weight[layer], dilation[layer], below
         )
     grad_act0 = grad_pre
-    grad_time = to_frames(grad_act0).reshape(frames_in.shape)
+    grad_time = fm_to_frames(grad_act0, used).reshape(frames_in.shape)
     grad_spre = (grad_time.astype(jnp.float32) * silu_grad(pre_spatial)).astype(jnp.bfloat16)
     grad_frames = spatial_back(grad_spre, spatial_weight).astype(jnp.bfloat16)
     grad_spatial = spatial_wgrad(frames_in, grad_spre)

time: 195 us -> 186 us (0.954)
  starting transfers between devices: 44.5 us -> 37.5 us
  waiting for transfers between devices: 59.2 us -> 65.5 us
  local copies, waits for them, and re-layouts: 32.7 us -> 27.2 us
  Pallas kernels: 24.9 us -> 22.4 us
    all_to_all x4, waiting for transfers between devices: 32.2 us -> 39.5 us  [the longest x2 22.7 us: fm_to_pixels(): lax.all_to_all(strided, ('seg', 'grp'), split_axis=1, concat_axis=1, tile...]
    all_to_all x4, starting transfers between devices: 35.7 us -> 28.7 us  [the longest x2 15.9 us: fm_to_pixels(): lax.all_to_all(strided, ('seg', 'grp'), split_axis=1, concat_axis=1, tile...]
    reshape x2 -> x0, local copies, waits for them, and re-layouts: 4.87 us -> none  [the longest x1 3.25 us: to_pixels(): strided = flat.reshape(-1, count, chans)]
    pallas_call x1 -> x0, local copies, waits for them, and re-layouts: 2.82 us -> none  [temporal_backward_k(): pl.pallas_call(functools.partial(tbwd_kernel, with_pre), grid_spec=pltpu....]
    all_to_all x1 -> x0, local copies, waits for them, and re-layouts: 2.55 us -> none  [to_frames(): lax.all_to_all(blocks, ('seg', 'grp'), split_axis=1, concat_axis=1, tiled...]
    slice x0 -> x1, local copies, waits for them, and re-layouts: none -> 2.55 us  [fm_to_frames(): return out[:used].reshape(1, -1, blocks.shape[-1])]
    optimization_barrier x1 -> x0, local copies, waits for them, and re-layouts: 2.55 us -> none  [local(): act_blocks, cot_local = lax.optimization_barrier((act_blocks, cot_local))]
    unnamed x36 -> x33, local copies, waits for them, and re-layouts: 3.4 us -> 5.93 us
  transfers between devices with their start and end apart: 6 -> 6, of which waited for: 5 -> 6; matrix products, arithmetic and copies ran while one was open for 17% -> 14% of each run, Pallas kernels for 13% -> 12%
where the time goes in v6:
time: 186 us; the launch traced here: 185 us
  waiting for transfers between devices  65.5 us (35%)
  starting transfers between devices  37.5 us (20%)
  local copies, waits for them, and re-layouts  27.2 us (15%)
  Pallas kernels  22.4 us (12%)
  matrix products  20.3 us (11%)
  other arithmetic  11 us (6%)
    all_to_all x2, waiting for transfers between devices, fm_to_pixels(): lax.all_to_all(strided, ('seg', 'grp'), split_axis=1, concat_axis=1, tile...  22.7 us
    all_to_all x2, waiting for transfers between devices, fm_to_frames(): lax.all_to_all(moved, ('seg', 'grp'), split_axis=1, concat_axis=1, tiled=...  16.8 us
    all_to_all x2, starting transfers between devices, fm_to_pixels(): lax.all_to_all(strided, ('seg', 'grp'), split_axis=1, concat_axis=1, tile...  15.9 us
    all_to_all x1, waiting for transfers between devices, all_sum(): lax.all_to_all(stack, ('seg', 'grp'), split_axis=0, concat_axis=0, tiled=...  14.7 us
    all_to_all x2, starting transfers between devices, fm_to_frames(): lax.all_to_all(moved, ('seg', 'grp'), split_axis=1, concat_axis=1, tiled=...  12.8 us
    pallas_call x2, Pallas kernels, temporal_backward_k(): pl.pallas_call(functools.partial(tbwd_kernel, with_pre), grid_spec=pltpu....  12 us
    all_to_all x1, waiting for transfers between devices, all_sum(): lax.all_to_all(spread, ('seg', 'grp'), split_axis=0, concat_axis=0, tiled...  11.2 us
    pallas_call x2, Pallas kernels, temporal_forward_k(): pl.pallas_call(tfwd_kernel, grid_spec=pltpu.PrefetchScalarGridSpec(num_sc...  10.4 us
  transfers between devices with their start and end apart: 6, of which 6 were waited for; matrix products, arithmetic and copies ran while one was open for 14% of the time, Pallas kernels for 12%

profile of v6, /device:TPU:1, one launch (start us, length us, event | category | flops | bytes accessed | tf_op | source)
XLA Modules:
  0.0 184.9 jit_solution(1025037681045300011)
XLA Ops:
  0.6 6.9 %pad_slice_fusion.8 = (bf16[1,32,120,128]{3,2,1,0:T(8,128)(2,1)S(1)}, bf16[1,32,120,128]{3,2,1,0:T(8,128)(2,1)S(1)}, bf16[1,32,120,128]{3,2,1,0:T(8,128)(2,1)S(1...) fusion(bf16[1,32,120,128]{3,2,1,0:T(8,128)(2,1)} %param.7), kind=kLoop, calls=%fused_computation.71 | loop fusion | bytes 8847360 | tf_op jit(solution)/shard_map/slice | solution.py:36
  14.4 11.5 %all-to-all-start = ((bf16[32,128,128]{2,0,1:T(8,128)(2,1)}), bf16[32,128,128]{2,0,1:T(8,128)(2,1)S(1)}, u32[]{:S(2)}, u32[]{:S(2)}) async-start(bf16[32,128,128]{2,0,1:T(8,128)(2,1)} %pad.16), calls=%async_computation | async-start | bytes 2097152 | tf_op jit(solution)/shard_map/all_to_all | solution.py:166
  26.7 18.2 %all-to-all-done = bf16[32,128,128]{2,0,1:T(8,128)(2,1)S(1)} async-done(((bf16[32,128,128]{2,0,1:T(8,128)(2,1)}), bf16[32,128,128]{2,0,1:T(8,128)(2,1)S(1)}, u32[]{:S(2)}, u32[]{:S(2)}) %all-to-all-start) | async-done | bytes 1048608 | tf_op jit(solution)/shard_map/all_to_all | solution.py:166
  44.9 2.2 %copy.56 = bf16[30,128,128]{2,0,1:T(8,128)(2,1)S(1)} copy(bf16[30,128,128]{2,1,0:T(8,128)(2,1)} %bitcast.282) | data formatting | bytes 1966080
  48.3 4.4 %all-to-all-start.2 = ((bf16[32,128,128]{2,0,1:T(8,128)(2,1)}), bf16[32,128,128]{2,0,1:T(8,128)(2,1)S(1)}, u32[]{:S(2)}, u32[]{:S(2)}) async-start(bf16[32,128,128]{2,0,1:T(8,128)(2,1)} %pad.17.clone), calls=%async_computation.2 | async-start | bytes 2097152 | tf_op jit(solution)/shard_map/all_to_all | solution.py:166
  53.3 5.2 %shard_map.110 = (f32[128,32,128]{2,1,0:T(8,128)}, bf16[128,32,128]{2,1,0:T(8,128)(2,1)}) custom-call(s32[1]{0:T(128)} %get-tuple-element.45.dil_ref, bf16[128,32,128]{2,1,0:T(8,128)(2,1)} %bitcast.279, bf16[640,128]{1,0:T(8,128)(2,1)} %bitcast.292), custom_call_target="tpu_custom_call" | custom-call | flops 671088640 | bytes 4194304 | tf_op jit(solution)/shard_map/pallas_call | solution.py:207
  58.5 5.2 %shard_map.111 = (f32[128,32,128]{2,1,0:T(8,128)}, bf16[128,32,128]{2,1,0:T(8,128)(2,1)}) custom-call(s32[1]{0:T(128)} %get-tuple-element.46.dil_ref, bf16[128,32,128]{2,1,0:T(8,128)(2,1)} %get-tuple-element.16.act_ref, bf16[640,128]{1,0:T(8,128)(2,1)} %bitcast.294), custom_call_target="tpu_custom_call" | custom-call | flops 671088640 | bytes 4194304 | tf_op jit(solution)/shard_map/pallas_call | solution.py:207
  63.7 1.7 fusion.13
  67.1 4.5 %all-to-all-done.2 = bf16[32,128,128]{2,0,1:T(8,128)(2,1)S(1)} async-done(((bf16[32,128,128]{2,0,1:T(8,128)(2,1)}), bf16[32,128,128]{2,0,1:T(8,128)(2,1)S(1)}, u32[]{:S(2)}, u32[]{:S(2)}) %all-to-all-start.2) | async-done | bytes 1048608 | tf_op jit(solution)/shard_map/all_to_all | solution.py:166
  71.6 5.7 %all-to-all-start.1 = ((bf16[32,128,128]{2,0,1:T(8,128)(2,1)}), bf16[32,128,128]{2,0,1:T(8,128)(2,1)}, u32[]{:S(2)}, u32[]{:S(2)}) async-start(bf16[32,128,128]{2,0,1:T(8,128)(2,1)} %bitcast.249), calls=%async_computation.1 | async-start | bytes 2097152 | tf_op jit(solution)/shard_map/all_to_all | solution.py:172
  79.1 1.7 fusion.1.grad_ref
  80.8 6.4 %shard_map.112 = (bf16[128,32,128]{2,1,0:T(8,128)(2,1)}, f32[5,128,128]{2,1,0:T(8,128)}) custom-call(s32[1]{0:T(128)} %get-tuple-element.46.dil_ref, bf16[128,32,128]{2,1,0:T(8,128)(2,1)} %get-tuple-element.16.act_ref, bf16[128,32,128]{2,1,0:T(8,128)(2,1)} %fusion.1.grad_ref, bf16[640,128]{1,0:T(8,128)(2,1)} %bitcast.295, ...), custom_call_target="tpu_custom_call" | custom-call | flops 1342177280 | bytes 5242880 | tf_op jit(solution)/shard_map/pallas_call | solution.py:283
  87.2 5.6 %shard_map.113 = (bf16[128,32,128]{2,1,0:T(8,128)(2,1)}, f32[5,128,128]{2,1,0:T(8,128)}) custom-call(s32[1]{0:T(128)} %get-tuple-element.45.dil_ref, bf16[128,32,128]{2,1,0:T(8,128)(2,1)} %bitcast.280, bf16[128,32,128]{2,1,0:T(8,128)(2,1)} %get-tuple-element.21.grad_ref, bf16[640,128]{1,0:T(8,128)(2,1)} %bitcast.293), custom_call_target="tpu_custom_call" | custom-call | flops 1342177280 | bytes 5242880 | tf_op jit(solution)/shard_map/pallas_call | solution.py:283
  92.8 3.1 %all-to-all-done.1 = bf16[32,128,128]{2,0,1:T(8,128)(2,1)} async-done(((bf16[32,128,128]{2,0,1:T(8,128)(2,1)}), bf16[32,128,128]{2,0,1:T(8,128)(2,1)}, u32[]{:S(2)}, u32[]{:S(2)}) %all-to-all-start.1) | async-done | bytes 1048608 | tf_op jit(solution)/shard_map/all_to_all | solution.py:172
  96.0 7.1 %all-to-all-start.3 = ((bf16[32,128,128]{2,0,1:T(8,128)(2,1)}), bf16[32,128,128]{2,0,1:T(8,128)(2,1)}, u32[]{:S(2)}, u32[]{:S(2)}) async-start(bf16[32,128,128]{2,0,1:T(8,128)(2,1)} %bitcast.281), calls=%async_computation.3 | async-start | bytes 2097152 | tf_op jit(solution)/shard_map/all_to_all | solution.py:172
  103.1 2.6 %copy.44 = bf16[30,128,128]{2,1,0:T(8,128)(2,1)} copy(bf16[30,128,128]{2,0,1:T(8,128)(2,1)} %bitcast.238) | data formatting | bytes 1966080 | tf_op jit(solution)/shard_map/slice | solution.py:173
  108.0 13.7 %all-to-all-done.3 = bf16[32,128,128]{2,0,1:T(8,128)(2,1)} async-done(((bf16[32,128,128]{2,0,1:T(8,128)(2,1)}), bf16[32,128,128]{2,0,1:T(8,128)(2,1)}, u32[]{:S(2)}, u32[]{:S(2)}) %all-to-all-start.3) | async-done | bytes 1048608 | tf_op jit(solution)/shard_map/all_to_all | solution.py:172
  121.7 2.8 %multiply_convert_fusion = bf16[30,128,128]{2,0,1:T(8,128)(2,1)S(1)} fusion(f32[30,128,128]{2,1,0:T(8,128)S(1)} %bitcast.240, bf16[32,128,128]{2,0,1:T(8,128)(2,1)} %all-to-all-done.3), kind=kLoop, calls=%fused_computation.19 | loop fusion | flops 4915200 | bytes 3932160 | tf_op jit(solution)/shard_map/convert_element_type | solution.py:386
  131.5 4.4 %all-to-all-start.4 = ((f32[128,24,128]{2,1,0:T(8,128)}), f32[128,24,128]{2,1,0:T(8,128)S(1)}, u32[]{:S(2)}, u32[]{:S(2)}) async-start(f32[128,24,128]{2,1,0:T(8,128)} %bitcast.246), calls=%async_computation.4 | async-start | bytes 3145728 | tf_op jit(solution)/shard_map/all_to_all | solution.py:313
  139.3 3.2 %pad_slice_fusion = (bf16[1,32,120,128]{3,2,1,0:T(8,128)(2,1)}, bf16[1,32,120,128]{3,2,1,0:T(8,128)(2,1)S(1)}, bf16[1,32,120,128]{3,2,1,0:T(8,128)(2,1)S(1)}, bf...) fusion(bf16[1,32,120,128]{3,2,1,0:T(8,128)(2,1)S(1)} %multiply_, ...), kind=kLoop, calls=%fused_computation.63 | loop fusion | bytes 8847360 | tf_op jit(solution)/shard_map/slice | solution.py:51
  145.8 14.7 %all-to-all-done.4 = f32[128,24,128]{2,1,0:T(8,128)S(1)} async-done(((f32[128,24,128]{2,1,0:T(8,128)}), f32[128,24,128]{2,1,0:T(8,128)S(1)}, u32[]{:S(2)}, u32[]{:S(2)}) %all-to-all-start.4) | async-done | bytes 1572896 | tf_op jit(solution)/shard_map/all_to_all | solution.py:313
  161.7 4.4 %all-to-all-start.5 = ((bf16[128,24,128]{2,1,0:T(8,128)(2,1)}), bf16[128,24,128]{2,1,0:T(8,128)(2,1)S(1)}, u32[]{:S(2)}, u32[]{:S(2)}) async-start(bf16[128,24,128]{2,1,0:T(8,128)(2,1)} %broadcast_in_dim.8), calls=%async_computation.5 | async-start | bytes 1572864 | tf_op jit(solution)/shard_map/all_to_all | solution.py:316
  169.1 2.1 %fusion = bf16[3840,128]{1,0:T(8,128)(2,1)} fusion(f32[3840,128]{1,0:T(8,128)S(1)} %convolution_add_fusion.1, bf16[3840,128]{1,0:T(8,128)(2,1)S(1)} %bitcast.275, bf16[9,128,128]{2,1,0:T(8,128)(2,1)} %param.8), kind=kOutput, calls=%fused_computation.16 | convolution fusion | flops 126812160 | bytes 3964928 | tf_op jit(solution)/shard_map/dot_general | solution.py:54
  171.2 11.2 %all-to-all-done.5 = bf16[128,24,128]{2,1,0:T(8,128)(2,1)S(1)} async-done(((bf16[128,24,128]{2,1,0:T(8,128)(2,1)}), bf16[128,24,128]{2,1,0:T(8,128)(2,1)S(1)}, u32[]{:S(2)}, u32[]{:S(2)}) %all-to-all-start.5) | async-done | bytes 786464 | tf_op jit(solution)/shard_map/all_to_all | solution.py:316
  (90 shorter events, 35.3 us)
Async XLA Ops:
  0.6 6.9 %copy-start.7 = (bf16[9,128,128]{2,1,0:T(8,128)(2,1)S(1)}, bf16[9,128,128]{2,1,0:T(8,128)(2,1)}, u32[]{:S(2)}) copy-start(bf16[9,128,128]{2,1,0:T(8,128)(2,1)} %param.8) | copy-start | bytes 884740
  8.7 1.2 copy-start
  13.3 12.6 %copy-start.12 = (bf16[2,5,128,128]{3,2,1,0:T(8,128)(2,1)S(1)}, bf16[2,5,128,128]{3,2,1,0:T(8,128)(2,1)}, u32[]{:S(2)}) copy-start(bf16[2,5,128,128]{3,2,1,0:T(8,128)(2,1)} %param.9) | copy-start | bytes 983044
  14.4 30.5 %all-to-all-start = ((bf16[32,128,128]{2,0,1:T(8,128)(2,1)}), bf16[32,128,128]{2,0,1:T(8,128)(2,1)S(1)}, u32[]{:S(2)}, u32[]{:S(2)}) async-start(bf16[32,128,128]{2,0,1:T(8,128)(2,1)} %pad.16), calls=%async_computation | async-start | bytes 2097152 | tf_op jit(solution)/shard_map/all_to_all | solution.py:166
  44.9 3.4 %copy-start.9 = (bf16[32,128,128]{2,0,1:T(8,128)(2,1)}, bf16[32,128,128]{2,0,1:T(8,128)(2,1)S(1)}, u32[]{:S(2)}) copy-start(bf16[32,128,128]{2,0,1:T(8,128)(2,1)S(1)} %all-to-all-done) | copy-start | bytes 3145732
  47.1 5.5 %copy-start.15 = (s32[8]{0:T(128)S(1)}, s32[8]{0:T(128)}, u32[]{:S(2)}) copy-start(s32[8]{0:T(128)} %param.11) | copy-start | bytes 100
  47.1 5.6 %copy-start.14 = (s32[2]{0:T(128)S(1)}, s32[2]{0:T(128)}, u32[]{:S(2)}) copy-start(s32[2]{0:T(128)} %param.12) | copy-start | bytes 28
  48.3 23.4 %all-to-all-start.2 = ((bf16[32,128,128]{2,0,1:T(8,128)(2,1)}), bf16[32,128,128]{2,0,1:T(8,128)(2,1)S(1)}, u32[]{:S(2)}, u32[]{:S(2)}) async-start(bf16[32,128,128]{2,0,1:T(8,128)(2,1)} %pad.17.clone), calls=%async_computation.2 | async-start | bytes 2097152 | tf_op jit(solution)/shard_map/all_to_all | solution.py:166
  58.5 6.9 %copy-start.13 = (bf16[2,128,128]{2,1,0:T(8,128)(2,1)S(1)}, bf16[2,128,128]{2,1,0:T(8,128)(2,1)}, u32[]{:S(2)}) copy-start(bf16[2,128,128]{2,1,0:T(8,128)(2,1)} %param.10) | copy-start | bytes 196612
  63.7 1.9 %copy-start.2 = (bf16[128,32,128]{2,1,0:T(8,128)(2,1)S(1)}, bf16[128,32,128]{2,1,0:T(8,128)(2,1)}, u32[]{:S(2)}) copy-start(bf16[128,32,128]{2,1,0:T(8,128)(2,1)} %get-tuple-element.17) | copy-start | bytes 3145732
  71.6 24.3 %all-to-all-start.1 = ((bf16[32,128,128]{2,0,1:T(8,128)(2,1)}), bf16[32,128,128]{2,0,1:T(8,128)(2,1)}, u32[]{:S(2)}, u32[]{:S(2)}) async-start(bf16[32,128,128]{2,0,1:T(8,128)(2,1)} %bitcast.249), calls=%async_computation.1 | async-start | bytes 2097152 | tf_op jit(solution)/shard_map/all_to_all | solution.py:172
  77.5 1.6 copy-start.6
  96.0 25.7 %all-to-all-start.3 = ((bf16[32,128,128]{2,0,1:T(8,128)(2,1)}), bf16[32,128,128]{2,0,1:T(8,128)(2,1)}, u32[]{:S(2)}, u32[]{:S(2)}) async-start(bf16[32,128,128]{2,0,1:T(8,128)(2,1)} %bitcast.281), calls=%async_computation.3 | async-start | bytes 2097152 | tf_op jit(solution)/shard_map/all_to_all | solution.py:172
  105.6 1.2 copy-start.3
  106.9 1.0 copy-start.10
  106.9 1.1 copy-start.11
  124.4 1.2 copy-start.1
  131.5 29.0 %all-to-all-start.4 = ((f32[128,24,128]{2,1,0:T(8,128)}), f32[128,24,128]{2,1,0:T(8,128)S(1)}, u32[]{:S(2)}, u32[]{:S(2)}) async-start(f32[128,24,128]{2,1,0:T(8,128)} %bitcast.246), calls=%async_computation.4 | async-start | bytes 3145728 | tf_op jit(solution)/shard_map/all_to_all | solution.py:313
  139.3 3.2 %copy-start.8 = (bf16[9,128,128]{2,1,0:T(8,128)(2,1)S(1)}, bf16[9,128,128]{2,1,0:T(8,128)(2,1)}, u32[]{:S(2)}) copy-start(bf16[9,128,128]{2,1,0:T(8,128)(2,1)} %param.8) | copy-start | bytes 884740
  161.7 20.7 %all-to-all-start.5 = ((bf16[128,24,128]{2,1,0:T(8,128)(2,1)}), bf16[128,24,128]{2,1,0:T(8,128)(2,1)S(1)}, u32[]{:S(2)}, u32[]{:S(2)}) async-start(bf16[128,24,128]{2,1,0:T(8,128)(2,1)} %broadcast_in_dim.8), calls=%async_computation.5 | async-start | bytes 1572864 | tf_op jit(solution)/shard_map/all_to_all | solution.py:316
  166.1 1.7 copy-start.4
  167.8 1.3 copy-start.5

commit v7 on v6

--- a/solution.py
+++ b/solution.py
@@ -190,16 +190,20 @@
     fill_halo(act_ref, pad_ref)
     step = dil_ref[0]
     rows = FB * width
-    for block in range(frames // FB):
-        base = HALO + block * FB
+
+    def body(block, carry):
+        first = pl.multiple_of(block * FB, FB)
         stacked = jnp.concatenate(
-            [tap_rows(pad_ref, base + (tap - 2) * step, rows) for tap in range(5)], axis=1
+            [tap_rows(pad_ref, HALO + first + (tap - 2) * step, rows) for tap in range(5)], axis=1
         )
         pre = jnp.dot(stacked, w_ref[...], preferred_element_type=jnp.float32)
-        pre_ref[block * FB : (block + 1) * FB] = pre.reshape(FB, width, chans)
-        out_ref[block * FB : (block + 1) * FB] = (
+        pre_ref[pl.ds(first, FB)] = pre.reshape(FB, width, chans)
+        out_ref[pl.ds(first, FB)] = (
             (pre / (1.0 + jnp.exp(-pre))).astype(jnp.bfloat16).reshape(FB, width, chans)
         )
+        return carry
+
+    lax.fori_loop(0, frames // FB, body, 0)
 
 
 def temporal_forward_k(acts, kernel, step_size):
@@ -240,11 +244,12 @@
     fill_halo(grad_ref, pad_ref)
     step = dil_ref[0]
     rows = FB * width
-    total = None
-    for block in range(frames // FB):
-        base = HALO + block * FB
+    tg_ref[...] = jnp.zeros_like(tg_ref)
+
+    def body(block, carry):
+        first = pl.multiple_of(block * FB, FB)
         stacked = jnp.concatenate(
-            [tap_rows(pad_ref, base - (tap - 2) * step, rows) for tap in range(5)], axis=1
+            [tap_rows(pad_ref, HALO + first - (tap - 2) * step, rows) for tap in range(5)], axis=1
         )
         grad_act = None
         for tap in range(5):
@@ -255,20 +260,20 @@
                 preferred_element_type=jnp.float32,
             )
             grad_act = term if grad_act is None else grad_act + term
-        flat_act = act_ref[block * FB : (block + 1) * FB].reshape(rows, chans)
+        flat_act = act_ref[pl.ds(first, FB)].reshape(rows, chans)
         part = lax.dot_general(
             flat_act, stacked, (((0,), (0,)), ((), ())), preferred_element_type=jnp.float32
         )
-        total = part if total is None else total + part
+        for tap in range(5):
+            tg_ref[tap] += part[:, tap * chans : (tap + 1) * chans]
         if with_pre:
-            pre = pre_ref[block * FB : (block + 1) * FB].reshape(rows, chans)
+            pre = pre_ref[pl.ds(first, FB)].reshape(rows, chans)
             sigma = 1.0 / (1.0 + jnp.exp(-pre))
             grad_act = grad_act * (sigma * (1.0 + pre * (1.0 - sigma)))
-        out_ref[block * FB : (block + 1) * FB] = (
-            grad_act.astype(jnp.bfloat16).reshape(FB, width, chans)
-        )
-    for tap in range(5):
-        tg_ref[tap] = total[:, tap * chans : (tap + 1) * chans]
+        out_ref[pl.ds(first, FB)] = grad_act.astype(jnp.bfloat16).reshape(FB, width, chans)
+        return carry
+
+    lax.fori_loop(0, frames // FB, body, 0)
 
 
 def temporal_backward_k(acts, grads, kernel, step_size, pre_below):

time: 186 us -> 191 us (1.027)
  waiting for transfers between devices: 65.5 us -> 60.1 us
  Pallas kernels: 22.4 us -> 27.7 us
  starting transfers between devices: 37.5 us -> 42.8 us
    all_to_all x2, starting transfers between devices: 12.8 us -> 18.1 us  [fm_to_frames(): lax.all_to_all(moved, ('seg', 'grp'), split_axis=1, concat_axis=1, tiled=...]
    all_to_all x2, waiting for transfers between devices: 22.7 us -> 20 us  [fm_to_pixels(): lax.all_to_all(strided, ('seg', 'grp'), split_axis=1, concat_axis=1, tile...]
    pallas_call x2, Pallas kernels: 10.4 us -> 13.1 us  [temporal_forward_k(): pl.pallas_call(tfwd_kernel, grid_spec=pltpu.PrefetchScalarGridSpec(num_sc...]
    pallas_call x2, Pallas kernels: 12 us -> 14.6 us  [temporal_backward_k(): pl.pallas_call(functools.partial(tbwd_kernel, with_pre), grid_spec=pltpu....]
    all_to_all x2, waiting for transfers between devices: 16.8 us -> 14.2 us  [fm_to_frames(): lax.all_to_all(moved, ('seg', 'grp'), split_axis=1, concat_axis=1, tiled=...]
  transfers between devices with their start and end apart: 6 -> 6, of which waited for: 6 -> 6; matrix products, arithmetic and copies ran while one was open for 14% -> 14% of each run, Pallas kernels for 12% -> 15%
where the time goes in v7:
time: 191 us; the launch traced here: 190 us
  waiting for transfers between devices  60.1 us (31%)
  starting transfers between devices  42.8 us (22%)
  Pallas kernels  27.7 us (15%)
  local copies, waits for them, and re-layouts  27.2 us (14%)
  matrix products  20.3 us (11%)
  other arithmetic  11 us (6%)
    all_to_all x2, waiting for transfers between devices, fm_to_pixels(): lax.all_to_all(strided, ('seg', 'grp'), split_axis=1, concat_axis=1, tile...  20 us
    all_to_all x2, starting transfers between devices, fm_to_frames(): lax.all_to_all(moved, ('seg', 'grp'), split_axis=1, concat_axis=1, tiled=...  18.1 us
    all_to_all x2, starting transfers between devices, fm_to_pixels(): lax.all_to_all(strided, ('seg', 'grp'), split_axis=1, concat_axis=1, tile...  15.9 us
    all_to_all x1, waiting for transfers between devices, all_sum(): lax.all_to_all(stack, ('seg', 'grp'), split_axis=0, concat_axis=0, tiled=...  14.7 us
    pallas_call x2, Pallas kernels, temporal_backward_k(): pl.pallas_call(functools.partial(tbwd_kernel, with_pre), grid_spec=pltpu....  14.6 us
    all_to_all x2, waiting for transfers between devices, fm_to_frames(): lax.all_to_all(moved, ('seg', 'grp'), split_axis=1, concat_axis=1, tiled=...  14.2 us
    pallas_call x2, Pallas kernels, temporal_forward_k(): pl.pallas_call(tfwd_kernel, grid_spec=pltpu.PrefetchScalarGridSpec(num_sc...  13.1 us
    all_to_all x1, waiting for transfers between devices, all_sum(): lax.all_to_all(spread, ('seg', 'grp'), split_axis=0, concat_axis=0, tiled...  11.2 us
  transfers between devices with their start and end apart: 6, of which 6 were waited for; matrix products, arithmetic and copies ran while one was open for 14% of the time, Pallas kernels for 15%

profile of v7, /device:TPU:1, one launch (start us, length us, event | category | flops | bytes accessed | tf_op | source)
XLA Modules:
  0.0 190.2 jit_solution(10566282952538718768)
XLA Ops:
  0.6 6.9 %pad_slice_fusion.8 = (bf16[1,32,120,128]{3,2,1,0:T(8,128)(2,1)S(1)}, bf16[1,32,120,128]{3,2,1,0:T(8,128)(2,1)S(1)}, bf16[1,32,120,128]{3,2,1,0:T(8,128)(2,1)S(1...) fusion(bf16[1,32,120,128]{3,2,1,0:T(8,128)(2,1)} %param.7), kind=kLoop, calls=%fused_computation.71 | loop fusion | bytes 8847360 | tf_op jit(solution)/shard_map/slice | solution.py:36
  14.4 11.5 %all-to-all-start = ((bf16[32,128,128]{2,0,1:T(8,128)(2,1)}), bf16[32,128,128]{2,0,1:T(8,128)(2,1)S(1)}, u32[]{:S(2)}, u32[]{:S(2)}) async-start(bf16[32,128,128]{2,0,1:T(8,128)(2,1)} %pad.16), calls=%async_computation | async-start | bytes 2097152 | tf_op jit(solution)/shard_map/all_to_all | solution.py:166
  26.7 18.2 %all-to-all-done = bf16[32,128,128]{2,0,1:T(8,128)(2,1)S(1)} async-done(((bf16[32,128,128]{2,0,1:T(8,128)(2,1)}), bf16[32,128,128]{2,0,1:T(8,128)(2,1)S(1)}, u32[]{:S(2)}, u32[]{:S(2)}) %all-to-all-start) | async-done | bytes 1048608 | tf_op jit(solution)/shard_map/all_to_all | solution.py:166
  44.9 2.2 %copy.56 = bf16[30,128,128]{2,0,1:T(8,128)(2,1)S(1)} copy(bf16[30,128,128]{2,1,0:T(8,128)(2,1)} %bitcast.282) | data formatting | bytes 1966080
  48.3 4.4 %all-to-all-start.2 = ((bf16[32,128,128]{2,0,1:T(8,128)(2,1)}), bf16[32,128,128]{2,0,1:T(8,128)(2,1)S(1)}, u32[]{:S(2)}, u32[]{:S(2)}) async-start(bf16[32,128,128]{2,0,1:T(8,128)(2,1)} %pad.17.clone), calls=%async_computation.2 | async-start | bytes 2097152 | tf_op jit(solution)/shard_map/all_to_all | solution.py:166
  53.3 6.6 %shard_map.110 = (f32[128,32,128]{2,1,0:T(8,128)}, bf16[128,32,128]{2,1,0:T(8,128)(2,1)}) custom-call(s32[1]{0:T(128)} %get-tuple-element.45.dil_ref, bf16[128,32,128]{2,1,0:T(8,128)(2,1)} %bitcast.279, bf16[640,128]{1,0:T(8,128)(2,1)} %bitcast.292), custom_call_target="tpu_custom_call" | custom-call | flops 671088640 | bytes 4194304 | tf_op jit(solution)/shard_map/pallas_call | solution.py:211
  59.9 6.5 %shard_map.111 = (f32[128,32,128]{2,1,0:T(8,128)}, bf16[128,32,128]{2,1,0:T(8,128)(2,1)}) custom-call(s32[1]{0:T(128)} %get-tuple-element.46.dil_ref, bf16[128,32,128]{2,1,0:T(8,128)(2,1)} %get-tuple-element.16.act_ref, bf16[640,128]{1,0:T(8,128)(2,1)} %bitcast.294), custom_call_target="tpu_custom_call" | custom-call | flops 671088640 | bytes 4194304 | tf_op jit(solution)/shard_map/pallas_call | solution.py:211
  66.4 1.7 fusion.13
  69.8 1.8 all-to-all-done.2
  71.6 8.4 %all-to-all-start.1 = ((bf16[32,128,128]{2,0,1:T(8,128)(2,1)}), bf16[32,128,128]{2,0,1:T(8,128)(2,1)}, u32[]{:S(2)}, u32[]{:S(2)}) async-start(bf16[32,128,128]{2,0,1:T(8,128)(2,1)} %bitcast.249), calls=%async_computation.1 | async-start | bytes 2097152 | tf_op jit(solution)/shard_map/all_to_all | solution.py:172
  81.8 1.7 fusion.1.grad_ref
  83.5 7.7 %shard_map.112 = (bf16[128,32,128]{2,1,0:T(8,128)(2,1)}, f32[5,128,128]{2,1,0:T(8,128)}) custom-call(s32[1]{0:T(128)} %get-tuple-element.46.dil_ref, bf16[128,32,128]{2,1,0:T(8,128)(2,1)} %get-tuple-element.16.act_ref, bf16[128,32,128]{2,1,0:T(8,128)(2,1)} %fusion.1.grad_ref, bf16[640,128]{1,0:T(8,128)(2,1)} %bitcast.295, ...), custom_call_target="tpu_custom_call" | custom-call | flops 1342177280 | bytes 5242880 | tf_op jit(solution)/shard_map/pallas_call | solution.py:288
  91.2 6.9 %shard_map.113 = (bf16[128,32,128]{2,1,0:T(8,128)(2,1)}, f32[5,128,128]{2,1,0:T(8,128)}) custom-call(s32[1]{0:T(128)} %get-tuple-element.45.dil_ref, bf16[128,32,128]{2,1,0:T(8,128)(2,1)} %bitcast.280, bf16[128,32,128]{2,1,0:T(8,128)(2,1)} %get-tuple-element.21.grad_ref, bf16[640,128]{1,0:T(8,128)(2,1)} %bitcast.293), custom_call_target="tpu_custom_call" | custom-call | flops 1342177280 | bytes 5242880 | tf_op jit(solution)/shard_map/pallas_call | solution.py:288
  98.6 9.7 %all-to-all-start.3 = ((bf16[32,128,128]{2,0,1:T(8,128)(2,1)}), bf16[32,128,128]{2,0,1:T(8,128)(2,1)}, u32[]{:S(2)}, u32[]{:S(2)}) async-start(bf16[32,128,128]{2,0,1:T(8,128)(2,1)} %bitcast.281), calls=%async_computation.3 | async-start | bytes 2097152 | tf_op jit(solution)/shard_map/all_to_all | solution.py:172
  108.4 2.6 %copy.44 = bf16[30,128,128]{2,1,0:T(8,128)(2,1)} copy(bf16[30,128,128]{2,0,1:T(8,128)(2,1)} %bitcast.238) | data formatting | bytes 1966080 | tf_op jit(solution)/shard_map/slice | solution.py:173
  113.3 13.7 %all-to-all-done.3 = bf16[32,128,128]{2,0,1:T(8,128)(2,1)} async-done(((bf16[32,128,128]{2,0,1:T(8,128)(2,1)}), bf16[32,128,128]{2,0,1:T(8,128)(2,1)}, u32[]{:S(2)}, u32[]{:S(2)}) %all-to-all-start.3) | async-done | bytes 1048608 | tf_op jit(solution)/shard_map/all_to_all | solution.py:172
  127.0 2.8 %multiply_convert_fusion = bf16[30,128,128]{2,0,1:T(8,128)(2,1)S(1)} fusion(f32[30,128,128]{2,1,0:T(8,128)S(1)} %bitcast.240, bf16[32,128,128]{2,0,1:T(8,128)(2,1)} %all-to-all-done.3), kind=kLoop, calls=%fused_computation.19 | loop fusion | flops 4915200 | bytes 3932160 | tf_op jit(solution)/shard_map/convert_element_type | solution.py:391
  136.8 4.4 %all-to-all-start.4 = ((f32[128,24,128]{2,1,0:T(8,128)}), f32[128,24,128]{2,1,0:T(8,128)S(1)}, u32[]{:S(2)}, u32[]{:S(2)}) async-start(f32[128,24,128]{2,1,0:T(8,128)} %bitcast.246), calls=%async_computation.4 | async-start | bytes 3145728 | tf_op jit(solution)/shard_map/all_to_all | solution.py:318
  144.6 3.2 %pad_slice_fusion = (bf16[1,32,120,128]{3,2,1,0:T(8,128)(2,1)}, bf16[1,32,120,128]{3,2,1,0:T(8,128)(2,1)S(1)}, bf16[1,32,120,128]{3,2,1,0:T(8,128)(2,1)S(1)}, bf...) fusion(bf16[1,32,120,128]{3,2,1,0:T(8,128)(2,1)S(1)} %multiply_, ...), kind=kLoop, calls=%fused_computation.63 | loop fusion | bytes 8847360 | tf_op jit(solution)/shard_map/slice | solution.py:51
  151.1 14.7 %all-to-all-done.4 = f32[128,24,128]{2,1,0:T(8,128)S(1)} async-done(((f32[128,24,128]{2,1,0:T(8,128)}), f32[128,24,128]{2,1,0:T(8,128)S(1)}, u32[]{:S(2)}, u32[]{:S(2)}) %all-to-all-start.4) | async-done | bytes 1572896 | tf_op jit(solution)/shard_map/all_to_all | solution.py:318
  167.0 4.4 %all-to-all-start.5 = ((bf16[128,24,128]{2,1,0:T(8,128)(2,1)}), bf16[128,24,128]{2,1,0:T(8,128)(2,1)S(1)}, u32[]{:S(2)}, u32[]{:S(2)}) async-start(bf16[128,24,128]{2,1,0:T(8,128)(2,1)} %broadcast_in_dim.8), calls=%async_computation.5 | async-start | bytes 1572864 | tf_op jit(solution)/shard_map/all_to_all | solution.py:321
  171.4 1.7 convolution_add_fusion.2
  174.4 2.1 %fusion = bf16[3840,128]{1,0:T(8,128)(2,1)} fusion(f32[3840,128]{1,0:T(8,128)S(1)} %convolution_add_fusion.1, bf16[3840,128]{1,0:T(8,128)(2,1)S(1)} %bitcast.275, bf16[9,128,128]{2,1,0:T(8,128)(2,1)} %param.8), kind=kOutput, calls=%fused_computation.16 | convolution fusion | flops 126812160 | bytes 3964928 | tf_op jit(solution)/shard_map/dot_general | solution.py:54
  176.5 11.2 %all-to-all-done.5 = bf16[128,24,128]{2,1,0:T(8,128)(2,1)S(1)} async-done(((bf16[128,24,128]{2,1,0:T(8,128)(2,1)}), bf16[128,24,128]{2,1,0:T(8,128)(2,1)S(1)}, u32[]{:S(2)}, u32[]{:S(2)}) %all-to-all-start.5) | async-done | bytes 786464 | tf_op jit(solution)/shard_map/all_to_all | solution.py:321
  (90 shorter events, 34.1 us)
Async XLA Ops:
  0.6 6.9 %copy-start.7 = (bf16[9,128,128]{2,1,0:T(8,128)(2,1)S(1)}, bf16[9,128,128]{2,1,0:T(8,128)(2,1)}, u32[]{:S(2)}) copy-start(bf16[9,128,128]{2,1,0:T(8,128)(2,1)} %param.8) | copy-start | bytes 884740
  8.7 1.2 copy-start
  13.3 12.6 %copy-start.12 = (bf16[2,5,128,128]{3,2,1,0:T(8,128)(2,1)S(1)}, bf16[2,5,128,128]{3,2,1,0:T(8,128)(2,1)}, u32[]{:S(2)}) copy-start(bf16[2,5,128,128]{3,2,1,0:T(8,128)(2,1)} %param.9) | copy-start | bytes 983044
  14.4 30.5 %all-to-all-start = ((bf16[32,128,128]{2,0,1:T(8,128)(2,1)}), bf16[32,128,128]{2,0,1:T(8,128)(2,1)S(1)}, u32[]{:S(2)}, u32[]{:S(2)}) async-start(bf16[32,128,128]{2,0,1:T(8,128)(2,1)} %pad.16), calls=%async_computation | async-start | bytes 2097152 | tf_op jit(solution)/shard_map/all_to_all | solution.py:166
  44.9 3.4 %copy-start.9 = (bf16[32,128,128]{2,0,1:T(8,128)(2,1)}, bf16[32,128,128]{2,0,1:T(8,128)(2,1)S(1)}, u32[]{:S(2)}) copy-start(bf16[32,128,128]{2,0,1:T(8,128)(2,1)S(1)} %all-to-all-done) | copy-start | bytes 3145732
  47.1 5.5 %copy-start.15 = (s32[8]{0:T(128)S(1)}, s32[8]{0:T(128)}, u32[]{:S(2)}) copy-start(s32[8]{0:T(128)} %param.11) | copy-start | bytes 100
  47.1 5.6 %copy-start.14 = (s32[2]{0:T(128)S(1)}, s32[2]{0:T(128)}, u32[]{:S(2)}) copy-start(s32[2]{0:T(128)} %param.12) | copy-start | bytes 28
  48.3 23.4 %all-to-all-start.2 = ((bf16[32,128,128]{2,0,1:T(8,128)(2,1)}), bf16[32,128,128]{2,0,1:T(8,128)(2,1)S(1)}, u32[]{:S(2)}, u32[]{:S(2)}) async-start(bf16[32,128,128]{2,0,1:T(8,128)(2,1)} %pad.17.clone), calls=%async_computation.2 | async-start | bytes 2097152 | tf_op jit(solution)/shard_map/all_to_all | solution.py:166
  59.9 8.2 %copy-start.13 = (bf16[2,128,128]{2,1,0:T(8,128)(2,1)S(1)}, bf16[2,128,128]{2,1,0:T(8,128)(2,1)}, u32[]{:S(2)}) copy-start(bf16[2,128,128]{2,1,0:T(8,128)(2,1)} %param.10) | copy-start | bytes 196612
  66.4 1.9 copy-start.2
  71.6 27.0 %all-to-all-start.1 = ((bf16[32,128,128]{2,0,1:T(8,128)(2,1)}), bf16[32,128,128]{2,0,1:T(8,128)(2,1)}, u32[]{:S(2)}, u32[]{:S(2)}) async-start(bf16[32,128,128]{2,0,1:T(8,128)(2,1)} %bitcast.249), calls=%async_computation.1 | async-start | bytes 2097152 | tf_op jit(solution)/shard_map/all_to_all | solution.py:172
  80.2 1.6 copy-start.6
  98.6 28.3 %all-to-all-start.3 = ((bf16[32,128,128]{2,0,1:T(8,128)(2,1)}), bf16[32,128,128]{2,0,1:T(8,128)(2,1)}, u32[]{:S(2)}, u32[]{:S(2)}) async-start(bf16[32,128,128]{2,0,1:T(8,128)(2,1)} %bitcast.281), calls=%async_computation.3 | async-start | bytes 2097152 | tf_op jit(solution)/shard_map/all_to_all | solution.py:172
  110.9 1.2 copy-start.3
  112.2 1.0 copy-start.10
  112.2 1.1 copy-start.11
  129.7 1.2 copy-start.1
  136.8 29.0 %all-to-all-start.4 = ((f32[128,24,128]{2,1,0:T(8,128)}), f32[128,24,128]{2,1,0:T(8,128)S(1)}, u32[]{:S(2)}, u32[]{:S(2)}) async-start(f32[128,24,128]{2,1,0:T(8,128)} %bitcast.246), calls=%async_computation.4 | async-start | bytes 3145728 | tf_op jit(solution)/shard_map/all_to_all | solution.py:318
  144.6 3.2 %copy-start.8 = (bf16[9,128,128]{2,1,0:T(8,128)(2,1)S(1)}, bf16[9,128,128]{2,1,0:T(8,128)(2,1)}, u32[]{:S(2)}) copy-start(bf16[9,128,128]{2,1,0:T(8,128)(2,1)} %param.8) | copy-start | bytes 884740
  167.0 20.7 %all-to-all-start.5 = ((bf16[128,24,128]{2,1,0:T(8,128)(2,1)}), bf16[128,24,128]{2,1,0:T(8,128)(2,1)S(1)}, u32[]{:S(2)}, u32[]{:S(2)}) async-start(bf16[128,24,128]{2,1,0:T(8,128)(2,1)} %broadcast_in_dim.8), calls=%async_computation.5 | async-start | bytes 1572864 | tf_op jit(solution)/shard_map/all_to_all | solution.py:321
  171.4 1.7 copy-start.4
  173.1 1.3 copy-start.5

commit v8 on v6

--- a/solution.py
+++ b/solution.py
@@ -233,9 +233,37 @@
 
 def tbwd_kernel(with_pre, dil_ref, act_ref, grad_ref, wt_ref, *rest):
     if with_pre:
-        pre_ref, out_ref, tg_ref, pad_ref = rest
+        pre_ref, out_ref, pad_ref = rest
     else:
-        out_ref, tg_ref, pad_ref = rest
+        out_ref, pad_ref = rest
+    frames, width, chans = act_ref.shape
+    fill_halo(grad_ref, pad_ref)
+    step = dil_ref[0]
+    rows = FB * width
+    for block in range(frames // FB):
+        base = HALO + block * FB
+        stacked = jnp.concatenate(
+            [tap_rows(pad_ref, base - (tap - 2) * step, rows) for tap in range(5)], axis=1
+        )
+        grad_act = None
+        for tap in range(5):
+            term = lax.dot_general(
+                stacked[:, tap * chans : (tap + 1) * chans],
+                wt_ref[tap * chans : (tap + 1) * chans, :],
+                (((1,), (1,)), ((), ())),
+                preferred_element_type=jnp.float32,
+            )
+            grad_act = term if grad_act is None else grad_act + term
+        if with_pre:
+            pre = pre_ref[block * FB : (block + 1) * FB].reshape(rows, chans)
+            sigma = 1.0 / (1.0 + jnp.exp(-pre))
+            grad_act = grad_act * (sigma * (1.0 + pre * (1.0 - sigma)))
+        out_ref[block * FB : (block + 1) * FB] = (
+            grad_act.astype(jnp.bfloat16).reshape(FB, width, chans)
+        )
+
+
+def twgrad_kernel(dil_ref, act_ref, grad_ref, tg_ref, pad_ref):
     frames, width, chans = act_ref.shape
     fill_halo(grad_ref, pad_ref)
     step = dil_ref[0]
@@ -246,29 +274,34 @@
         stacked = jnp.concatenate(
             [tap_rows(pad_ref, base - (tap - 2) * step, rows) for tap in range(5)], axis=1
         )
-        grad_act = None
-        for tap in range(5):
-            term = lax.dot_general(
-                stacked[:, tap * chans : (tap + 1) * chans],
-                wt_ref[tap * chans : (tap + 1) * chans, :],
-                (((1,), (1,)), ((), ())),
-                preferred_element_type=jnp.float32,
-            )
-            grad_act = term if grad_act is None else grad_act + term
         flat_act = act_ref[block * FB : (block + 1) * FB].reshape(rows, chans)
         part = lax.dot_general(
             flat_act, stacked, (((0,), (0,)), ((), ())), preferred_element_type=jnp.float32
         )
         total = part if total is None else total + part
-        if with_pre:
-            pre = pre_ref[block * FB : (block + 1) * FB].reshape(rows, chans)
-            sigma = 1.0 / (1.0 + jnp.exp(-pre))
-            grad_act = grad_act * (sigma * (1.0 + pre * (1.0 - sigma)))
-        out_ref[block * FB : (block + 1) * FB] = (
-            grad_act.astype(jnp.bfloat16).reshape(FB, width, chans)
-        )
     for tap in range(5):
         tg_ref[tap] = total[:, tap * chans : (tap + 1) * chans]
+
+
+def temporal_wgrad_k(acts, grads, step_size):
+    frames, width, chans = acts.shape
+    full = pl.BlockSpec(acts.shape, lambda i, d: (0, 0, 0))
+    return pl.pallas_call(
+        twgrad_kernel,
+        grid_spec=pltpu.PrefetchScalarGridSpec(
+            num_scalar_prefetch=1,
+            grid=(1,),
+            in_specs=[full, full],
+            out_specs=pl.BlockSpec((5, chans, chans), lambda i, d: (0, 0, 0)),
+            scratch_shapes=[pltpu.VMEM((frames + 2 * HALO, width, chans), jnp.bfloat16)],
+        ),
+        out_shape=jax.ShapeDtypeStruct((5, chans, chans), jnp.float32),
+        cost_estimate=pl.CostEstimate(
+            flops=2 * frames * width * chans * chans * 5,
+            transcendentals=0,
+            bytes_accessed=frames * width * chans * 4,
+        ),
+    )(step_size.reshape(1), acts, grads)
 
 
 def temporal_backward_k(acts, grads, kernel, step_size, pre_below):
@@ -280,26 +313,22 @@
     if with_pre:
         in_specs.append(full)
         operands.append(pre_below)
-    out, tg = pl.pallas_call(
+    return pl.pallas_call(
         functools.partial(tbwd_kernel, with_pre),
         grid_spec=pltpu.PrefetchScalarGridSpec(
             num_scalar_prefetch=1,
             grid=(1,),
             in_specs=in_specs,
-            out_specs=[full, pl.BlockSpec((5, chans, chans), lambda i, d: (0, 0, 0))],
+            out_specs=full,
             scratch_shapes=[pltpu.VMEM((frames + 2 * HALO, width, chans), jnp.bfloat16)],
         ),
-        out_shape=[
-            jax.ShapeDtypeStruct(acts.shape, jnp.bfloat16),
-            jax.ShapeDtypeStruct((5, chans, chans), jnp.float32),
-        ],
+        out_shape=jax.ShapeDtypeStruct(acts.shape, jnp.bfloat16),
         cost_estimate=pl.CostEstimate(
-            flops=2 * frames * width * chans * chans * 10,
+            flops=2 * frames * width * chans * chans * 5,
             transcendentals=frames * width * chans,
             bytes_accessed=frames * width * chans * 10,
         ),
     )(*operands)
-    return out, tg
 
 
 def all_sum(parts, scale):
@@ -376,13 +405,17 @@
     grad_uniting = jnp.stack([inner(feat_flat, cot_flat), inner(key_full, cot_flat)])
     grad_pre = (grad_feat * silu_grad(pres[-1])).astype(jnp.bfloat16)
     tgrads = [None] * LAYERS
+    layer_grads = [None] * LAYERS
     for layer in range(LAYERS - 1, -1, -1):
         below = pres[layer - 1] if layer > 0 else None
-        grad_pre, tgrads[layer] = temporal_backward_k(
+        layer_grads[layer] = grad_pre
+        grad_pre = temporal_backward_k(
             acts[layer], grad_pre, temporal_weight[layer], dilation[layer], below
         )
     grad_act0 = grad_pre
     grad_time = fm_to_frames(grad_act0, used).reshape(frames_in.shape)
+    for layer in range(LAYERS):
+        tgrads[layer] = temporal_wgrad_k(acts[layer], layer_grads[layer], dilation[layer])
     grad_spre = (grad_time.astype(jnp.float32) * silu_grad(pre_spatial)).astype(jnp.bfloat16)
     grad_frames = spatial_back(grad_spre, spatial_weight).astype(jnp.bfloat16)
     grad_spatial = spatial_wgrad(frames_in, grad_spre)

time: 186 us -> 185 us (level)
  waiting for transfers between devices: 65.5 us -> 59.1 us
  Pallas kernels: 22.4 us -> 28.7 us
    pallas_call x0 -> x2, Pallas kernels: none -> 8.04 us  [temporal_wgrad_k(): pl.pallas_call(twgrad_kernel, grid_spec=pltpu.PrefetchScalarGridSpec(num_...]
    all_to_all x2, waiting for transfers between devices: 16.8 us -> 10.4 us  [fm_to_frames(): lax.all_to_all(moved, ('seg', 'grp'), split_axis=1, concat_axis=1, tiled=...]
  transfers between devices with their start and end apart: 6 -> 6, of which waited for: 6 -> 6; matrix products, arithmetic and copies ran while one was open for 14% -> 14% of each run, Pallas kernels for 12% -> 16%
where the time goes in v8:
time: 185 us; the launch traced here: 183 us
  waiting for transfers between devices  59.1 us (32%)
  starting transfers between devices  35.8 us (19%)
  Pallas kernels  28.7 us (16%)
  local copies, waits for them, and re-layouts  27.5 us (15%)
  matrix products  20.2 us (11%)
  other arithmetic  11.1 us (6%)
    all_to_all x2, waiting for transfers between devices, fm_to_pixels(): lax.all_to_all(strided, ('seg', 'grp'), split_axis=1, concat_axis=1, tile...  22.8 us
    all_to_all x2, starting transfers between devices, fm_to_pixels(): lax.all_to_all(strided, ('seg', 'grp'), split_axis=1, concat_axis=1, tile...  15.9 us
    all_to_all x1, waiting for transfers between devices, all_sum(): lax.all_to_all(stack, ('seg', 'grp'), split_axis=0, concat_axis=0, tiled=...  14.7 us
    all_to_all x1, waiting for transfers between devices, all_sum(): lax.all_to_all(spread, ('seg', 'grp'), split_axis=0, concat_axis=0, tiled...  11.2 us
    all_to_all x2, starting transfers between devices, fm_to_frames(): lax.all_to_all(moved, ('seg', 'grp'), split_axis=1, concat_axis=1, tiled=...  11.2 us
    all_to_all x2, waiting for transfers between devices, fm_to_frames(): lax.all_to_all(moved, ('seg', 'grp'), split_axis=1, concat_axis=1, tiled=...  10.4 us
    pallas_call x2, Pallas kernels, temporal_forward_k(): pl.pallas_call(tfwd_kernel, grid_spec=pltpu.PrefetchScalarGridSpec(num_sc...  10.3 us
    pallas_call x2, Pallas kernels, temporal_backward_k(): pl.pallas_call(functools.partial(tbwd_kernel, with_pre), grid_spec=pltpu....  10.3 us
  transfers between devices with their start and end apart: 6, of which 6 were waited for; matrix products, arithmetic and copies ran while one was open for 14% of the time, Pallas kernels for 16%

profile of v8, /device:TPU:1, one launch (start us, length us, event | category | flops | bytes accessed | tf_op | source)
XLA Modules:
  0.0 183.5 jit_solution(4190084795677013323)
XLA Ops:
  0.6 7.0 %pad_slice_fusion.8 = (bf16[1,32,120,128]{3,2,1,0:T(8,128)(2,1)S(1)}, bf16[1,32,120,128]{3,2,1,0:T(8,128)(2,1)S(1)}, bf16[1,32,120,128]{3,2,1,0:T(8,128)(2,1)S(1...) fusion(bf16[1,32,120,128]{3,2,1,0:T(8,128)(2,1)} %param.7), kind=kLoop, calls=%fused_computation.71 | loop fusion | bytes 8847360 | tf_op jit(solution)/shard_map/slice | solution.py:36
  14.6 11.5 %all-to-all-start = ((bf16[32,128,128]{2,0,1:T(8,128)(2,1)}), bf16[32,128,128]{2,0,1:T(8,128)(2,1)S(1)}, u32[]{:S(2)}, u32[]{:S(2)}) async-start(bf16[32,128,128]{2,0,1:T(8,128)(2,1)} %pad.16), calls=%async_computation | async-start | bytes 2097152 | tf_op jit(solution)/shard_map/all_to_all | solution.py:166
  26.8 18.2 %all-to-all-done = bf16[32,128,128]{2,0,1:T(8,128)(2,1)S(1)} async-done(((bf16[32,128,128]{2,0,1:T(8,128)(2,1)}), bf16[32,128,128]{2,0,1:T(8,128)(2,1)S(1)}, u32[]{:S(2)}, u32[]{:S(2)}) %all-to-all-start) | async-done | bytes 1048608 | tf_op jit(solution)/shard_map/all_to_all | solution.py:166
  45.1 2.2 %copy.56 = bf16[30,128,128]{2,0,1:T(8,128)(2,1)S(1)} copy(bf16[30,128,128]{2,1,0:T(8,128)(2,1)} %bitcast.283) | data formatting | bytes 1966080
  48.5 4.4 %all-to-all-start.2 = ((bf16[32,128,128]{2,0,1:T(8,128)(2,1)}), bf16[32,128,128]{2,0,1:T(8,128)(2,1)S(1)}, u32[]{:S(2)}, u32[]{:S(2)}) async-start(bf16[32,128,128]{2,0,1:T(8,128)(2,1)} %pad.17.clone), calls=%async_computation.2 | async-start | bytes 2097152 | tf_op jit(solution)/shard_map/all_to_all | solution.py:166
  53.6 5.2 %shard_map.110 = (f32[128,32,128]{2,1,0:T(8,128)}, bf16[128,32,128]{2,1,0:T(8,128)(2,1)}) custom-call(s32[1]{0:T(128)} %get-tuple-element.37.dil_ref, bf16[128,32,128]{2,1,0:T(8,128)(2,1)} %bitcast.247, bf16[640,128]{1,0:T(8,128)(2,1)} %bitcast.286), custom_call_target="tpu_custom_call" | custom-call | flops 671088640 | bytes 4194304 | tf_op jit(solution)/shard_map/pallas_call | solution.py:207
  58.8 5.2 %shard_map.111 = (f32[128,32,128]{2,1,0:T(8,128)}, bf16[128,32,128]{2,1,0:T(8,128)(2,1)}) custom-call(s32[1]{0:T(128)} %get-tuple-element.38.dil_ref, bf16[128,32,128]{2,1,0:T(8,128)(2,1)} %get-tuple-element.12.act_ref, bf16[640,128]{1,0:T(8,128)(2,1)} %bitcast.288), custom_call_target="tpu_custom_call" | custom-call | flops 671088640 | bytes 4194304 | tf_op jit(solution)/shard_map/pallas_call | solution.py:207
  67.3 4.6 %all-to-all-done.2 = bf16[32,128,128]{2,0,1:T(8,128)(2,1)S(1)} async-done(((bf16[32,128,128]{2,0,1:T(8,128)(2,1)}), bf16[32,128,128]{2,0,1:T(8,128)(2,1)S(1)}, u32[]{:S(2)}, u32[]{:S(2)}) %all-to-all-start.2) | async-done | bytes 1048608 | tf_op jit(solution)/shard_map/all_to_all | solution.py:166
  71.9 5.7 %all-to-all-start.1 = ((bf16[32,128,128]{2,0,1:T(8,128)(2,1)}), bf16[32,128,128]{2,0,1:T(8,128)(2,1)}, u32[]{:S(2)}, u32[]{:S(2)}) async-start(bf16[32,128,128]{2,0,1:T(8,128)(2,1)} %bitcast.253), calls=%async_computation.1 | async-start | bytes 2097152 | tf_op jit(solution)/shard_map/all_to_all | solution.py:172
  81.1 5.6 %shard_map.112.grad_ref = bf16[128,32,128]{2,1,0:T(8,128)(2,1)} custom-call(s32[1]{0:T(128)} %get-tuple-element.38.dil_ref, bf16[128,32,128]{2,1,0:T(8,128)(2,1)} %get-tuple-element.12.act_ref, bf16[128,32,128]{2,1,0:T(8,128)(2,1)} %fusion.1.grad_ref, bf16[640,128]{1,0:T(8,128)(2,1)} %bitcast.289, f32[128,32,128]{2,1,0:T(8,128)} %get-tuple-element.16.rest_0_), custom_call_target="tpu_custom_call" | custom-call | flops 671088640 | bytes 5242880 | tf_op jit(solution)/shard_map/pallas_call | solution.py:316
  86.7 4.8 %shard_map.113 = bf16[128,32,128]{2,1,0:T(8,128)(2,1)} custom-call(s32[1]{0:T(128)} %get-tuple-element.37.dil_ref, bf16[128,32,128]{2,1,0:T(8,128)(2,1)} %bitcast.248, bf16[128,32,128]{2,1,0:T(8,128)(2,1)} %shard_map.112.grad_ref, bf16[640,128]{1,0:T(8,128)(2,1)} %bitcast.287), custom_call_target="tpu_custom_call" | custom-call | flops 671088640 | bytes 5242880 | tf_op jit(solution)/shard_map/pallas_call | solution.py:316
  91.4 4.8 %all-to-all-done.1 = bf16[32,128,128]{2,0,1:T(8,128)(2,1)} async-done(((bf16[32,128,128]{2,0,1:T(8,128)(2,1)}), bf16[32,128,128]{2,0,1:T(8,128)(2,1)}, u32[]{:S(2)}, u32[]{:S(2)}) %all-to-all-start.1) | async-done | bytes 1048608 | tf_op jit(solution)/shard_map/all_to_all | solution.py:172
  96.2 5.5 %all-to-all-start.3 = ((bf16[32,128,128]{2,0,1:T(8,128)(2,1)}), bf16[32,128,128]{2,0,1:T(8,128)(2,1)}, u32[]{:S(2)}, u32[]{:S(2)}) async-start(bf16[32,128,128]{2,0,1:T(8,128)(2,1)} %bitcast.252), calls=%async_computation.3 | async-start | bytes 2097152 | tf_op jit(solution)/shard_map/all_to_all | solution.py:172
  101.7 2.6 %copy.44 = bf16[30,128,128]{2,1,0:T(8,128)(2,1)} copy(bf16[30,128,128]{2,0,1:T(8,128)(2,1)} %bitcast.238) | data formatting | bytes 1966080 | tf_op jit(solution)/shard_map/slice | solution.py:173
  104.2 4.0 %shard_map.115 = f32[5,128,128]{2,1,0:T(8,128)} custom-call(s32[1]{0:T(128)} %get-tuple-element.38.dil_ref, bf16[128,32,128]{2,1,0:T(8,128)(2,1)} %get-tuple-element.12.act_ref, bf16[128,32,128]{2,1,0:T(8,128)(2,1)} %fusion.1.grad_ref), custom_call_target="tpu_custom_call" | custom-call | flops 671088640 | bytes 2097152 | tf_op jit(solution)/shard_map/pallas_call | solution.py:289
  108.3 4.0 %shard_map.114 = f32[5,128,128]{2,1,0:T(8,128)} custom-call(s32[1]{0:T(128)} %get-tuple-element.37.dil_ref, bf16[128,32,128]{2,1,0:T(8,128)(2,1)} %bitcast.249, bf16[128,32,128]{2,1,0:T(8,128)(2,1)} %shard_map.112.grad_ref), custom_call_target="tpu_custom_call" | custom-call | flops 671088640 | bytes 2097152 | tf_op jit(solution)/shard_map/pallas_call | solution.py:289
  114.6 5.6 %all-to-all-done.3 = bf16[32,128,128]{2,0,1:T(8,128)(2,1)} async-done(((bf16[32,128,128]{2,0,1:T(8,128)(2,1)}), bf16[32,128,128]{2,0,1:T(8,128)(2,1)}, u32[]{:S(2)}, u32[]{:S(2)}) %all-to-all-start.3) | async-done | bytes 1048608 | tf_op jit(solution)/shard_map/all_to_all | solution.py:172
  120.3 2.8 %multiply_convert_fusion = bf16[30,128,128]{2,0,1:T(8,128)(2,1)S(1)} fusion(f32[30,128,128]{2,1,0:T(8,128)S(1)} %bitcast.240, bf16[32,128,128]{2,0,1:T(8,128)(2,1)} %all-to-all-done.3), kind=kLoop, calls=%fused_computation.19 | loop fusion | flops 4915200 | bytes 3932160 | tf_op jit(solution)/shard_map/convert_element_type | solution.py:419
  130.1 4.4 %all-to-all-start.4 = ((f32[128,24,128]{2,1,0:T(8,128)}), f32[128,24,128]{2,1,0:T(8,128)S(1)}, u32[]{:S(2)}, u32[]{:S(2)}) async-start(f32[128,24,128]{2,1,0:T(8,128)} %bitcast.246), calls=%async_computation.4 | async-start | bytes 3145728 | tf_op jit(solution)/shard_map/all_to_all | solution.py:342
  137.9 3.2 %pad_slice_fusion = (bf16[1,32,120,128]{3,2,1,0:T(8,128)(2,1)}, bf16[1,32,120,128]{3,2,1,0:T(8,128)(2,1)S(1)}, bf16[1,32,120,128]{3,2,1,0:T(8,128)(2,1)S(1)}, bf...) fusion(bf16[1,32,120,128]{3,2,1,0:T(8,128)(2,1)S(1)} %multiply_, ...), kind=kLoop, calls=%fused_computation.63 | loop fusion | bytes 8847360 | tf_op jit(solution)/shard_map/slice | solution.py:51
  144.4 14.7 %all-to-all-done.4 = f32[128,24,128]{2,1,0:T(8,128)S(1)} async-done(((f32[128,24,128]{2,1,0:T(8,128)}), f32[128,24,128]{2,1,0:T(8,128)S(1)}, u32[]{:S(2)}, u32[]{:S(2)}) %all-to-all-start.4) | async-done | bytes 1572896 | tf_op jit(solution)/shard_map/all_to_all | solution.py:342
  160.3 4.4 %all-to-all-start.5 = ((bf16[128,24,128]{2,1,0:T(8,128)(2,1)}), bf16[128,24,128]{2,1,0:T(8,128)(2,1)S(1)}, u32[]{:S(2)}, u32[]{:S(2)}) async-start(bf16[128,24,128]{2,1,0:T(8,128)(2,1)} %broadcast_in_dim.8), calls=%async_computation.5 | async-start | bytes 1572864 | tf_op jit(solution)/shard_map/all_to_all | solution.py:345
  167.6 2.1 %fusion = bf16[3840,128]{1,0:T(8,128)(2,1)} fusion(f32[3840,128]{1,0:T(8,128)S(1)} %convolution_add_fusion.1, bf16[3840,128]{1,0:T(8,128)(2,1)S(1)} %bitcast.279, bf16[9,128,128]{2,1,0:T(8,128)(2,1)} %param.8), kind=kOutput, calls=%fused_computation.16 | convolution fusion | flops 126812160 | bytes 3964928 | tf_op jit(solution)/shard_map/dot_general | solution.py:54
  169.8 11.2 %all-to-all-done.5 = bf16[128,24,128]{2,1,0:T(8,128)(2,1)S(1)} async-done(((bf16[128,24,128]{2,1,0:T(8,128)(2,1)}), bf16[128,24,128]{2,1,0:T(8,128)(2,1)S(1)}, u32[]{:S(2)}, u32[]{:S(2)}) %all-to-all-start.5) | async-done | bytes 786464 | tf_op jit(solution)/shard_map/all_to_all | solution.py:345
  (92 shorter events, 38.8 us)
Async XLA Ops:
  0.6 7.1 %copy-start.8 = (bf16[9,128,128]{2,1,0:T(8,128)(2,1)S(1)}, bf16[9,128,128]{2,1,0:T(8,128)(2,1)}, u32[]{:S(2)}) copy-start(bf16[9,128,128]{2,1,0:T(8,128)(2,1)} %param.8) | copy-start | bytes 884740
  8.9 1.2 copy-start
  13.5 12.6 %copy-start.12 = (bf16[2,5,128,128]{3,2,1,0:T(8,128)(2,1)S(1)}, bf16[2,5,128,128]{3,2,1,0:T(8,128)(2,1)}, u32[]{:S(2)}) copy-start(bf16[2,5,128,128]{3,2,1,0:T(8,128)(2,1)} %param.9) | copy-start | bytes 983044
  14.6 30.5 %all-to-all-start = ((bf16[32,128,128]{2,0,1:T(8,128)(2,1)}), bf16[32,128,128]{2,0,1:T(8,128)(2,1)S(1)}, u32[]{:S(2)}, u32[]{:S(2)}) async-start(bf16[32,128,128]{2,0,1:T(8,128)(2,1)} %pad.16), calls=%async_computation | async-start | bytes 2097152 | tf_op jit(solution)/shard_map/all_to_all | solution.py:166
  45.1 3.5 %copy-start.2 = (bf16[32,128,128]{2,0,1:T(8,128)(2,1)}, bf16[32,128,128]{2,0,1:T(8,128)(2,1)S(1)}, u32[]{:S(2)}) copy-start(bf16[32,128,128]{2,0,1:T(8,128)(2,1)S(1)} %all-to-all-done) | copy-start | bytes 3145732
  47.3 5.7 %copy-start.15 = (s32[8]{0:T(128)S(1)}, s32[8]{0:T(128)}, u32[]{:S(2)}) copy-start(s32[8]{0:T(128)} %param.11) | copy-start | bytes 100
  47.3 5.7 %copy-start.14 = (s32[2]{0:T(128)S(1)}, s32[2]{0:T(128)}, u32[]{:S(2)}) copy-start(s32[2]{0:T(128)} %param.12) | copy-start | bytes 28
  48.5 23.4 %all-to-all-start.2 = ((bf16[32,128,128]{2,0,1:T(8,128)(2,1)}), bf16[32,128,128]{2,0,1:T(8,128)(2,1)S(1)}, u32[]{:S(2)}, u32[]{:S(2)}) async-start(bf16[32,128,128]{2,0,1:T(8,128)(2,1)} %pad.17.clone), calls=%async_computation.2 | async-start | bytes 2097152 | tf_op jit(solution)/shard_map/all_to_all | solution.py:166
  58.8 6.9 %copy-start.13 = (bf16[2,128,128]{2,1,0:T(8,128)(2,1)S(1)}, bf16[2,128,128]{2,1,0:T(8,128)(2,1)}, u32[]{:S(2)}) copy-start(bf16[2,128,128]{2,1,0:T(8,128)(2,1)} %param.10) | copy-start | bytes 196612
  63.9 1.9 %copy-start.3 = (bf16[128,32,128]{2,1,0:T(8,128)(2,1)S(1)}, bf16[128,32,128]{2,1,0:T(8,128)(2,1)}, u32[]{:S(2)}) copy-start(bf16[128,32,128]{2,1,0:T(8,128)(2,1)} %get-tuple-element.13) | copy-start | bytes 3145732
  71.9 24.3 %all-to-all-start.1 = ((bf16[32,128,128]{2,0,1:T(8,128)(2,1)}), bf16[32,128,128]{2,0,1:T(8,128)(2,1)}, u32[]{:S(2)}, u32[]{:S(2)}) async-start(bf16[32,128,128]{2,0,1:T(8,128)(2,1)} %bitcast.253), calls=%async_computation.1 | async-start | bytes 2097152 | tf_op jit(solution)/shard_map/all_to_all | solution.py:172
  77.7 1.6 copy-start.7
  96.2 24.1 %all-to-all-start.3 = ((bf16[32,128,128]{2,0,1:T(8,128)(2,1)}), bf16[32,128,128]{2,0,1:T(8,128)(2,1)}, u32[]{:S(2)}, u32[]{:S(2)}) async-start(bf16[32,128,128]{2,0,1:T(8,128)(2,1)} %bitcast.252), calls=%async_computation.3 | async-start | bytes 2097152 | tf_op jit(solution)/shard_map/all_to_all | solution.py:172
  112.3 1.2 copy-start.4
  113.5 1.0 copy-start.10
  113.5 1.1 copy-start.11
  123.0 1.2 copy-start.1
  130.1 29.0 %all-to-all-start.4 = ((f32[128,24,128]{2,1,0:T(8,128)}), f32[128,24,128]{2,1,0:T(8,128)S(1)}, u32[]{:S(2)}, u32[]{:S(2)}) async-start(f32[128,24,128]{2,1,0:T(8,128)} %bitcast.246), calls=%async_computation.4 | async-start | bytes 3145728 | tf_op jit(solution)/shard_map/all_to_all | solution.py:342
  137.9 3.2 %copy-start.9 = (bf16[9,128,128]{2,1,0:T(8,128)(2,1)S(1)}, bf16[9,128,128]{2,1,0:T(8,128)(2,1)}, u32[]{:S(2)}) copy-start(bf16[9,128,128]{2,1,0:T(8,128)(2,1)} %param.8) | copy-start | bytes 884740
  160.3 20.7 %all-to-all-start.5 = ((bf16[128,24,128]{2,1,0:T(8,128)(2,1)}), bf16[128,24,128]{2,1,0:T(8,128)(2,1)S(1)}, u32[]{:S(2)}, u32[]{:S(2)}) async-start(bf16[128,24,128]{2,1,0:T(8,128)(2,1)} %broadcast_in_dim.8), calls=%async_computation.5 | async-start | bytes 1572864 | tf_op jit(solution)/shard_map/all_to_all | solution.py:345
  164.6 1.7 copy-start.5
  166.4 1.3 copy-start.6

commit v9 on v8

--- a/solution.py
+++ b/solution.py
@@ -154,7 +154,7 @@
 
 
 HALO = 2 * DMAX
-FB = 16
+FB = 32
 
 
 def fm_to_pixels(flat):

time: 185 us -> 185 us (level)
  no operation moved by 1% of the time
where the time goes in v9:
time: 185 us; the launch traced here: 184 us
  waiting for transfers between devices  58.8 us (32%)
  starting transfers between devices  36.1 us (20%)
  Pallas kernels  28.9 us (16%)
  local copies, waits for them, and re-layouts  27.5 us (15%)
  matrix products  20.3 us (11%)
  other arithmetic  11.1 us (6%)
    all_to_all x2, waiting for transfers between devices, fm_to_pixels(): lax.all_to_all(strided, ('seg', 'grp'), split_axis=1, concat_axis=1, tile...  22.8 us
    all_to_all x2, starting transfers between devices, fm_to_pixels(): lax.all_to_all(strided, ('seg', 'grp'), split_axis=1, concat_axis=1, tile...  15.9 us
    all_to_all x1, waiting for transfers between devices, all_sum(): lax.all_to_all(stack, ('seg', 'grp'), split_axis=0, concat_axis=0, tiled=...  14.7 us
    all_to_all x2, starting transfers between devices, fm_to_frames(): lax.all_to_all(moved, ('seg', 'grp'), split_axis=1, concat_axis=1, tiled=...  11.4 us
    all_to_all x1, waiting for transfers between devices, all_sum(): lax.all_to_all(spread, ('seg', 'grp'), split_axis=0, concat_axis=0, tiled...  11.2 us
    pallas_call x2, Pallas kernels, temporal_backward_k(): pl.pallas_call(functools.partial(tbwd_kernel, with_pre), grid_spec=pltpu....  10.6 us
    pallas_call x2, Pallas kernels, temporal_forward_k(): pl.pallas_call(tfwd_kernel, grid_spec=pltpu.PrefetchScalarGridSpec(num_sc...  10.3 us
    all_to_all x2, waiting for transfers between devices, fm_to_frames(): lax.all_to_all(moved, ('seg', 'grp'), split_axis=1, concat_axis=1, tiled=...  10.2 us
  transfers between devices with their start and end apart: 6, of which 6 were waited for; matrix products, arithmetic and copies ran while one was open for 14% of the time, Pallas kernels for 16%

profile of v9, /device:TPU:1, one launch (start us, length us, event | category | flops | bytes accessed | tf_op | source)
XLA Modules:
  0.0 183.7 jit_solution(9881014098945214485)
XLA Ops:
  0.6 7.0 %pad_slice_fusion.8 = (bf16[1,32,120,128]{3,2,1,0:T(8,128)(2,1)S(1)}, bf16[1,32,120,128]{3,2,1,0:T(8,128)(2,1)S(1)}, bf16[1,32,120,128]{3,2,1,0:T(8,128)(2,1)S(1...) fusion(bf16[1,32,120,128]{3,2,1,0:T(8,128)(2,1)} %param.7), kind=kLoop, calls=%fused_computation.71 | loop fusion | bytes 8847360 | tf_op jit(solution)/shard_map/slice | solution.py:36
  14.6 11.5 %all-to-all-start = ((bf16[32,128,128]{2,0,1:T(8,128)(2,1)}), bf16[32,128,128]{2,0,1:T(8,128)(2,1)S(1)}, u32[]{:S(2)}, u32[]{:S(2)}) async-start(bf16[32,128,128]{2,0,1:T(8,128)(2,1)} %pad.16), calls=%async_computation | async-start | bytes 2097152 | tf_op jit(solution)/shard_map/all_to_all | solution.py:166
  26.8 18.2 %all-to-all-done = bf16[32,128,128]{2,0,1:T(8,128)(2,1)S(1)} async-done(((bf16[32,128,128]{2,0,1:T(8,128)(2,1)}), bf16[32,128,128]{2,0,1:T(8,128)(2,1)S(1)}, u32[]{:S(2)}, u32[]{:S(2)}) %all-to-all-start) | async-done | bytes 1048608 | tf_op jit(solution)/shard_map/all_to_all | solution.py:166
  45.1 2.2 %copy.56 = bf16[30,128,128]{2,0,1:T(8,128)(2,1)S(1)} copy(bf16[30,128,128]{2,1,0:T(8,128)(2,1)} %bitcast.283) | data formatting | bytes 1966080
  48.5 4.4 %all-to-all-start.2 = ((bf16[32,128,128]{2,0,1:T(8,128)(2,1)}), bf16[32,128,128]{2,0,1:T(8,128)(2,1)S(1)}, u32[]{:S(2)}, u32[]{:S(2)}) async-start(bf16[32,128,128]{2,0,1:T(8,128)(2,1)} %pad.17.clone), calls=%async_computation.2 | async-start | bytes 2097152 | tf_op jit(solution)/shard_map/all_to_all | solution.py:166
  53.6 5.2 %shard_map.110 = (f32[128,32,128]{2,1,0:T(8,128)}, bf16[128,32,128]{2,1,0:T(8,128)(2,1)}) custom-call(s32[1]{0:T(128)} %get-tuple-element.37.dil_ref, bf16[128,32,128]{2,1,0:T(8,128)(2,1)} %bitcast.247, bf16[640,128]{1,0:T(8,128)(2,1)} %bitcast.286), custom_call_target="tpu_custom_call" | custom-call | flops 671088640 | bytes 4194304 | tf_op jit(solution)/shard_map/pallas_call | solution.py:207
  58.8 5.2 %shard_map.111 = (f32[128,32,128]{2,1,0:T(8,128)}, bf16[128,32,128]{2,1,0:T(8,128)(2,1)}) custom-call(s32[1]{0:T(128)} %get-tuple-element.38.dil_ref, bf16[128,32,128]{2,1,0:T(8,128)(2,1)} %get-tuple-element.12.act_ref, bf16[640,128]{1,0:T(8,128)(2,1)} %bitcast.288), custom_call_target="tpu_custom_call" | custom-call | flops 671088640 | bytes 4194304 | tf_op jit(solution)/shard_map/pallas_call | solution.py:207
  67.3 4.6 %all-to-all-done.2 = bf16[32,128,128]{2,0,1:T(8,128)(2,1)S(1)} async-done(((bf16[32,128,128]{2,0,1:T(8,128)(2,1)}), bf16[32,128,128]{2,0,1:T(8,128)(2,1)S(1)}, u32[]{:S(2)}, u32[]{:S(2)}) %all-to-all-start.2) | async-done | bytes 1048608 | tf_op jit(solution)/shard_map/all_to_all | solution.py:166
  71.9 5.7 %all-to-all-start.1 = ((bf16[32,128,128]{2,0,1:T(8,128)(2,1)}), bf16[32,128,128]{2,0,1:T(8,128)(2,1)}, u32[]{:S(2)}, u32[]{:S(2)}) async-start(bf16[32,128,128]{2,0,1:T(8,128)(2,1)} %bitcast.253), calls=%async_computation.1 | async-start | bytes 2097152 | tf_op jit(solution)/shard_map/all_to_all | solution.py:172
  81.1 5.8 %shard_map.112.grad_ref = bf16[128,32,128]{2,1,0:T(8,128)(2,1)} custom-call(s32[1]{0:T(128)} %get-tuple-element.38.dil_ref, bf16[128,32,128]{2,1,0:T(8,128)(2,1)} %get-tuple-element.12.act_ref, bf16[128,32,128]{2,1,0:T(8,128)(2,1)} %fusion.1.grad_ref, bf16[640,128]{1,0:T(8,128)(2,1)} %bitcast.289, f32[128,32,128]{2,1,0:T(8,128)} %get-tuple-element.16.rest_0_), custom_call_target="tpu_custom_call" | custom-call | flops 671088640 | bytes 5242880 | tf_op jit(solution)/shard_map/pallas_call | solution.py:316
  86.9 4.8 %shard_map.113 = bf16[128,32,128]{2,1,0:T(8,128)(2,1)} custom-call(s32[1]{0:T(128)} %get-tuple-element.37.dil_ref, bf16[128,32,128]{2,1,0:T(8,128)(2,1)} %bitcast.248, bf16[128,32,128]{2,1,0:T(8,128)(2,1)} %shard_map.112.grad_ref, bf16[640,128]{1,0:T(8,128)(2,1)} %bitcast.287), custom_call_target="tpu_custom_call" | custom-call | flops 671088640 | bytes 5242880 | tf_op jit(solution)/shard_map/pallas_call | solution.py:316
  91.7 4.5 %all-to-all-done.1 = bf16[32,128,128]{2,0,1:T(8,128)(2,1)} async-done(((bf16[32,128,128]{2,0,1:T(8,128)(2,1)}), bf16[32,128,128]{2,0,1:T(8,128)(2,1)}, u32[]{:S(2)}, u32[]{:S(2)}) %all-to-all-start.1) | async-done | bytes 1048608 | tf_op jit(solution)/shard_map/all_to_all | solution.py:172
  96.2 5.7 %all-to-all-start.3 = ((bf16[32,128,128]{2,0,1:T(8,128)(2,1)}), bf16[32,128,128]{2,0,1:T(8,128)(2,1)}, u32[]{:S(2)}, u32[]{:S(2)}) async-start(bf16[32,128,128]{2,0,1:T(8,128)(2,1)} %bitcast.252), calls=%async_computation.3 | async-start | bytes 2097152 | tf_op jit(solution)/shard_map/all_to_all | solution.py:172
  101.9 2.6 %copy.44 = bf16[30,128,128]{2,1,0:T(8,128)(2,1)} copy(bf16[30,128,128]{2,0,1:T(8,128)(2,1)} %bitcast.238) | data formatting | bytes 1966080 | tf_op jit(solution)/shard_map/slice | solution.py:173
  104.5 4.0 %shard_map.115 = f32[5,128,128]{2,1,0:T(8,128)} custom-call(s32[1]{0:T(128)} %get-tuple-element.38.dil_ref, bf16[128,32,128]{2,1,0:T(8,128)(2,1)} %get-tuple-element.12.act_ref, bf16[128,32,128]{2,1,0:T(8,128)(2,1)} %fusion.1.grad_ref), custom_call_target="tpu_custom_call" | custom-call | flops 671088640 | bytes 2097152 | tf_op jit(solution)/shard_map/pallas_call | solution.py:289
  108.5 4.0 %shard_map.114 = f32[5,128,128]{2,1,0:T(8,128)} custom-call(s32[1]{0:T(128)} %get-tuple-element.37.dil_ref, bf16[128,32,128]{2,1,0:T(8,128)(2,1)} %bitcast.249, bf16[128,32,128]{2,1,0:T(8,128)(2,1)} %shard_map.112.grad_ref), custom_call_target="tpu_custom_call" | custom-call | flops 671088640 | bytes 2097152 | tf_op jit(solution)/shard_map/pallas_call | solution.py:289
  114.9 5.7 %all-to-all-done.3 = bf16[32,128,128]{2,0,1:T(8,128)(2,1)} async-done(((bf16[32,128,128]{2,0,1:T(8,128)(2,1)}), bf16[32,128,128]{2,0,1:T(8,128)(2,1)}, u32[]{:S(2)}, u32[]{:S(2)}) %all-to-all-start.3) | async-done | bytes 1048608 | tf_op jit(solution)/shard_map/all_to_all | solution.py:172
  120.5 2.8 %multiply_convert_fusion = bf16[30,128,128]{2,0,1:T(8,128)(2,1)S(1)} fusion(f32[30,128,128]{2,1,0:T(8,128)S(1)} %bitcast.240, bf16[32,128,128]{2,0,1:T(8,128)(2,1)} %all-to-all-done.3), kind=kLoop, calls=%fused_computation.19 | loop fusion | flops 4915200 | bytes 3932160 | tf_op jit(solution)/shard_map/convert_element_type | solution.py:419
  130.4 4.4 %all-to-all-start.4 = ((f32[128,24,128]{2,1,0:T(8,128)}), f32[128,24,128]{2,1,0:T(8,128)S(1)}, u32[]{:S(2)}, u32[]{:S(2)}) async-start(f32[128,24,128]{2,1,0:T(8,128)} %bitcast.246), calls=%async_computation.4 | async-start | bytes 3145728 | tf_op jit(solution)/shard_map/all_to_all | solution.py:342
  138.2 3.2 %pad_slice_fusion = (bf16[1,32,120,128]{3,2,1,0:T(8,128)(2,1)}, bf16[1,32,120,128]{3,2,1,0:T(8,128)(2,1)S(1)}, bf16[1,32,120,128]{3,2,1,0:T(8,128)(2,1)S(1)}, bf...) fusion(bf16[1,32,120,128]{3,2,1,0:T(8,128)(2,1)S(1)} %multiply_, ...), kind=kLoop, calls=%fused_computation.63 | loop fusion | bytes 8847360 | tf_op jit(solution)/shard_map/slice | solution.py:51
  144.6 14.7 %all-to-all-done.4 = f32[128,24,128]{2,1,0:T(8,128)S(1)} async-done(((f32[128,24,128]{2,1,0:T(8,128)}), f32[128,24,128]{2,1,0:T(8,128)S(1)}, u32[]{:S(2)}, u32[]{:S(2)}) %all-to-all-start.4) | async-done | bytes 1572896 | tf_op jit(solution)/shard_map/all_to_all | solution.py:342
  160.5 4.4 %all-to-all-start.5 = ((bf16[128,24,128]{2,1,0:T(8,128)(2,1)}), bf16[128,24,128]{2,1,0:T(8,128)(2,1)S(1)}, u32[]{:S(2)}, u32[]{:S(2)}) async-start(bf16[128,24,128]{2,1,0:T(8,128)(2,1)} %broadcast_in_dim.8), calls=%async_computation.5 | async-start | bytes 1572864 | tf_op jit(solution)/shard_map/all_to_all | solution.py:345
  167.9 2.1 %fusion = bf16[3840,128]{1,0:T(8,128)(2,1)} fusion(f32[3840,128]{1,0:T(8,128)S(1)} %convolution_add_fusion.1, bf16[3840,128]{1,0:T(8,128)(2,1)S(1)} %bitcast.279, bf16[9,128,128]{2,1,0:T(8,128)(2,1)} %param.8), kind=kOutput, calls=%fused_computation.16 | convolution fusion | flops 126812160 | bytes 3964928 | tf_op jit(solution)/shard_map/dot_general | solution.py:54
  170.0 11.2 %all-to-all-done.5 = bf16[128,24,128]{2,1,0:T(8,128)(2,1)S(1)} async-done(((bf16[128,24,128]{2,1,0:T(8,128)(2,1)}), bf16[128,24,128]{2,1,0:T(8,128)(2,1)S(1)}, u32[]{:S(2)}, u32[]{:S(2)}) %all-to-all-start.5) | async-done | bytes 786464 | tf_op jit(solution)/shard_map/all_to_all | solution.py:345
  (92 shorter events, 38.9 us)
Async XLA Ops:
  0.6 7.1 %copy-start.8 = (bf16[9,128,128]{2,1,0:T(8,128)(2,1)S(1)}, bf16[9,128,128]{2,1,0:T(8,128)(2,1)}, u32[]{:S(2)}) copy-start(bf16[9,128,128]{2,1,0:T(8,128)(2,1)} %param.8) | copy-start | bytes 884740
  8.9 1.2 copy-start
  13.5 12.6 %copy-start.12 = (bf16[2,5,128,128]{3,2,1,0:T(8,128)(2,1)S(1)}, bf16[2,5,128,128]{3,2,1,0:T(8,128)(2,1)}, u32[]{:S(2)}) copy-start(bf16[2,5,128,128]{3,2,1,0:T(8,128)(2,1)} %param.9) | copy-start | bytes 983044
  14.6 30.5 %all-to-all-start = ((bf16[32,128,128]{2,0,1:T(8,128)(2,1)}), bf16[32,128,128]{2,0,1:T(8,128)(2,1)S(1)}, u32[]{:S(2)}, u32[]{:S(2)}) async-start(bf16[32,128,128]{2,0,1:T(8,128)(2,1)} %pad.16), calls=%async_computation | async-start | bytes 2097152 | tf_op jit(solution)/shard_map/all_to_all | solution.py:166
  45.1 3.5 %copy-start.2 = (bf16[32,128,128]{2,0,1:T(8,128)(2,1)}, bf16[32,128,128]{2,0,1:T(8,128)(2,1)S(1)}, u32[]{:S(2)}) copy-start(bf16[32,128,128]{2,0,1:T(8,128)(2,1)S(1)} %all-to-all-done) | copy-start | bytes 3145732
  47.3 5.7 %copy-start.15 = (s32[8]{0:T(128)S(1)}, s32[8]{0:T(128)}, u32[]{:S(2)}) copy-start(s32[8]{0:T(128)} %param.11) | copy-start | bytes 100
  47.3 5.7 %copy-start.14 = (s32[2]{0:T(128)S(1)}, s32[2]{0:T(128)}, u32[]{:S(2)}) copy-start(s32[2]{0:T(128)} %param.12) | copy-start | bytes 28
  48.5 23.4 %all-to-all-start.2 = ((bf16[32,128,128]{2,0,1:T(8,128)(2,1)}), bf16[32,128,128]{2,0,1:T(8,128)(2,1)S(1)}, u32[]{:S(2)}, u32[]{:S(2)}) async-start(bf16[32,128,128]{2,0,1:T(8,128)(2,1)} %pad.17.clone), calls=%async_computation.2 | async-start | bytes 2097152 | tf_op jit(solution)/shard_map/all_to_all | solution.py:166
  58.8 6.9 %copy-start.13 = (bf16[2,128,128]{2,1,0:T(8,128)(2,1)S(1)}, bf16[2,128,128]{2,1,0:T(8,128)(2,1)}, u32[]{:S(2)}) copy-start(bf16[2,128,128]{2,1,0:T(8,128)(2,1)} %param.10) | copy-start | bytes 196612
  63.9 1.9 %copy-start.3 = (bf16[128,32,128]{2,1,0:T(8,128)(2,1)S(1)}, bf16[128,32,128]{2,1,0:T(8,128)(2,1)}, u32[]{:S(2)}) copy-start(bf16[128,32,128]{2,1,0:T(8,128)(2,1)} %get-tuple-element.13) | copy-start | bytes 3145732
  71.9 24.3 %all-to-all-start.1 = ((bf16[32,128,128]{2,0,1:T(8,128)(2,1)}), bf16[32,128,128]{2,0,1:T(8,128)(2,1)}, u32[]{:S(2)}, u32[]{:S(2)}) async-start(bf16[32,128,128]{2,0,1:T(8,128)(2,1)} %bitcast.253), calls=%async_computation.1 | async-start | bytes 2097152 | tf_op jit(solution)/shard_map/all_to_all | solution.py:172
  77.7 1.6 copy-start.7
  96.2 24.3 %all-to-all-start.3 = ((bf16[32,128,128]{2,0,1:T(8,128)(2,1)}), bf16[32,128,128]{2,0,1:T(8,128)(2,1)}, u32[]{:S(2)}, u32[]{:S(2)}) async-start(bf16[32,128,128]{2,0,1:T(8,128)(2,1)} %bitcast.252), calls=%async_computation.3 | async-start | bytes 2097152 | tf_op jit(solution)/shard_map/all_to_all | solution.py:172
  112.5 1.2 copy-start.4
  113.7 1.0 copy-start.10
  113.7 1.1 copy-start.11
  123.3 1.2 copy-start.1
  130.4 29.0 %all-to-all-start.4 = ((f32[128,24,128]{2,1,0:T(8,128)}), f32[128,24,128]{2,1,0:T(8,128)S(1)}, u32[]{:S(2)}, u32[]{:S(2)}) async-start(f32[128,24,128]{2,1,0:T(8,128)} %bitcast.246), calls=%async_computation.4 | async-start | bytes 3145728 | tf_op jit(solution)/shard_map/all_to_all | solution.py:342
  138.2 3.2 %copy-start.9 = (bf16[9,128,128]{2,1,0:T(8,128)(2,1)S(1)}, bf16[9,128,128]{2,1,0:T(8,128)(2,1)}, u32[]{:S(2)}) copy-start(bf16[9,128,128]{2,1,0:T(8,128)(2,1)} %param.8) | copy-start | bytes 884740
  160.5 20.7 %all-to-all-start.5 = ((bf16[128,24,128]{2,1,0:T(8,128)(2,1)}), bf16[128,24,128]{2,1,0:T(8,128)(2,1)S(1)}, u32[]{:S(2)}, u32[]{:S(2)}) async-start(bf16[128,24,128]{2,1,0:T(8,128)(2,1)} %broadcast_in_dim.8), calls=%async_computation.5 | async-start | bytes 1572864 | tf_op jit(solution)/shard_map/all_to_all | solution.py:345
  164.9 1.7 copy-start.5
  166.6 1.3 copy-start.6

commit v10 on v9

--- a/solution.py
+++ b/solution.py
@@ -187,42 +187,42 @@
 
 def tfwd_kernel(dil_ref, act_ref, w_ref, pre_ref, out_ref, pad_ref):
     frames, width, chans = act_ref.shape
-    fill_halo(act_ref, pad_ref)
+
+    @pl.when(pl.program_id(0) == 0)
+    def _():
+        fill_halo(act_ref, pad_ref)
+
     step = dil_ref[0]
     rows = FB * width
-    for block in range(frames // FB):
-        base = HALO + block * FB
-        stacked = jnp.concatenate(
-            [tap_rows(pad_ref, base + (tap - 2) * step, rows) for tap in range(5)], axis=1
-        )
-        pre = jnp.dot(stacked, w_ref[...], preferred_element_type=jnp.float32)
-        pre_ref[block * FB : (block + 1) * FB] = pre.reshape(FB, width, chans)
-        out_ref[block * FB : (block + 1) * FB] = (
-            (pre / (1.0 + jnp.exp(-pre))).astype(jnp.bfloat16).reshape(FB, width, chans)
-        )
+    base = HALO + pl.program_id(0) * FB
+    stacked = jnp.concatenate(
+        [tap_rows(pad_ref, base + (tap - 2) * step, rows) for tap in range(5)], axis=1
+    )
+    pre = jnp.dot(stacked, w_ref[...], preferred_element_type=jnp.float32)
+    pre_ref[...] = pre.reshape(FB, width, chans)
+    out_ref[...] = (pre / (1.0 + jnp.exp(-pre))).astype(jnp.bfloat16).reshape(FB, width, chans)
 
 
 def temporal_forward_k(acts, kernel, step_size):
     frames, width, chans = acts.shape
+    part = pl.BlockSpec((FB, width, chans), lambda i, d: (i, 0, 0))
     return pl.pallas_call(
         tfwd_kernel,
         grid_spec=pltpu.PrefetchScalarGridSpec(
             num_scalar_prefetch=1,
-            grid=(1,),
+            grid=(frames // FB,),
             in_specs=[
                 pl.BlockSpec(acts.shape, lambda i, d: (0, 0, 0)),
                 pl.BlockSpec((5 * chans, chans), lambda i, d: (0, 0)),
             ],
-            out_specs=[
-                pl.BlockSpec(acts.shape, lambda i, d: (0, 0, 0)),
-                pl.BlockSpec(acts.shape, lambda i, d: (0, 0, 0)),
-            ],
+            out_specs=[part, part],
             scratch_shapes=[pltpu.VMEM((frames + 2 * HALO, width, chans), jnp.bfloat16)],
         ),
         out_shape=[
             jax.ShapeDtypeStruct(acts.shape, jnp.float32),
             jax.ShapeDtypeStruct(acts.shape, jnp.bfloat16),
         ],
+        compiler_params=pltpu.CompilerParams(dimension_semantics=("arbitrary",)),
         cost_estimate=pl.CostEstimate(
             flops=2 * frames * width * chans * chans * 5,
             transcendentals=frames * width * chans,
@@ -231,36 +231,37 @@
     )(step_size.reshape(1), acts, kernel.reshape(5 * chans, chans))
 
 
-def tbwd_kernel(with_pre, dil_ref, act_ref, grad_ref, wt_ref, *rest):
+def tbwd_kernel(with_pre, dil_ref, grad_ref, wt_ref, *rest):
     if with_pre:
         pre_ref, out_ref, pad_ref = rest
     else:
         out_ref, pad_ref = rest
-    frames, width, chans = act_ref.shape
-    fill_halo(grad_ref, pad_ref)
+    frames, width, chans = grad_ref.shape
+
+    @pl.when(pl.program_id(0) == 0)
+    def _():
+        fill_halo(grad_ref, pad_ref)
+
     step = dil_ref[0]
     rows = FB * width
-    for block in range(frames // FB):
-        base = HALO + block * FB
-        stacked = jnp.concatenate(
-            [tap_rows(pad_ref, base - (tap - 2) * step, rows) for tap in range(5)], axis=1
+    base = HALO + pl.program_id(0) * FB
+    stacked = jnp.concatenate(
+        [tap_rows(pad_ref, base - (tap - 2) * step, rows) for tap in range(5)], axis=1
+    )
+    grad_act = None
+    for tap in range(5):
+        term = lax.dot_general(
+            stacked[:, tap * chans : (tap + 1) * chans],
+            wt_ref[tap * chans : (tap + 1) * chans, :],
+            (((1,), (1,)), ((), ())),
+            preferred_element_type=jnp.float32,
         )
-        grad_act = None
-        for tap in range(5):
-            term = lax.dot_general(
-                stacked[:, tap * chans : (tap + 1) * chans],
-                wt_ref[tap * chans : (tap + 1) * chans, :],
-                (((1,), (1,)), ((), ())),
-                preferred_element_type=jnp.float32,
-            )
-            grad_act = term if grad_act is None else grad_act + term
-        if with_pre:
-            pre = pre_ref[block * FB : (block + 1) * FB].reshape(rows, chans)
-            sigma = 1.0 / (1.0 + jnp.exp(-pre))
-            grad_act = grad_act * (sigma * (1.0 + pre * (1.0 - sigma)))
-        out_ref[block * FB : (block + 1) * FB] = (
-            grad_act.astype(jnp.bfloat16).reshape(FB, width, chans)
-        )
+        grad_act = term if grad_act is None else grad_act + term
+    if with_pre:
+        pre = pre_ref[...].reshape(rows, chans)
+        sigma = 1.0 / (1.0 + jnp.exp(-pre))
+        grad_act = grad_act * (sigma * (1.0 + pre * (1.0 - sigma)))
+    out_ref[...] = grad_act.astype(jnp.bfloat16).reshape(FB, width, chans)
 
 
 def twgrad_kernel(dil_ref, act_ref, grad_ref, tg_ref, pad_ref):
@@ -305,24 +306,28 @@
 
 
 def temporal_backward_k(acts, grads, kernel, step_size, pre_below):
-    frames, width, chans = acts.shape
-    full = pl.BlockSpec(acts.shape, lambda i, d: (0, 0, 0))
+    frames, width, chans = grads.shape
+    part = pl.BlockSpec((FB, width, chans), lambda i, d: (i, 0, 0))
     with_pre = pre_below is not None
-    in_specs = [full, full, pl.BlockSpec((5 * chans, chans), lambda i, d: (0, 0))]
-    operands = [step_size.reshape(1), acts, grads, kernel.reshape(5 * chans, chans)]
+    in_specs = [
+        pl.BlockSpec(grads.shape, lambda i, d: (0, 0, 0)),
+        pl.BlockSpec((5 * chans, chans), lambda i, d: (0, 0)),
+    ]
+    operands = [step_size.reshape(1), grads, kernel.reshape(5 * chans, chans)]
     if with_pre:
-        in_specs.append(full)
+        in_specs.append(part)
         operands.append(pre_below)
     return pl.pallas_call(
         functools.partial(tbwd_kernel, with_pre),
         grid_spec=pltpu.PrefetchScalarGridSpec(
             num_scalar_prefetch=1,
-            grid=(1,),
+            grid=(frames // FB,),
             in_specs=in_specs,
-            out_specs=full,
+            out_specs=part,
             scratch_shapes=[pltpu.VMEM((frames + 2 * HALO, width, chans), jnp.bfloat16)],
         ),
-        out_shape=jax.ShapeDtypeStruct(acts.shape, jnp.bfloat16),
+        out_shape=jax.ShapeDtypeStruct(grads.shape, jnp.bfloat16),
+        compiler_params=pltpu.CompilerParams(dimension_semantics=("arbitrary",)),
         cost_estimate=pl.CostEstimate(
             flops=2 * frames * width * chans * chans * 5,
             transcendentals=frames * width * chans,

time: 185 us -> 185 us (level)
  no operation moved by 1% of the time
where the time goes in v10:
time: 185 us; the launch traced here: 184 us
  waiting for transfers between devices  58.4 us (32%)
  starting transfers between devices  36.6 us (20%)
  Pallas kernels  29.5 us (16%)
  local copies, waits for them, and re-layouts  27.5 us (15%)
  matrix products  20.2 us (11%)
  other arithmetic  11.1 us (6%)
    all_to_all x2, waiting for transfers between devices, fm_to_pixels(): lax.all_to_all(strided, ('seg', 'grp'), split_axis=1, concat_axis=1, tile...  22.3 us
    all_to_all x2, starting transfers between devices, fm_to_pixels(): lax.all_to_all(strided, ('seg', 'grp'), split_axis=1, concat_axis=1, tile...  15.9 us
    all_to_all x1, waiting for transfers between devices, all_sum(): lax.all_to_all(stack, ('seg', 'grp'), split_axis=0, concat_axis=0, tiled=...  14.7 us
    all_to_all x2, starting transfers between devices, fm_to_frames(): lax.all_to_all(moved, ('seg', 'grp'), split_axis=1, concat_axis=1, tiled=...  11.9 us
    all_to_all x1, waiting for transfers between devices, all_sum(): lax.all_to_all(spread, ('seg', 'grp'), split_axis=0, concat_axis=0, tiled...  11.2 us
    pallas_call x2, Pallas kernels, temporal_forward_k(): pl.pallas_call(tfwd_kernel, grid_spec=pltpu.PrefetchScalarGridSpec(num_sc...  10.8 us
    pallas_call x2, Pallas kernels, temporal_backward_k(): pl.pallas_call(functools.partial(tbwd_kernel, with_pre), grid_spec=pltpu....  10.6 us
    all_to_all x2, waiting for transfers between devices, fm_to_frames(): lax.all_to_all(moved, ('seg', 'grp'), split_axis=1, concat_axis=1, tiled=...  10.1 us
  transfers between devices with their start and end apart: 6, of which 6 were waited for; matrix products, arithmetic and copies ran while one was open for 14% of the time, Pallas kernels for 16%

profile of v10, /device:TPU:1, one launch (start us, length us, event | category | flops | bytes accessed | tf_op | source)
XLA Modules:
  0.0 184.2 jit_solution(17142539050648196079)
XLA Ops:
  0.6 7.0 %pad_slice_fusion.8 = (bf16[1,32,120,128]{3,2,1,0:T(8,128)(2,1)S(1)}, bf16[1,32,120,128]{3,2,1,0:T(8,128)(2,1)S(1)}, bf16[1,32,120,128]{3,2,1,0:T(8,128)(2,1)S(1...) fusion(bf16[1,32,120,128]{3,2,1,0:T(8,128)(2,1)} %param.7), kind=kLoop, calls=%fused_computation.71 | loop fusion | bytes 8847360 | tf_op jit(solution)/shard_map/slice | solution.py:36
  14.6 11.5 %all-to-all-start = ((bf16[32,128,128]{2,0,1:T(8,128)(2,1)}), bf16[32,128,128]{2,0,1:T(8,128)(2,1)S(1)}, u32[]{:S(2)}, u32[]{:S(2)}) async-start(bf16[32,128,128]{2,0,1:T(8,128)(2,1)} %pad.16), calls=%async_computation | async-start | bytes 2097152 | tf_op jit(solution)/shard_map/all_to_all | solution.py:166
  26.8 18.2 %all-to-all-done = bf16[32,128,128]{2,0,1:T(8,128)(2,1)S(1)} async-done(((bf16[32,128,128]{2,0,1:T(8,128)(2,1)}), bf16[32,128,128]{2,0,1:T(8,128)(2,1)S(1)}, u32[]{:S(2)}, u32[]{:S(2)}) %all-to-all-start) | async-done | bytes 1048608 | tf_op jit(solution)/shard_map/all_to_all | solution.py:166
  45.1 2.2 %copy.56 = bf16[30,128,128]{2,0,1:T(8,128)(2,1)S(1)} copy(bf16[30,128,128]{2,1,0:T(8,128)(2,1)} %bitcast.282) | data formatting | bytes 1966080
  48.5 4.4 %all-to-all-start.2 = ((bf16[32,128,128]{2,0,1:T(8,128)(2,1)}), bf16[32,128,128]{2,0,1:T(8,128)(2,1)S(1)}, u32[]{:S(2)}, u32[]{:S(2)}) async-start(bf16[32,128,128]{2,0,1:T(8,128)(2,1)} %pad.17.clone), calls=%async_computation.2 | async-start | bytes 2097152 | tf_op jit(solution)/shard_map/all_to_all | solution.py:166
  53.6 5.4 %shard_map.110 = (f32[128,32,128]{2,1,0:T(8,128)}, bf16[128,32,128]{2,1,0:T(8,128)(2,1)}) custom-call(s32[1]{0:T(128)} %get-tuple-element.37.dil_ref, bf16[128,32,128]{2,1,0:T(8,128)(2,1)} %bitcast.279, bf16[640,128]{1,0:T(8,128)(2,1)} %bitcast.294), custom_call_target="tpu_custom_call" | custom-call | flops 671088640 | bytes 4194304 | tf_op jit(solution)/shard_map/pallas_call | solution.py:209
  59.0 5.4 %shard_map.111 = (f32[128,32,128]{2,1,0:T(8,128)}, bf16[128,32,128]{2,1,0:T(8,128)(2,1)}) custom-call(s32[1]{0:T(128)} %get-tuple-element.38.dil_ref, bf16[128,32,128]{2,1,0:T(8,128)(2,1)} %get-tuple-element.12.act_ref, bf16[640,128]{1,0:T(8,128)(2,1)} %bitcast.285), custom_call_target="tpu_custom_call" | custom-call | flops 671088640 | bytes 4194304 | tf_op jit(solution)/shard_map/pallas_call | solution.py:209
  67.8 4.1 %all-to-all-done.2 = bf16[32,128,128]{2,0,1:T(8,128)(2,1)S(1)} async-done(((bf16[32,128,128]{2,0,1:T(8,128)(2,1)}), bf16[32,128,128]{2,0,1:T(8,128)(2,1)S(1)}, u32[]{:S(2)}, u32[]{:S(2)}) %all-to-all-start.2) | async-done | bytes 1048608 | tf_op jit(solution)/shard_map/all_to_all | solution.py:166
  71.9 6.1 %all-to-all-start.1 = ((bf16[32,128,128]{2,0,1:T(8,128)(2,1)}), bf16[32,128,128]{2,0,1:T(8,128)(2,1)}, u32[]{:S(2)}, u32[]{:S(2)}) async-start(bf16[32,128,128]{2,0,1:T(8,128)(2,1)} %bitcast.249), calls=%async_computation.1 | async-start | bytes 2097152 | tf_op jit(solution)/shard_map/all_to_all | solution.py:172
  81.5 5.7 %shard_map.112.grad_ref = bf16[128,32,128]{2,1,0:T(8,128)(2,1)} custom-call(s32[1]{0:T(128)} %get-tuple-element.38.dil_ref, bf16[128,32,128]{2,1,0:T(8,128)(2,1)} %fusion.1.grad_ref, bf16[640,128]{1,0:T(8,128)(2,1)} %bitcast.286, f32[128,32,128]{2,1,0:T(8,128)} %get-tuple-element.16.rest_0_), custom_call_target="tpu_custom_call" | custom-call | flops 671088640 | bytes 5242880 | tf_op jit(solution)/shard_map/pallas_call | solution.py:320
  87.2 5.0 %shard_map.113 = bf16[128,32,128]{2,1,0:T(8,128)(2,1)} custom-call(s32[1]{0:T(128)} %get-tuple-element.37.dil_ref, bf16[128,32,128]{2,1,0:T(8,128)(2,1)} %shard_map.112.grad_ref, bf16[640,128]{1,0:T(8,128)(2,1)} %bitcast.295), custom_call_target="tpu_custom_call" | custom-call | flops 671088640 | bytes 5242880 | tf_op jit(solution)/shard_map/pallas_call | solution.py:320
  92.2 4.5 %all-to-all-done.1 = bf16[32,128,128]{2,0,1:T(8,128)(2,1)} async-done(((bf16[32,128,128]{2,0,1:T(8,128)(2,1)}), bf16[32,128,128]{2,0,1:T(8,128)(2,1)}, u32[]{:S(2)}, u32[]{:S(2)}) %all-to-all-start.1) | async-done | bytes 1048608 | tf_op jit(solution)/shard_map/all_to_all | solution.py:172
  96.6 5.8 %all-to-all-start.3 = ((bf16[32,128,128]{2,0,1:T(8,128)(2,1)}), bf16[32,128,128]{2,0,1:T(8,128)(2,1)}, u32[]{:S(2)}, u32[]{:S(2)}) async-start(bf16[32,128,128]{2,0,1:T(8,128)(2,1)} %bitcast.281), calls=%async_computation.3 | async-start | bytes 2097152 | tf_op jit(solution)/shard_map/all_to_all | solution.py:172
  102.4 2.6 %copy.44 = bf16[30,128,128]{2,1,0:T(8,128)(2,1)} copy(bf16[30,128,128]{2,0,1:T(8,128)(2,1)} %bitcast.238) | data formatting | bytes 1966080 | tf_op jit(solution)/shard_map/slice | solution.py:173
  105.0 4.0 %shard_map.115 = f32[5,128,128]{2,1,0:T(8,128)} custom-call(s32[1]{0:T(128)} %get-tuple-element.38.dil_ref, bf16[128,32,128]{2,1,0:T(8,128)(2,1)} %get-tuple-element.12.act_ref, bf16[128,32,128]{2,1,0:T(8,128)(2,1)} %fusion.1.grad_ref), custom_call_target="tpu_custom_call" | custom-call | flops 671088640 | bytes 2097152 | tf_op jit(solution)/shard_map/pallas_call | solution.py:290
  109.0 4.0 %shard_map.114 = f32[5,128,128]{2,1,0:T(8,128)} custom-call(s32[1]{0:T(128)} %get-tuple-element.37.dil_ref, bf16[128,32,128]{2,1,0:T(8,128)(2,1)} %bitcast.280, bf16[128,32,128]{2,1,0:T(8,128)(2,1)} %shard_map.112.grad_ref), custom_call_target="tpu_custom_call" | custom-call | flops 671088640 | bytes 2097152 | tf_op jit(solution)/shard_map/pallas_call | solution.py:290
  115.3 5.7 %all-to-all-done.3 = bf16[32,128,128]{2,0,1:T(8,128)(2,1)} async-done(((bf16[32,128,128]{2,0,1:T(8,128)(2,1)}), bf16[32,128,128]{2,0,1:T(8,128)(2,1)}, u32[]{:S(2)}, u32[]{:S(2)}) %all-to-all-start.3) | async-done | bytes 1048608 | tf_op jit(solution)/shard_map/all_to_all | solution.py:172
  121.0 2.8 %multiply_convert_fusion = bf16[30,128,128]{2,0,1:T(8,128)(2,1)S(1)} fusion(f32[30,128,128]{2,1,0:T(8,128)S(1)} %bitcast.240, bf16[32,128,128]{2,0,1:T(8,128)(2,1)} %all-to-all-done.3), kind=kLoop, calls=%fused_computation.19 | loop fusion | flops 4915200 | bytes 3932160 | tf_op jit(solution)/shard_map/convert_element_type | solution.py:424
  130.9 4.4 %all-to-all-start.4 = ((f32[128,24,128]{2,1,0:T(8,128)}), f32[128,24,128]{2,1,0:T(8,128)S(1)}, u32[]{:S(2)}, u32[]{:S(2)}) async-start(f32[128,24,128]{2,1,0:T(8,128)} %bitcast.246), calls=%async_computation.4 | async-start | bytes 3145728 | tf_op jit(solution)/shard_map/all_to_all | solution.py:347
  138.7 3.2 %pad_slice_fusion = (bf16[1,32,120,128]{3,2,1,0:T(8,128)(2,1)}, bf16[1,32,120,128]{3,2,1,0:T(8,128)(2,1)S(1)}, bf16[1,32,120,128]{3,2,1,0:T(8,128)(2,1)S(1)}, bf...) fusion(bf16[1,32,120,128]{3,2,1,0:T(8,128)(2,1)S(1)} %multiply_, ...), kind=kLoop, calls=%fused_computation.63 | loop fusion | bytes 8847360 | tf_op jit(solution)/shard_map/slice | solution.py:51
  145.1 14.7 %all-to-all-done.4 = f32[128,24,128]{2,1,0:T(8,128)S(1)} async-done(((f32[128,24,128]{2,1,0:T(8,128)}), f32[128,24,128]{2,1,0:T(8,128)S(1)}, u32[]{:S(2)}, u32[]{:S(2)}) %all-to-all-start.4) | async-done | bytes 1572896 | tf_op jit(solution)/shard_map/all_to_all | solution.py:347
  161.0 4.4 %all-to-all-start.5 = ((bf16[128,24,128]{2,1,0:T(8,128)(2,1)}), bf16[128,24,128]{2,1,0:T(8,128)(2,1)S(1)}, u32[]{:S(2)}, u32[]{:S(2)}) async-start(bf16[128,24,128]{2,1,0:T(8,128)(2,1)} %broadcast_in_dim.8), calls=%async_computation.5 | async-start | bytes 1572864 | tf_op jit(solution)/shard_map/all_to_all | solution.py:350
  168.4 2.1 %fusion = bf16[3840,128]{1,0:T(8,128)(2,1)} fusion(f32[3840,128]{1,0:T(8,128)S(1)} %convolution_add_fusion.1, bf16[3840,128]{1,0:T(8,128)(2,1)S(1)} %bitcast.275, bf16[9,128,128]{2,1,0:T(8,128)(2,1)} %param.8), kind=kOutput, calls=%fused_computation.16 | convolution fusion | flops 126812160 | bytes 3964928 | tf_op jit(solution)/shard_map/dot_general | solution.py:54
  170.5 11.2 %all-to-all-done.5 = bf16[128,24,128]{2,1,0:T(8,128)(2,1)S(1)} async-done(((bf16[128,24,128]{2,1,0:T(8,128)(2,1)}), bf16[128,24,128]{2,1,0:T(8,128)(2,1)S(1)}, u32[]{:S(2)}, u32[]{:S(2)}) %all-to-all-start.5) | async-done | bytes 786464 | tf_op jit(solution)/shard_map/all_to_all | solution.py:350
  (92 shorter events, 38.9 us)
Async XLA Ops:
  0.6 7.1 %copy-start.7 = (bf16[9,128,128]{2,1,0:T(8,128)(2,1)S(1)}, bf16[9,128,128]{2,1,0:T(8,128)(2,1)}, u32[]{:S(2)}) copy-start(bf16[9,128,128]{2,1,0:T(8,128)(2,1)} %param.8) | copy-start | bytes 884740
  8.9 1.2 copy-start
  13.5 12.6 %copy-start.12 = (bf16[2,5,128,128]{3,2,1,0:T(8,128)(2,1)S(1)}, bf16[2,5,128,128]{3,2,1,0:T(8,128)(2,1)}, u32[]{:S(2)}) copy-start(bf16[2,5,128,128]{3,2,1,0:T(8,128)(2,1)} %param.9) | copy-start | bytes 983044
  14.6 30.5 %all-to-all-start = ((bf16[32,128,128]{2,0,1:T(8,128)(2,1)}), bf16[32,128,128]{2,0,1:T(8,128)(2,1)S(1)}, u32[]{:S(2)}, u32[]{:S(2)}) async-start(bf16[32,128,128]{2,0,1:T(8,128)(2,1)} %pad.16), calls=%async_computation | async-start | bytes 2097152 | tf_op jit(solution)/shard_map/all_to_all | solution.py:166
  45.1 3.5 %copy-start.9 = (bf16[32,128,128]{2,0,1:T(8,128)(2,1)}, bf16[32,128,128]{2,0,1:T(8,128)(2,1)S(1)}, u32[]{:S(2)}) copy-start(bf16[32,128,128]{2,0,1:T(8,128)(2,1)S(1)} %all-to-all-done) | copy-start | bytes 3145732
  47.3 5.6 %copy-start.15 = (s32[8]{0:T(128)S(1)}, s32[8]{0:T(128)}, u32[]{:S(2)}) copy-start(s32[8]{0:T(128)} %param.11) | copy-start | bytes 100
  47.3 5.7 %copy-start.14 = (s32[2]{0:T(128)S(1)}, s32[2]{0:T(128)}, u32[]{:S(2)}) copy-start(s32[2]{0:T(128)} %param.12) | copy-start | bytes 28
  48.5 23.4 %all-to-all-start.2 = ((bf16[32,128,128]{2,0,1:T(8,128)(2,1)}), bf16[32,128,128]{2,0,1:T(8,128)(2,1)S(1)}, u32[]{:S(2)}, u32[]{:S(2)}) async-start(bf16[32,128,128]{2,0,1:T(8,128)(2,1)} %pad.17.clone), calls=%async_computation.2 | async-start | bytes 2097152 | tf_op jit(solution)/shard_map/all_to_all | solution.py:166
  59.0 7.2 %copy-start.13 = (bf16[2,128,128]{2,1,0:T(8,128)(2,1)S(1)}, bf16[2,128,128]{2,1,0:T(8,128)(2,1)}, u32[]{:S(2)}) copy-start(bf16[2,128,128]{2,1,0:T(8,128)(2,1)} %param.10) | copy-start | bytes 196612
  64.4 1.9 %copy-start.2 = (bf16[128,32,128]{2,1,0:T(8,128)(2,1)S(1)}, bf16[128,32,128]{2,1,0:T(8,128)(2,1)}, u32[]{:S(2)}) copy-start(bf16[128,32,128]{2,1,0:T(8,128)(2,1)} %get-tuple-element.13) | copy-start | bytes 3145732
  71.9 24.7 %all-to-all-start.1 = ((bf16[32,128,128]{2,0,1:T(8,128)(2,1)}), bf16[32,128,128]{2,0,1:T(8,128)(2,1)}, u32[]{:S(2)}, u32[]{:S(2)}) async-start(bf16[32,128,128]{2,0,1:T(8,128)(2,1)} %bitcast.249), calls=%async_computation.1 | async-start | bytes 2097152 | tf_op jit(solution)/shard_map/all_to_all | solution.py:172
  78.2 1.6 copy-start.6
  96.6 24.4 %all-to-all-start.3 = ((bf16[32,128,128]{2,0,1:T(8,128)(2,1)}), bf16[32,128,128]{2,0,1:T(8,128)(2,1)}, u32[]{:S(2)}, u32[]{:S(2)}) async-start(bf16[32,128,128]{2,0,1:T(8,128)(2,1)} %bitcast.281), calls=%async_computation.3 | async-start | bytes 2097152 | tf_op jit(solution)/shard_map/all_to_all | solution.py:172
  113.0 1.2 copy-start.3
  114.2 1.0 copy-start.10
  114.2 1.1 copy-start.11
  123.8 1.2 copy-start.1
  130.9 29.0 %all-to-all-start.4 = ((f32[128,24,128]{2,1,0:T(8,128)}), f32[128,24,128]{2,1,0:T(8,128)S(1)}, u32[]{:S(2)}, u32[]{:S(2)}) async-start(f32[128,24,128]{2,1,0:T(8,128)} %bitcast.246), calls=%async_computation.4 | async-start | bytes 3145728 | tf_op jit(solution)/shard_map/all_to_all | solution.py:347
  138.7 3.2 %copy-start.8 = (bf16[9,128,128]{2,1,0:T(8,128)(2,1)S(1)}, bf16[9,128,128]{2,1,0:T(8,128)(2,1)}, u32[]{:S(2)}) copy-start(bf16[9,128,128]{2,1,0:T(8,128)(2,1)} %param.8) | copy-start | bytes 884740
  161.0 20.7 %all-to-all-start.5 = ((bf16[128,24,128]{2,1,0:T(8,128)(2,1)}), bf16[128,24,128]{2,1,0:T(8,128)(2,1)S(1)}, u32[]{:S(2)}, u32[]{:S(2)}) async-start(bf16[128,24,128]{2,1,0:T(8,128)(2,1)} %broadcast_in_dim.8), calls=%async_computation.5 | async-start | bytes 1572864 | tf_op jit(solution)/shard_map/all_to_all | solution.py:350
  165.4 1.7 copy-start.4
  167.1 1.3 copy-start.5

commit v11 on v9

--- a/solution.py
+++ b/solution.py
@@ -263,45 +263,46 @@
         )
 
 
-def twgrad_kernel(dil_ref, act_ref, grad_ref, tg_ref, pad_ref):
-    frames, width, chans = act_ref.shape
-    fill_halo(grad_ref, pad_ref)
-    step = dil_ref[0]
+def twgrad_kernel(dil_ref, act0_ref, act1_ref, grad0_ref, grad1_ref, tg_ref, pad_ref):
+    frames, width, chans = act0_ref.shape
     rows = FB * width
-    total = None
-    for block in range(frames // FB):
-        base = HALO + block * FB
-        stacked = jnp.concatenate(
-            [tap_rows(pad_ref, base - (tap - 2) * step, rows) for tap in range(5)], axis=1
-        )
-        flat_act = act_ref[block * FB : (block + 1) * FB].reshape(rows, chans)
-        part = lax.dot_general(
-            flat_act, stacked, (((0,), (0,)), ((), ())), preferred_element_type=jnp.float32
-        )
-        total = part if total is None else total + part
-    for tap in range(5):
-        tg_ref[tap] = total[:, tap * chans : (tap + 1) * chans]
-
-
-def temporal_wgrad_k(acts, grads, step_size):
-    frames, width, chans = acts.shape
-    full = pl.BlockSpec(acts.shape, lambda i, d: (0, 0, 0))
+    for layer, (act_ref, grad_ref) in enumerate(((act0_ref, grad0_ref), (act1_ref, grad1_ref))):
+        fill_halo(grad_ref, pad_ref)
+        step = dil_ref[layer]
+        total = None
+        for block in range(frames // FB):
+            base = HALO + block * FB
+            stacked = jnp.concatenate(
+                [tap_rows(pad_ref, base - (tap - 2) * step, rows) for tap in range(5)], axis=1
+            )
+            flat_act = act_ref[block * FB : (block + 1) * FB].reshape(rows, chans)
+            part = lax.dot_general(
+                flat_act, stacked, (((0,), (0,)), ((), ())), preferred_element_type=jnp.float32
+            )
+            total = part if total is None else total + part
+        for tap in range(5):
+            tg_ref[layer, tap] = total[:, tap * chans : (tap + 1) * chans]
+
+
+def temporal_wgrad_k(acts, grads, dilation):
+    frames, width, chans = acts[0].shape
+    full = pl.BlockSpec(acts[0].shape, lambda i, d: (0, 0, 0))
     return pl.pallas_call(
         twgrad_kernel,
         grid_spec=pltpu.PrefetchScalarGridSpec(
             num_scalar_prefetch=1,
             grid=(1,),
-            in_specs=[full, full],
-            out_specs=pl.BlockSpec((5, chans, chans), lambda i, d: (0, 0, 0)),
+            in_specs=[full, full, full, full],
+            out_specs=pl.BlockSpec((2, 5, chans, chans), lambda i, d: (0, 0, 0, 0)),
             scratch_shapes=[pltpu.VMEM((frames + 2 * HALO, width, chans), jnp.bfloat16)],
         ),
-        out_shape=jax.ShapeDtypeStruct((5, chans, chans), jnp.float32),
+        out_shape=jax.ShapeDtypeStruct((2, 5, chans, chans), jnp.float32),
         cost_estimate=pl.CostEstimate(
-            flops=2 * frames * width * chans * chans * 5,
+            flops=2 * 2 * frames * width * chans * chans * 5,
             transcendentals=0,
-            bytes_accessed=frames * width * chans * 4,
-        ),
-    )(step_size.reshape(1), acts, grads)
+            bytes_accessed=2 * frames * width * chans * 4,
+        ),
+    )(dilation, acts[0], acts[1], grads[0], grads[1])
 
 
 def temporal_backward_k(acts, grads, kernel, step_size, pre_below):
@@ -414,13 +415,12 @@
         )
     grad_act0 = grad_pre
     grad_time = fm_to_frames(grad_act0, used).reshape(frames_in.shape)
-    for layer in range(LAYERS):
-        tgrads[layer] = temporal_wgrad_k(acts[layer], layer_grads[layer], dilation[layer])
+    tgrad_all = temporal_wgrad_k(acts[:LAYERS], layer_grads, dilation)
     grad_spre = (grad_time.astype(jnp.float32) * silu_grad(pre_spatial)).astype(jnp.bfloat16)
     grad_frames = spatial_back(grad_spre, spatial_weight).astype(jnp.bfloat16)
     grad_spatial = spatial_wgrad(frames_in, grad_spre)
     scale = 1.0 / jnp.sqrt(jnp.float32(total_frames * pixels))
-    summed = all_sum((grad_spatial, jnp.stack(tgrads), grad_uniting), scale)
+    summed = all_sum((grad_spatial, tgrad_all, grad_uniting), scale)
     return (
         united.reshape(frames_in.shape),
         grad_frames,

time: 185 us -> 185 us (level)
  waiting for transfers between devices: 58.8 us -> 61.8 us
  Pallas kernels: 28.9 us -> 26.5 us
    all_to_all x2, waiting for transfers between devices: 10.2 us -> 13.1 us  [fm_to_frames(): lax.all_to_all(moved, ('seg', 'grp'), split_axis=1, concat_axis=1, tiled=...]
    pallas_call x2 -> x1, Pallas kernels: 8.02 us -> 5.71 us  [temporal_wgrad_k(): pl.pallas_call(twgrad_kernel, grid_spec=pltpu.PrefetchScalarGridSpec(num_...]
    unnamed x33 -> x31, local copies, waits for them, and re-layouts: 5.93 us -> 5.5 us
  transfers between devices with their start and end apart: 6 -> 6, of which waited for: 6 -> 6; matrix products, arithmetic and copies ran while one was open for 14% -> 14% of each run, Pallas kernels for 16% -> 14%
where the time goes in v11:
time: 185 us; the launch traced here: 184 us
  waiting for transfers between devices  61.8 us (33%)
  starting transfers between devices  36 us (19%)
  local copies, waits for them, and re-layouts  26.9 us (15%)
  Pallas kernels  26.5 us (14%)
  matrix products  20.3 us (11%)
  other arithmetic  11 us (6%)
    all_to_all x2, waiting for transfers between devices, fm_to_pixels(): lax.all_to_all(strided, ('seg', 'grp'), split_axis=1, concat_axis=1, tile...  22.8 us
    all_to_all x2, starting transfers between devices, fm_to_pixels(): lax.all_to_all(strided, ('seg', 'grp'), split_axis=1, concat_axis=1, tile...  15.9 us
    all_to_all x1, waiting for transfers between devices, all_sum(): lax.all_to_all(stack, ('seg', 'grp'), split_axis=0, concat_axis=0, tiled=...  14.7 us
    all_to_all x2, waiting for transfers between devices, fm_to_frames(): lax.all_to_all(moved, ('seg', 'grp'), split_axis=1, concat_axis=1, tiled=...  13.1 us
    all_to_all x2, starting transfers between devices, fm_to_frames(): lax.all_to_all(moved, ('seg', 'grp'), split_axis=1, concat_axis=1, tiled=...  11.3 us
    all_to_all x1, waiting for transfers between devices, all_sum(): lax.all_to_all(spread, ('seg', 'grp'), split_axis=0, concat_axis=0, tiled...  11.2 us
    pallas_call x2, Pallas kernels, temporal_backward_k(): pl.pallas_call(functools.partial(tbwd_kernel, with_pre), grid_spec=pltpu....  10.6 us
    pallas_call x2, Pallas kernels, temporal_forward_k(): pl.pallas_call(tfwd_kernel, grid_spec=pltpu.PrefetchScalarGridSpec(num_sc...  10.2 us
  transfers between devices with their start and end apart: 6, of which 6 were waited for; matrix products, arithmetic and copies ran while one was open for 14% of the time, Pallas kernels for 14%

profile of v11, /device:TPU:1, one launch (start us, length us, event | category | flops | bytes accessed | tf_op | source)
XLA Modules:
  0.0 183.7 jit_solution(2034253105499094932)
XLA Ops:
  0.6 6.9 %pad_slice_fusion.8 = (bf16[1,32,120,128]{3,2,1,0:T(8,128)(2,1)S(1)}, bf16[1,32,120,128]{3,2,1,0:T(8,128)(2,1)S(1)}, bf16[1,32,120,128]{3,2,1,0:T(8,128)(2,1)S(1...) fusion(bf16[1,32,120,128]{3,2,1,0:T(8,128)(2,1)} %param.7), kind=kLoop, calls=%fused_computation.70 | loop fusion | bytes 8847360 | tf_op jit(solution)/shard_map/slice | solution.py:36
  14.5 11.5 %all-to-all-start = ((bf16[32,128,128]{2,0,1:T(8,128)(2,1)}), bf16[32,128,128]{2,0,1:T(8,128)(2,1)S(1)}, u32[]{:S(2)}, u32[]{:S(2)}) async-start(bf16[32,128,128]{2,0,1:T(8,128)(2,1)} %pad.16), calls=%async_computation | async-start | bytes 2097152 | tf_op jit(solution)/shard_map/all_to_all | solution.py:166
  26.7 18.2 %all-to-all-done = bf16[32,128,128]{2,0,1:T(8,128)(2,1)S(1)} async-done(((bf16[32,128,128]{2,0,1:T(8,128)(2,1)}), bf16[32,128,128]{2,0,1:T(8,128)(2,1)S(1)}, u32[]{:S(2)}, u32[]{:S(2)}) %all-to-all-start) | async-done | bytes 1048608 | tf_op jit(solution)/shard_map/all_to_all | solution.py:166
  44.9 2.2 %copy.56 = bf16[30,128,128]{2,0,1:T(8,128)(2,1)S(1)} copy(bf16[30,128,128]{2,1,0:T(8,128)(2,1)} %bitcast.280) | data formatting | bytes 1966080
  48.4 4.4 %all-to-all-start.2 = ((bf16[32,128,128]{2,0,1:T(8,128)(2,1)}), bf16[32,128,128]{2,0,1:T(8,128)(2,1)S(1)}, u32[]{:S(2)}, u32[]{:S(2)}) async-start(bf16[32,128,128]{2,0,1:T(8,128)(2,1)} %pad.17.clone), calls=%async_computation.2 | async-start | bytes 2097152 | tf_op jit(solution)/shard_map/all_to_all | solution.py:166
  53.5 5.1 %shard_map.110 = (f32[128,32,128]{2,1,0:T(8,128)}, bf16[128,32,128]{2,1,0:T(8,128)(2,1)}) custom-call(s32[1]{0:T(128)} %get-tuple-element.37.dil_ref, bf16[128,32,128]{2,1,0:T(8,128)(2,1)} %bitcast.245, bf16[640,128]{1,0:T(8,128)(2,1)} %bitcast.283), custom_call_target="tpu_custom_call" | custom-call | flops 671088640 | bytes 4194304 | tf_op jit(solution)/shard_map/pallas_call | solution.py:207
  58.6 5.1 %shard_map.111 = (f32[128,32,128]{2,1,0:T(8,128)}, bf16[128,32,128]{2,1,0:T(8,128)(2,1)}) custom-call(s32[1]{0:T(128)} %get-tuple-element.38.dil_ref, bf16[128,32,128]{2,1,0:T(8,128)(2,1)} %get-tuple-element.12.act_ref.act1_ref, bf16[640,128]{1,0:T(8,128)(2,1)} %bitcast.285), custom_call_target="tpu_custom_call" | custom-call | flops 671088640 | bytes 4194304 | tf_op jit(solution)/shard_map/pallas_call | solution.py:207
  67.1 4.6 %all-to-all-done.2 = bf16[32,128,128]{2,0,1:T(8,128)(2,1)S(1)} async-done(((bf16[32,128,128]{2,0,1:T(8,128)(2,1)}), bf16[32,128,128]{2,0,1:T(8,128)(2,1)S(1)}, u32[]{:S(2)}, u32[]{:S(2)}) %all-to-all-start.2) | async-done | bytes 1048608 | tf_op jit(solution)/shard_map/all_to_all | solution.py:166
  71.7 5.6 %all-to-all-start.1 = ((bf16[32,128,128]{2,0,1:T(8,128)(2,1)}), bf16[32,128,128]{2,0,1:T(8,128)(2,1)}, u32[]{:S(2)}, u32[]{:S(2)}) async-start(bf16[32,128,128]{2,0,1:T(8,128)(2,1)} %bitcast.251), calls=%async_computation.1 | async-start | bytes 2097152 | tf_op jit(solution)/shard_map/all_to_all | solution.py:172
  79.1 1.8 fusion.1.grad_ref.grad1_ref
  80.9 5.8 %shard_map.112.grad_ref.grad0_ref = bf16[128,32,128]{2,1,0:T(8,128)(2,1)} custom-call(s32[1]{0:T(128)} %get-tuple-element.38.dil_ref, bf16[128,32,128]{2,1,0:T(8,128)(2,1)} %get-tuple-element.12.act_ref.act1_ref, bf16[128,32,128]{2,1,0:T(8,128)(2,1)} %fusion.1.grad_ref.grad1_ref, bf16[640,128]{1,0:T(8,128)(2,1)} %bitcast.286, ...), custom_call_target="tpu_custom_call" | custom-call | flops 671088640 | bytes 5242880 | tf_op jit(solution)/shard_map/pallas_call | solution.py:317
  86.7 4.8 %shard_map.113 = bf16[128,32,128]{2,1,0:T(8,128)(2,1)} custom-call(s32[1]{0:T(128)} %get-tuple-element.37.dil_ref, bf16[128,32,128]{2,1,0:T(8,128)(2,1)} %bitcast.246, bf16[128,32,128]{2,1,0:T(8,128)(2,1)} %shard_map.112.grad_ref.grad0_ref, bf16[640,128]{1,0:T(8,128)(2,1)} %bitcast.284), custom_call_target="tpu_custom_call" | custom-call | flops 671088640 | bytes 5242880 | tf_op jit(solution)/shard_map/pallas_call | solution.py:317
  91.4 4.5 %all-to-all-done.1 = bf16[32,128,128]{2,0,1:T(8,128)(2,1)} async-done(((bf16[32,128,128]{2,0,1:T(8,128)(2,1)}), bf16[32,128,128]{2,0,1:T(8,128)(2,1)}, u32[]{:S(2)}, u32[]{:S(2)}) %all-to-all-start.1) | async-done | bytes 1048608 | tf_op jit(solution)/shard_map/all_to_all | solution.py:172
  96.0 5.7 %all-to-all-start.3 = ((bf16[32,128,128]{2,0,1:T(8,128)(2,1)}), bf16[32,128,128]{2,0,1:T(8,128)(2,1)}, u32[]{:S(2)}, u32[]{:S(2)}) async-start(bf16[32,128,128]{2,0,1:T(8,128)(2,1)} %bitcast.250), calls=%async_computation.3 | async-start | bytes 2097152 | tf_op jit(solution)/shard_map/all_to_all | solution.py:172
  101.7 2.6 %copy.44 = bf16[30,128,128]{2,1,0:T(8,128)(2,1)} copy(bf16[30,128,128]{2,0,1:T(8,128)(2,1)} %bitcast.236) | data formatting | bytes 1966080 | tf_op jit(solution)/shard_map/slice | solution.py:173
  106.0 5.7 %shard_map.114 = f32[2,5,128,128]{3,2,1,0:T(8,128)} custom-call(s32[2]{0:T(128)} %dil_ref.1, bf16[128,32,128]{2,1,0:T(8,128)(2,1)} %bitcast.247, bf16[128,32,128]{2,1,0:T(8,128)(2,1)} %get-tuple-element.12.act_ref.act1_ref, bf16[128,32,128]{2,1,0:T(8,128)(2,1)} %shard_map.112.grad_ref.grad0_ref, bf16[128,32,128]{2,1,0:T(8,128)(2,1)} %fusion.1.grad_ref.grad1_ref), custom_call_target="tpu_custom_call" | custom-call | flops 1342177280 | bytes 4194304 | tf_op jit(solution)/shard_map/pallas_call | solution.py:290
  111.7 8.6 %all-to-all-done.3 = bf16[32,128,128]{2,0,1:T(8,128)(2,1)} async-done(((bf16[32,128,128]{2,0,1:T(8,128)(2,1)}), bf16[32,128,128]{2,0,1:T(8,128)(2,1)}, u32[]{:S(2)}, u32[]{:S(2)}) %all-to-all-start.3) | async-done | bytes 1048608 | tf_op jit(solution)/shard_map/all_to_all | solution.py:172
  120.3 2.8 %multiply_convert_fusion = bf16[30,128,128]{2,0,1:T(8,128)(2,1)S(1)} fusion(f32[30,128,128]{2,1,0:T(8,128)S(1)} %bitcast.238, bf16[32,128,128]{2,0,1:T(8,128)(2,1)} %all-to-all-done.3), kind=kLoop, calls=%fused_computation.19 | loop fusion | flops 4915200 | bytes 3932160 | tf_op jit(solution)/shard_map/convert_element_type | solution.py:419
  130.3 4.4 %all-to-all-start.4 = ((f32[128,24,128]{2,1,0:T(8,128)}), f32[128,24,128]{2,1,0:T(8,128)S(1)}, u32[]{:S(2)}, u32[]{:S(2)}) async-start(f32[128,24,128]{2,1,0:T(8,128)} %bitcast.244), calls=%async_computation.4 | async-start | bytes 3145728 | tf_op jit(solution)/shard_map/all_to_all | solution.py:343
  138.1 3.2 %pad_slice_fusion = (bf16[1,32,120,128]{3,2,1,0:T(8,128)(2,1)}, bf16[1,32,120,128]{3,2,1,0:T(8,128)(2,1)S(1)}, bf16[1,32,120,128]{3,2,1,0:T(8,128)(2,1)S(1)}, bf...) fusion(bf16[1,32,120,128]{3,2,1,0:T(8,128)(2,1)S(1)} %multiply_, ...), kind=kLoop, calls=%fused_computation.62 | loop fusion | bytes 8847360 | tf_op jit(solution)/shard_map/slice | solution.py:51
  144.6 14.7 %all-to-all-done.4 = f32[128,24,128]{2,1,0:T(8,128)S(1)} async-done(((f32[128,24,128]{2,1,0:T(8,128)}), f32[128,24,128]{2,1,0:T(8,128)S(1)}, u32[]{:S(2)}, u32[]{:S(2)}) %all-to-all-start.4) | async-done | bytes 1572896 | tf_op jit(solution)/shard_map/all_to_all | solution.py:343
  160.4 4.4 %all-to-all-start.5 = ((bf16[128,24,128]{2,1,0:T(8,128)(2,1)}), bf16[128,24,128]{2,1,0:T(8,128)(2,1)S(1)}, u32[]{:S(2)}, u32[]{:S(2)}) async-start(bf16[128,24,128]{2,1,0:T(8,128)(2,1)} %broadcast_in_dim.8), calls=%async_computation.5 | async-start | bytes 1572864 | tf_op jit(solution)/shard_map/all_to_all | solution.py:346
  167.8 2.1 %fusion = bf16[3840,128]{1,0:T(8,128)(2,1)} fusion(f32[3840,128]{1,0:T(8,128)S(1)} %convolution_add_fusion.1, bf16[3840,128]{1,0:T(8,128)(2,1)S(1)} %bitcast.277, bf16[9,128,128]{2,1,0:T(8,128)(2,1)} %param.8), kind=kOutput, calls=%fused_computation.16 | convolution fusion | flops 126812160 | bytes 3964928 | tf_op jit(solution)/shard_map/dot_general | solution.py:54
  170.0 11.2 %all-to-all-done.5 = bf16[128,24,128]{2,1,0:T(8,128)(2,1)S(1)} async-done(((bf16[128,24,128]{2,1,0:T(8,128)(2,1)}), bf16[128,24,128]{2,1,0:T(8,128)(2,1)S(1)}, u32[]{:S(2)}, u32[]{:S(2)}) %all-to-all-start.5) | async-done | bytes 786464 | tf_op jit(solution)/shard_map/all_to_all | solution.py:346
  (88 shorter events, 36.7 us)
Async XLA Ops:
  0.6 6.9 %copy-start.8 = (bf16[9,128,128]{2,1,0:T(8,128)(2,1)S(1)}, bf16[9,128,128]{2,1,0:T(8,128)(2,1)}, u32[]{:S(2)}) copy-start(bf16[9,128,128]{2,1,0:T(8,128)(2,1)} %param.8) | copy-start | bytes 884740
  8.8 1.2 copy-start
  13.3 12.7 %copy-start.11 = (bf16[2,5,128,128]{3,2,1,0:T(8,128)(2,1)S(1)}, bf16[2,5,128,128]{3,2,1,0:T(8,128)(2,1)}, u32[]{:S(2)}) copy-start(bf16[2,5,128,128]{3,2,1,0:T(8,128)(2,1)} %param.9) | copy-start | bytes 983044
  14.5 30.5 %all-to-all-start = ((bf16[32,128,128]{2,0,1:T(8,128)(2,1)}), bf16[32,128,128]{2,0,1:T(8,128)(2,1)S(1)}, u32[]{:S(2)}, u32[]{:S(2)}) async-start(bf16[32,128,128]{2,0,1:T(8,128)(2,1)} %pad.16), calls=%async_computation | async-start | bytes 2097152 | tf_op jit(solution)/shard_map/all_to_all | solution.py:166
  44.9 3.5 %copy-start.2 = (bf16[32,128,128]{2,0,1:T(8,128)(2,1)}, bf16[32,128,128]{2,0,1:T(8,128)(2,1)S(1)}, u32[]{:S(2)}) copy-start(bf16[32,128,128]{2,0,1:T(8,128)(2,1)S(1)} %all-to-all-done) | copy-start | bytes 3145732
  47.2 5.6 %copy-start.14 = (s32[8]{0:T(128)S(1)}, s32[8]{0:T(128)}, u32[]{:S(2)}) copy-start(s32[8]{0:T(128)} %param.11) | copy-start | bytes 100
  47.2 5.7 %copy-start.13 = (s32[2]{0:T(128)S(1)}, s32[2]{0:T(128)}, u32[]{:S(2)}) copy-start(s32[2]{0:T(128)} %dil_ref.1) | copy-start | bytes 28
  48.4 23.4 %all-to-all-start.2 = ((bf16[32,128,128]{2,0,1:T(8,128)(2,1)}), bf16[32,128,128]{2,0,1:T(8,128)(2,1)S(1)}, u32[]{:S(2)}, u32[]{:S(2)}) async-start(bf16[32,128,128]{2,0,1:T(8,128)(2,1)} %pad.17.clone), calls=%async_computation.2 | async-start | bytes 2097152 | tf_op jit(solution)/shard_map/all_to_all | solution.py:166
  58.6 6.9 %copy-start.12 = (bf16[2,128,128]{2,1,0:T(8,128)(2,1)S(1)}, bf16[2,128,128]{2,1,0:T(8,128)(2,1)}, u32[]{:S(2)}) copy-start(bf16[2,128,128]{2,1,0:T(8,128)(2,1)} %param.10) | copy-start | bytes 196612
  63.7 1.9 %copy-start.3 = (bf16[128,32,128]{2,1,0:T(8,128)(2,1)S(1)}, bf16[128,32,128]{2,1,0:T(8,128)(2,1)}, u32[]{:S(2)}) copy-start(bf16[128,32,128]{2,1,0:T(8,128)(2,1)} %get-tuple-element.13) | copy-start | bytes 3145732
  71.7 24.2 %all-to-all-start.1 = ((bf16[32,128,128]{2,0,1:T(8,128)(2,1)}), bf16[32,128,128]{2,0,1:T(8,128)(2,1)}, u32[]{:S(2)}, u32[]{:S(2)}) async-start(bf16[32,128,128]{2,0,1:T(8,128)(2,1)} %bitcast.251), calls=%async_computation.1 | async-start | bytes 2097152 | tf_op jit(solution)/shard_map/all_to_all | solution.py:172
  77.5 1.6 copy-start.7
  96.0 24.3 %all-to-all-start.3 = ((bf16[32,128,128]{2,0,1:T(8,128)(2,1)}), bf16[32,128,128]{2,0,1:T(8,128)(2,1)}, u32[]{:S(2)}, u32[]{:S(2)}) async-start(bf16[32,128,128]{2,0,1:T(8,128)(2,1)} %bitcast.250), calls=%async_computation.3 | async-start | bytes 2097152 | tf_op jit(solution)/shard_map/all_to_all | solution.py:172
  104.3 1.2 copy-start.4
  123.1 1.2 copy-start.1
  127.5 1.1 copy-start.10
  130.3 29.0 %all-to-all-start.4 = ((f32[128,24,128]{2,1,0:T(8,128)}), f32[128,24,128]{2,1,0:T(8,128)S(1)}, u32[]{:S(2)}, u32[]{:S(2)}) async-start(f32[128,24,128]{2,1,0:T(8,128)} %bitcast.244), calls=%async_computation.4 | async-start | bytes 3145728 | tf_op jit(solution)/shard_map/all_to_all | solution.py:343
  138.1 3.2 %copy-start.9 = (bf16[9,128,128]{2,1,0:T(8,128)(2,1)S(1)}, bf16[9,128,128]{2,1,0:T(8,128)(2,1)}, u32[]{:S(2)}) copy-start(bf16[9,128,128]{2,1,0:T(8,128)(2,1)} %param.8) | copy-start | bytes 884740
  160.4 20.7 %all-to-all-start.5 = ((bf16[128,24,128]{2,1,0:T(8,128)(2,1)}), bf16[128,24,128]{2,1,0:T(8,128)(2,1)S(1)}, u32[]{:S(2)}, u32[]{:S(2)}) async-start(bf16[128,24,128]{2,1,0:T(8,128)(2,1)} %broadcast_in_dim.8), calls=%async_computation.5 | async-start | bytes 1572864 | tf_op jit(solution)/shard_map/all_to_all | solution.py:346
  164.8 1.7 copy-start.5
  166.5 1.3 copy-start.6

commit v12 on v9

--- a/solution.py
+++ b/solution.py
@@ -365,7 +365,10 @@
     act_zero = jax.nn.silu(pre_spatial).astype(jnp.bfloat16).reshape(local_frames, pixels, chans)
     cot_local = cotangent.reshape(local_frames, pixels, chans)
     act_blocks = fm_to_pixels(act_zero)
-    act_blocks, cot_local = lax.optimization_barrier((act_blocks, cot_local))
+    spatial_slope = silu_grad(pre_spatial)
+    act_blocks, cot_local, spatial_slope = lax.optimization_barrier(
+        (act_blocks, cot_local, spatial_slope)
+    )
     cot_blocks = fm_to_pixels(cot_local)
     acts = [act_blocks]
     total_frames, width = act_blocks.shape[0], act_blocks.shape[1]
@@ -416,7 +419,7 @@
     grad_time = fm_to_frames(grad_act0, used).reshape(frames_in.shape)
     for layer in range(LAYERS):
         tgrads[layer] = temporal_wgrad_k(acts[layer], layer_grads[layer], dilation[layer])
-    grad_spre = (grad_time.astype(jnp.float32) * silu_grad(pre_spatial)).astype(jnp.bfloat16)
+    grad_spre = (grad_time.astype(jnp.float32) * spatial_slope).astype(jnp.bfloat16)
     grad_frames = spatial_back(grad_spre, spatial_weight).astype(jnp.bfloat16)
     grad_spatial = spatial_wgrad(frames_in, grad_spre)
     scale = 1.0 / jnp.sqrt(jnp.float32(total_frames * pixels))

time: 185 us -> 188 us (1.016)
    all_to_all x1, waiting for transfers between devices: 14.7 us -> 19.2 us  [all_sum(): lax.all_to_all(stack, ('seg', 'grp'), split_axis=0, concat_axis=0, tiled=...]
    convert_element_type x4 -> x2, other arithmetic: 5.74 us -> 1.69 us  [the longest x1 1.5 us: local(): grad_time.astype(jnp.float32) * spatial_slope]
    all_to_all x2, waiting for transfers between devices: 22.8 us -> 20.4 us  [fm_to_pixels(): lax.all_to_all(strided, ('seg', 'grp'), split_axis=1, concat_axis=1, tile...]
    mul x0 -> x1, other arithmetic: none -> 1.95 us  [silu_grad(): return sigma * (1.0 + value * (1.0 - sigma))]
    unnamed x33 -> x39, local copies, waits for them, and re-layouts: 5.93 us -> 6.83 us
  transfers between devices with their start and end apart: 6 -> 6, of which waited for: 6 -> 6; matrix products, arithmetic and copies ran while one was open for 14% -> 12% of each run, Pallas kernels for 16% -> 16%
where the time goes in v12:
time: 188 us; the launch traced here: 187 us
  waiting for transfers between devices  60 us (32%)
  starting transfers between devices  37.2 us (20%)
  Pallas kernels  29.1 us (15%)
  local copies, waits for them, and re-layouts  27.8 us (15%)
  matrix products  21.5 us (11%)
  other arithmetic  9.81 us (5%)
    all_to_all x2, waiting for transfers between devices, fm_to_pixels(): lax.all_to_all(strided, ('seg', 'grp'), split_axis=1, concat_axis=1, tile...  20.4 us
    all_to_all x1, waiting for transfers between devices, all_sum(): lax.all_to_all(stack, ('seg', 'grp'), split_axis=0, concat_axis=0, tiled=...  19.2 us
    all_to_all x2, starting transfers between devices, fm_to_pixels(): lax.all_to_all(strided, ('seg', 'grp'), split_axis=1, concat_axis=1, tile...  16.3 us
    all_to_all x2, starting transfers between devices, fm_to_frames(): lax.all_to_all(moved, ('seg', 'grp'), split_axis=1, concat_axis=1, tiled=...  11.5 us
    all_to_all x1, waiting for transfers between devices, all_sum(): lax.all_to_all(spread, ('seg', 'grp'), split_axis=0, concat_axis=0, tiled...  11.2 us
    pallas_call x2, Pallas kernels, temporal_backward_k(): pl.pallas_call(functools.partial(tbwd_kernel, with_pre), grid_spec=pltpu....  10.6 us
    pallas_call x2, Pallas kernels, temporal_forward_k(): pl.pallas_call(tfwd_kernel, grid_spec=pltpu.PrefetchScalarGridSpec(num_sc...  10.5 us
    all_to_all x2, waiting for transfers between devices, fm_to_frames(): lax.all_to_all(moved, ('seg', 'grp'), split_axis=1, concat_axis=1, tiled=...  9.34 us
  transfers between devices with their start and end apart: 6, of which 6 were waited for; matrix products, arithmetic and copies ran while one was open for 12% of the time, Pallas kernels for 16%

profile of v12, /device:TPU:1, one launch (start us, length us, event | category | flops | bytes accessed | tf_op | source)
XLA Modules:
  0.0 186.5 jit_solution(9096897961165034668)
XLA Ops:
  0.6 6.6 %pad_slice_fusion.8 = (bf16[1,32,120,128]{3,2,1,0:T(8,128)(2,1)S(1)}, bf16[1,32,120,128]{3,2,1,0:T(8,128)(2,1)S(1)}, bf16[1,32,120,128]{3,2,1,0:T(8,128)(2,1)S(1...) fusion(bf16[1,32,120,128]{3,2,1,0:T(8,128)(2,1)} %param.7), kind=kLoop, calls=%fused_computation.77 | loop fusion | bytes 8847360 | tf_op jit(solution)/shard_map/slice | solution.py:36
  14.2 11.9 %all-to-all-start = ((bf16[32,128,128]{2,0,1:T(8,128)(2,1)}), bf16[32,128,128]{2,0,1:T(8,128)(2,1)}, u32[]{:S(2)}, u32[]{:S(2)}) async-start(bf16[32,128,128]{2,0,1:T(8,128)(2,1)} %pad.16), calls=%async_computation | async-start | bytes 2097152 | tf_op jit(solution)/shard_map/all_to_all | solution.py:166
  26.9 1.9 %add_multiply_fusion = f32[1,32,120,128]{3,2,1,0:T(8,128)} fusion(f32[1,32,120,128]{3,2,1,0:T(8,128)S(1)} %bitcast.246), kind=kLoop, calls=%fused_computation.24 | loop fusion | flops 3440640 | bytes 3932160 | tf_op jit(solution)/shard_map/mul | solution.py:21
  28.8 15.9 %all-to-all-done = bf16[32,128,128]{2,0,1:T(8,128)(2,1)} async-done(((bf16[32,128,128]{2,0,1:T(8,128)(2,1)}), bf16[32,128,128]{2,0,1:T(8,128)(2,1)}, u32[]{:S(2)}, u32[]{:S(2)}) %all-to-all-start) | async-done | bytes 1048608 | tf_op jit(solution)/shard_map/all_to_all | solution.py:166
  44.7 1.8 copy.42
  47.7 4.4 %all-to-all-start.2 = ((bf16[32,128,128]{2,0,1:T(8,128)(2,1)}), bf16[32,128,128]{2,0,1:T(8,128)(2,1)S(1)}, u32[]{:S(2)}, u32[]{:S(2)}) async-start(bf16[32,128,128]{2,0,1:T(8,128)(2,1)} %pad.17.clone), calls=%async_computation.2 | async-start | bytes 2097152 | tf_op jit(solution)/shard_map/all_to_all | solution.py:166
  52.8 5.2 %shard_map.110 = (f32[128,32,128]{2,1,0:T(8,128)}, bf16[128,32,128]{2,1,0:T(8,128)(2,1)}) custom-call(s32[1]{0:T(128)} %get-tuple-element.39.dil_ref, bf16[128,32,128]{2,1,0:T(8,128)(2,1)} %bitcast.19.act_ref, bf16[640,128]{1,0:T(8,128)(2,1)} %bitcast.280), custom_call_target="tpu_custom_call" | custom-call | flops 671088640 | bytes 4194304 | tf_op jit(solution)/shard_map/pallas_call | solution.py:207
  58.0 5.3 %shard_map.111 = (f32[128,32,128]{2,1,0:T(8,128)}, bf16[128,32,128]{2,1,0:T(8,128)(2,1)}) custom-call(s32[1]{0:T(128)} %get-tuple-element.40.dil_ref, bf16[128,32,128]{2,1,0:T(8,128)(2,1)} %get-tuple-element.13.act_ref, bf16[640,128]{1,0:T(8,128)(2,1)} %bitcast.282), custom_call_target="tpu_custom_call" | custom-call | flops 671088640 | bytes 4194304 | tf_op jit(solution)/shard_map/pallas_call | solution.py:207
  66.6 4.5 %all-to-all-done.2 = bf16[32,128,128]{2,0,1:T(8,128)(2,1)S(1)} async-done(((bf16[32,128,128]{2,0,1:T(8,128)(2,1)}), bf16[32,128,128]{2,0,1:T(8,128)(2,1)S(1)}, u32[]{:S(2)}, u32[]{:S(2)}) %all-to-all-start.2) | async-done | bytes 1048608 | tf_op jit(solution)/shard_map/all_to_all | solution.py:166
  71.1 5.8 %all-to-all-start.1 = ((bf16[32,128,128]{2,0,1:T(8,128)(2,1)}), bf16[32,128,128]{2,0,1:T(8,128)(2,1)}, u32[]{:S(2)}, u32[]{:S(2)}) async-start(bf16[32,128,128]{2,0,1:T(8,128)(2,1)} %bitcast.256), calls=%async_computation.1 | async-start | bytes 2097152 | tf_op jit(solution)/shard_map/all_to_all | solution.py:172
  80.4 5.8 %shard_map.112.grad_ref = bf16[128,32,128]{2,1,0:T(8,128)(2,1)} custom-call(s32[1]{0:T(128)} %get-tuple-element.40.dil_ref, bf16[128,32,128]{2,1,0:T(8,128)(2,1)} %get-tuple-element.13.act_ref, bf16[128,32,128]{2,1,0:T(8,128)(2,1)} %fusion.1.grad_ref, bf16[640,128]{1,0:T(8,128)(2,1)} %bitcast.283, f32[128,32,128]{2,1,0:T(8,128)} %get-tuple-element.17.rest_0_), custom_call_target="tpu_custom_call" | custom-call | flops 671088640 | bytes 5242880 | tf_op jit(solution)/shard_map/pallas_call | solution.py:316
  86.2 4.8 %shard_map.113 = bf16[128,32,128]{2,1,0:T(8,128)(2,1)} custom-call(s32[1]{0:T(128)} %get-tuple-element.39.dil_ref, bf16[128,32,128]{2,1,0:T(8,128)(2,1)} %bitcast.19.act_ref, bf16[128,32,128]{2,1,0:T(8,128)(2,1)} %shard_map.112.grad_ref, bf16[640,128]{1,0:T(8,128)(2,1)} %bitcast.281), custom_call_target="tpu_custom_call" | custom-call | flops 671088640 | bytes 5242880 | tf_op jit(solution)/shard_map/pallas_call | solution.py:316
  90.9 4.5 %all-to-all-done.1 = bf16[32,128,128]{2,0,1:T(8,128)(2,1)} async-done(((bf16[32,128,128]{2,0,1:T(8,128)(2,1)}), bf16[32,128,128]{2,0,1:T(8,128)(2,1)}, u32[]{:S(2)}, u32[]{:S(2)}) %all-to-all-start.1) | async-done | bytes 1048608 | tf_op jit(solution)/shard_map/all_to_all | solution.py:172
  95.5 5.7 %all-to-all-start.3 = ((bf16[32,128,128]{2,0,1:T(8,128)(2,1)}), bf16[32,128,128]{2,0,1:T(8,128)(2,1)}, u32[]{:S(2)}, u32[]{:S(2)}) async-start(bf16[32,128,128]{2,0,1:T(8,128)(2,1)} %bitcast.255), calls=%async_computation.3 | async-start | bytes 2097152 | tf_op jit(solution)/shard_map/all_to_all | solution.py:172
  101.2 2.6 %copy.35 = bf16[30,128,128]{2,1,0:T(8,128)(2,1)} copy(bf16[30,128,128]{2,0,1:T(8,128)(2,1)} %bitcast.244) | data formatting | bytes 1966080 | tf_op jit(solution)/shard_map/slice | solution.py:173
  103.8 4.0 %shard_map.115 = f32[5,128,128]{2,1,0:T(8,128)} custom-call(s32[1]{0:T(128)} %get-tuple-element.40.dil_ref, bf16[128,32,128]{2,1,0:T(8,128)(2,1)} %get-tuple-element.13.act_ref, bf16[128,32,128]{2,1,0:T(8,128)(2,1)} %fusion.1.grad_ref), custom_call_target="tpu_custom_call" | custom-call | flops 671088640 | bytes 2097152 | tf_op jit(solution)/shard_map/pallas_call | solution.py:289
  107.8 4.0 %shard_map.114 = f32[5,128,128]{2,1,0:T(8,128)} custom-call(s32[1]{0:T(128)} %get-tuple-element.39.dil_ref, bf16[128,32,128]{2,1,0:T(8,128)(2,1)} %bitcast.19.act_ref, bf16[128,32,128]{2,1,0:T(8,128)(2,1)} %shard_map.112.grad_ref), custom_call_target="tpu_custom_call" | custom-call | flops 671088640 | bytes 2097152 | tf_op jit(solution)/shard_map/pallas_call | solution.py:289
  115.0 4.8 %all-to-all-done.3 = bf16[32,128,128]{2,0,1:T(8,128)(2,1)} async-done(((bf16[32,128,128]{2,0,1:T(8,128)(2,1)}), bf16[32,128,128]{2,0,1:T(8,128)(2,1)}, u32[]{:S(2)}, u32[]{:S(2)}) %all-to-all-start.3) | async-done | bytes 1048608 | tf_op jit(solution)/shard_map/all_to_all | solution.py:172
  123.5 3.5 %pad_slice_fusion = (bf16[1,32,120,128]{3,2,1,0:T(8,128)(2,1)}, bf16[1,32,120,128]{3,2,1,0:T(8,128)(2,1)}, bf16[1,32,120,128]{3,2,1,0:T(8,128)(2,1)}, bf16[1,32,...) fusion(bf16[1,32,120,128]{3,2,1,0:T(8,128)(2,1)S(1)} %multiply_, ...), kind=kLoop, calls=%fused_computation.69 | loop fusion | bytes 8847360 | tf_op jit(solution)/shard_map/slice | solution.py:51
  132.6 5.0 %all-to-all-start.4 = ((f32[128,24,128]{2,1,0:T(8,128)}), f32[128,24,128]{2,1,0:T(8,128)S(1)}, u32[]{:S(2)}, u32[]{:S(2)}) async-start(f32[128,24,128]{2,1,0:T(8,128)} %bitcast.252), calls=%async_computation.4 | async-start | bytes 3145728 | tf_op jit(solution)/shard_map/all_to_all | solution.py:342
  143.0 19.2 %all-to-all-done.4 = f32[128,24,128]{2,1,0:T(8,128)S(1)} async-done(((f32[128,24,128]{2,1,0:T(8,128)}), f32[128,24,128]{2,1,0:T(8,128)S(1)}, u32[]{:S(2)}, u32[]{:S(2)}) %all-to-all-start.4) | async-done | bytes 1572896 | tf_op jit(solution)/shard_map/all_to_all | solution.py:342
  163.3 4.4 %all-to-all-start.5 = ((bf16[128,24,128]{2,1,0:T(8,128)(2,1)}), bf16[128,24,128]{2,1,0:T(8,128)(2,1)S(1)}, u32[]{:S(2)}, u32[]{:S(2)}) async-start(bf16[128,24,128]{2,1,0:T(8,128)(2,1)} %broadcast_in_dim.8), calls=%async_computation.5 | async-start | bytes 1572864 | tf_op jit(solution)/shard_map/all_to_all | solution.py:345
  170.7 2.1 %fusion = bf16[3840,128]{1,0:T(8,128)(2,1)} fusion(f32[3840,128]{1,0:T(8,128)S(1)} %convolution_add_fusion.1, bf16[3840,128]{1,0:T(8,128)(2,1)S(1)} %bitcast.273, bf16[9,128,128]{2,1,0:T(8,128)(2,1)} %param.8), kind=kOutput, calls=%fused_computation.16 | convolution fusion | flops 126812160 | bytes 3964928 | tf_op jit(solution)/shard_map/dot_general | solution.py:54
  172.8 11.2 %all-to-all-done.5 = bf16[128,24,128]{2,1,0:T(8,128)(2,1)S(1)} async-done(((bf16[128,24,128]{2,1,0:T(8,128)(2,1)}), bf16[128,24,128]{2,1,0:T(8,128)(2,1)S(1)}, u32[]{:S(2)}, u32[]{:S(2)}) %all-to-all-start.5) | async-done | bytes 786464 | tf_op jit(solution)/shard_map/all_to_all | solution.py:345
  (96 shorter events, 40.5 us)
Async XLA Ops:
  0.6 6.6 %copy-start.11 = (bf16[9,128,128]{2,1,0:T(8,128)(2,1)S(1)}, bf16[9,128,128]{2,1,0:T(8,128)(2,1)}, u32[]{:S(2)}) copy-start(bf16[9,128,128]{2,1,0:T(8,128)(2,1)} %param.8) | copy-start | bytes 884740
  8.5 1.2 copy-start
  13.0 13.1 %copy-start.15 = (bf16[2,5,128,128]{3,2,1,0:T(8,128)(2,1)S(1)}, bf16[2,5,128,128]{3,2,1,0:T(8,128)(2,1)}, u32[]{:S(2)}) copy-start(bf16[2,5,128,128]{3,2,1,0:T(8,128)(2,1)} %param.9) | copy-start | bytes 983044
  14.2 30.6 %all-to-all-start = ((bf16[32,128,128]{2,0,1:T(8,128)(2,1)}), bf16[32,128,128]{2,0,1:T(8,128)(2,1)}, u32[]{:S(2)}, u32[]{:S(2)}) async-start(bf16[32,128,128]{2,0,1:T(8,128)(2,1)} %pad.16), calls=%async_computation | async-start | bytes 2097152 | tf_op jit(solution)/shard_map/all_to_all | solution.py:166
  46.6 5.6 %copy-start.18 = (s32[8]{0:T(128)S(1)}, s32[8]{0:T(128)}, u32[]{:S(2)}) copy-start(s32[8]{0:T(128)} %param.11) | copy-start | bytes 100
  46.6 5.6 %copy-start.17 = (s32[2]{0:T(128)S(1)}, s32[2]{0:T(128)}, u32[]{:S(2)}) copy-start(s32[2]{0:T(128)} %param.12) | copy-start | bytes 28
  47.7 23.4 %all-to-all-start.2 = ((bf16[32,128,128]{2,0,1:T(8,128)(2,1)}), bf16[32,128,128]{2,0,1:T(8,128)(2,1)S(1)}, u32[]{:S(2)}, u32[]{:S(2)}) async-start(bf16[32,128,128]{2,0,1:T(8,128)(2,1)} %pad.17.clone), calls=%async_computation.2 | async-start | bytes 2097152 | tf_op jit(solution)/shard_map/all_to_all | solution.py:166
  58.0 7.0 %copy-start.16 = (bf16[2,128,128]{2,1,0:T(8,128)(2,1)S(1)}, bf16[2,128,128]{2,1,0:T(8,128)(2,1)}, u32[]{:S(2)}) copy-start(bf16[2,128,128]{2,1,0:T(8,128)(2,1)} %param.10) | copy-start | bytes 196612
  63.3 1.9 %copy-start.2 = (bf16[128,32,128]{2,1,0:T(8,128)(2,1)S(1)}, bf16[128,32,128]{2,1,0:T(8,128)(2,1)}, u32[]{:S(2)}) copy-start(bf16[128,32,128]{2,1,0:T(8,128)(2,1)} %get-tuple-element.14) | copy-start | bytes 3145732
  71.1 24.4 %all-to-all-start.1 = ((bf16[32,128,128]{2,0,1:T(8,128)(2,1)}), bf16[32,128,128]{2,0,1:T(8,128)(2,1)}, u32[]{:S(2)}, u32[]{:S(2)}) async-start(bf16[32,128,128]{2,0,1:T(8,128)(2,1)} %bitcast.256), calls=%async_computation.1 | async-start | bytes 2097152 | tf_op jit(solution)/shard_map/all_to_all | solution.py:172
  77.0 1.6 copy-start.10
  95.5 24.3 %all-to-all-start.3 = ((bf16[32,128,128]{2,0,1:T(8,128)(2,1)}), bf16[32,128,128]{2,0,1:T(8,128)(2,1)}, u32[]{:S(2)}, u32[]{:S(2)}) async-start(bf16[32,128,128]{2,0,1:T(8,128)(2,1)} %bitcast.255), calls=%async_computation.3 | async-start | bytes 2097152 | tf_op jit(solution)/shard_map/all_to_all | solution.py:172
  111.8 1.2 copy-start.3
  113.0 1.1 copy-start.14
  121.3 1.6 copy-start.1
  129.8 1.1 copy-start.9
  132.6 29.5 %all-to-all-start.4 = ((f32[128,24,128]{2,1,0:T(8,128)}), f32[128,24,128]{2,1,0:T(8,128)S(1)}, u32[]{:S(2)}, u32[]{:S(2)}) async-start(f32[128,24,128]{2,1,0:T(8,128)} %bitcast.252), calls=%async_computation.4 | async-start | bytes 3145728 | tf_op jit(solution)/shard_map/all_to_all | solution.py:342
  137.6 1.7 copy-start.7
  137.6 1.7 copy-start.12
  139.3 1.2 copy-start.6
  141.4 1.2 copy-start.5
  163.3 20.7 %all-to-all-start.5 = ((bf16[128,24,128]{2,1,0:T(8,128)(2,1)}), bf16[128,24,128]{2,1,0:T(8,128)(2,1)S(1)}, u32[]{:S(2)}, u32[]{:S(2)}) async-start(bf16[128,24,128]{2,1,0:T(8,128)(2,1)} %broadcast_in_dim.8), calls=%async_computation.5 | async-start | bytes 1572864 | tf_op jit(solution)/shard_map/all_to_all | solution.py:345
  167.7 1.7 copy-start.4
  169.4 1.3 copy-start.8
  (1 other events, 1.0 us)

commit v13 on v9

--- a/solution.py
+++ b/solution.py
@@ -365,7 +365,6 @@
     act_zero = jax.nn.silu(pre_spatial).astype(jnp.bfloat16).reshape(local_frames, pixels, chans)
     cot_local = cotangent.reshape(local_frames, pixels, chans)
     act_blocks = fm_to_pixels(act_zero)
-    act_blocks, cot_local = lax.optimization_barrier((act_blocks, cot_local))
     cot_blocks = fm_to_pixels(cot_local)
     acts = [act_blocks]
     total_frames, width = act_blocks.shape[0], act_blocks.shape[1]

time: 185 us -> 197 us (1.065)
  waiting for transfers between devices: 58.8 us -> 69.9 us
  matrix products: 20.3 us -> 27.8 us
  local copies, waits for them, and re-layouts: 27.5 us -> 21.1 us
    all_to_all x2, waiting for transfers between devices: 10.2 us -> 23 us  [fm_to_frames(): lax.all_to_all(moved, ('seg', 'grp'), split_axis=1, concat_axis=1, tiled=...]
    dot_general x9, matrix products: 7.58 us -> 14 us  [spatial_back(): jnp.dot(piece, kernel[3 * row_tap + col_tap].T, preferred_element_type=jn...]
    slice x1, local copies, waits for them, and re-layouts: 7.04 us -> 2.52 us  [spatial_forward(): padded[:, row_tap:row_tap + rows, col_tap:col_tap + cols, :]]
    all_to_all x2, waiting for transfers between devices: 22.8 us -> 27.1 us  [fm_to_pixels(): lax.all_to_all(strided, ('seg', 'grp'), split_axis=1, concat_axis=1, tile...]
    all_to_all x1, waiting for transfers between devices: 14.7 us -> 11.1 us  [all_sum(): lax.all_to_all(stack, ('seg', 'grp'), split_axis=0, concat_axis=0, tiled=...]
    all_to_all x1, waiting for transfers between devices: 11.2 us -> 8.65 us  [all_sum(): lax.all_to_all(spread, ('seg', 'grp'), split_axis=0, concat_axis=0, tiled...]
    unnamed x33, local copies, waits for them, and re-layouts: 5.93 us -> 3.86 us
  transfers between devices with their start and end apart: 6 -> 6, of which waited for: 6 -> 6; matrix products, arithmetic and copies ran while one was open for 14% -> 21% of each run, Pallas kernels for 16% -> 2%
where the time goes in v13:
time: 197 us; the launch traced here: 196 us
  waiting for transfers between devices  69.9 us (35%)
  starting transfers between devices  34.9 us (18%)
  Pallas kernels  28.8 us (15%)
  matrix products  27.8 us (14%)
  local copies, waits for them, and re-layouts  21.1 us (11%)
  other arithmetic  12 us (6%)
    all_to_all x2, waiting for transfers between devices, fm_to_pixels(): lax.all_to_all(strided, ('seg', 'grp'), split_axis=1, concat_axis=1, tile...  27.1 us
    all_to_all x2, waiting for transfers between devices, fm_to_frames(): lax.all_to_all(moved, ('seg', 'grp'), split_axis=1, concat_axis=1, tiled=...  23 us
    all_to_all x2, starting transfers between devices, fm_to_pixels(): lax.all_to_all(strided, ('seg', 'grp'), split_axis=1, concat_axis=1, tile...  16.4 us
    dot_general x9, matrix products, spatial_back(): jnp.dot(piece, kernel[3 * row_tap + col_tap].T, preferred_element_type=jn...  14 us
    all_to_all x1, waiting for transfers between devices, all_sum(): lax.all_to_all(stack, ('seg', 'grp'), split_axis=0, concat_axis=0, tiled=...  11.1 us
    pallas_call x2, Pallas kernels, temporal_backward_k(): pl.pallas_call(functools.partial(tbwd_kernel, with_pre), grid_spec=pltpu....  10.5 us
    pallas_call x2, Pallas kernels, temporal_forward_k(): pl.pallas_call(tfwd_kernel, grid_spec=pltpu.PrefetchScalarGridSpec(num_sc...  10.2 us
    all_to_all x2, starting transfers between devices, fm_to_frames(): lax.all_to_all(moved, ('seg', 'grp'), split_axis=1, concat_axis=1, tiled=...  9.75 us
  transfers between devices with their start and end apart: 6, of which 6 were waited for; matrix products, arithmetic and copies ran while one was open for 21% of the time, Pallas kernels for 2%

profile of v13, /device:TPU:1, one launch (start us, length us, event | category | flops | bytes accessed | tf_op | source)
XLA Modules:
  0.0 195.7 jit_solution(16225676341602149108)
XLA Ops:
  3.6 11.5 %all-to-all-start.2 = ((bf16[32,128,128]{2,0,1:T(8,128)(2,1)}), bf16[32,128,128]{2,0,1:T(8,128)(2,1)S(1)}, u32[]{:S(2)}, u32[]{:S(2)}) async-start(bf16[32,128,128]{2,0,1:T(8,128)(2,1)} %pad.17.clone), calls=%async_computation.2 | async-start | bytes 2097152 | tf_op jit(solution)/shard_map/all_to_all | solution.py:166
  15.1 2.5 %pad_slice_fusion.8 = (bf16[1,32,120,128]{3,2,1,0:T(8,128)(2,1)S(1)}, bf16[1,32,120,128]{3,2,1,0:T(8,128)(2,1)S(1)}, bf16[1,32,120,128]{3,2,1,0:T(8,128)(2,1)S(1...) fusion(bf16[1,32,120,128]{3,2,1,0:T(8,128)(2,1)S(1)} %copy-done), kind=kLoop, calls=%fused_computation.71 | loop fusion | bytes 8847360 | tf_op jit(solution)/shard_map/slice | solution.py:36
  23.8 10.3 %all-to-all-done.2 = bf16[32,128,128]{2,0,1:T(8,128)(2,1)S(1)} async-done(((bf16[32,128,128]{2,0,1:T(8,128)(2,1)}), bf16[32,128,128]{2,0,1:T(8,128)(2,1)S(1)}, u32[]{:S(2)}, u32[]{:S(2)}) %all-to-all-start.2) | async-done | bytes 1048608 | tf_op jit(solution)/shard_map/all_to_all | solution.py:166
  34.0 4.9 %all-to-all-start = ((bf16[32,128,128]{2,0,1:T(8,128)(2,1)}), bf16[32,128,128]{2,0,1:T(8,128)(2,1)}, u32[]{:S(2)}, u32[]{:S(2)}) async-start(bf16[32,128,128]{2,0,1:T(8,128)(2,1)} %pad.16), calls=%async_computation | async-start | bytes 2097152 | tf_op jit(solution)/shard_map/all_to_all | solution.py:166
  40.8 16.8 %all-to-all-done = bf16[32,128,128]{2,0,1:T(8,128)(2,1)} async-done(((bf16[32,128,128]{2,0,1:T(8,128)(2,1)}), bf16[32,128,128]{2,0,1:T(8,128)(2,1)}, u32[]{:S(2)}, u32[]{:S(2)}) %all-to-all-start) | async-done | bytes 1048608 | tf_op jit(solution)/shard_map/all_to_all | solution.py:166
  57.6 5.1 %shard_map.110 = (f32[128,32,128]{2,1,0:T(8,128)}, bf16[128,32,128]{2,1,0:T(8,128)(2,1)}) custom-call(s32[1]{0:T(128)} %get-tuple-element.33.dil_ref, bf16[128,32,128]{2,1,0:T(8,128)(2,1)} %bitcast.19.act_ref, bf16[640,128]{1,0:T(8,128)(2,1)} %bitcast.282), custom_call_target="tpu_custom_call" | custom-call | flops 671088640 | bytes 4194304 | tf_op jit(solution)/shard_map/pallas_call | solution.py:207
  62.7 5.1 %shard_map.111 = (f32[128,32,128]{2,1,0:T(8,128)}, bf16[128,32,128]{2,1,0:T(8,128)(2,1)}) custom-call(s32[1]{0:T(128)} %get-tuple-element.34.dil_ref, bf16[128,32,128]{2,1,0:T(8,128)(2,1)} %get-tuple-element.9.act_ref, bf16[640,128]{1,0:T(8,128)(2,1)} %bitcast.284), custom_call_target="tpu_custom_call" | custom-call | flops 671088640 | bytes 4194304 | tf_op jit(solution)/shard_map/pallas_call | solution.py:207
  71.1 5.8 %shard_map.112.grad_ref = bf16[128,32,128]{2,1,0:T(8,128)(2,1)} custom-call(s32[1]{0:T(128)} %get-tuple-element.34.dil_ref, bf16[128,32,128]{2,1,0:T(8,128)(2,1)} %get-tuple-element.9.act_ref, bf16[128,32,128]{2,1,0:T(8,128)(2,1)} %fusion.1.grad_ref, bf16[640,128]{1,0:T(8,128)(2,1)} %bitcast.285, f32[128,32,128]{2,1,0:T(8,128)} %get-tuple-element.12.rest_0_), custom_call_target="tpu_custom_call" | custom-call | flops 671088640 | bytes 5242880 | tf_op jit(solution)/shard_map/pallas_call | solution.py:316
  76.9 4.8 %shard_map.113 = bf16[128,32,128]{2,1,0:T(8,128)(2,1)} custom-call(s32[1]{0:T(128)} %get-tuple-element.33.dil_ref, bf16[128,32,128]{2,1,0:T(8,128)(2,1)} %bitcast.19.act_ref, bf16[128,32,128]{2,1,0:T(8,128)(2,1)} %shard_map.112.grad_ref, bf16[640,128]{1,0:T(8,128)(2,1)} %bitcast.283), custom_call_target="tpu_custom_call" | custom-call | flops 671088640 | bytes 5242880 | tf_op jit(solution)/shard_map/pallas_call | solution.py:316
  81.7 4.0 %shard_map.114 = f32[5,128,128]{2,1,0:T(8,128)} custom-call(s32[1]{0:T(128)} %get-tuple-element.33.dil_ref, bf16[128,32,128]{2,1,0:T(8,128)(2,1)} %bitcast.19.act_ref, bf16[128,32,128]{2,1,0:T(8,128)(2,1)} %shard_map.112.grad_ref), custom_call_target="tpu_custom_call" | custom-call | flops 671088640 | bytes 2097152 | tf_op jit(solution)/shard_map/pallas_call | solution.py:289
  85.7 4.9 %all-to-all-start.3 = ((bf16[32,128,128]{2,0,1:T(8,128)(2,1)}), bf16[32,128,128]{2,0,1:T(8,128)(2,1)}, u32[]{:S(2)}, u32[]{:S(2)}) async-start(bf16[32,128,128]{2,0,1:T(8,128)(2,1)} %bitcast.249), calls=%async_computation.3 | async-start | bytes 2097152 | tf_op jit(solution)/shard_map/all_to_all | solution.py:172
  92.9 4.0 %shard_map.115 = f32[5,128,128]{2,1,0:T(8,128)} custom-call(s32[1]{0:T(128)} %get-tuple-element.34.dil_ref, bf16[128,32,128]{2,1,0:T(8,128)(2,1)} %get-tuple-element.9.act_ref, bf16[128,32,128]{2,1,0:T(8,128)(2,1)} %fusion.1.grad_ref), custom_call_target="tpu_custom_call" | custom-call | flops 671088640 | bytes 2097152 | tf_op jit(solution)/shard_map/pallas_call | solution.py:289
  100.4 8.8 %all-to-all-done.3 = bf16[32,128,128]{2,0,1:T(8,128)(2,1)} async-done(((bf16[32,128,128]{2,0,1:T(8,128)(2,1)}), bf16[32,128,128]{2,0,1:T(8,128)(2,1)}, u32[]{:S(2)}, u32[]{:S(2)}) %all-to-all-start.3) | async-done | bytes 1048608 | tf_op jit(solution)/shard_map/all_to_all | solution.py:172
  109.2 2.8 %multiply_convert_fusion = bf16[30,128,128]{2,0,1:T(8,128)(2,1)S(1)} fusion(f32[30,128,128]{2,1,0:T(8,128)S(1)} %bitcast.239, bf16[32,128,128]{2,0,1:T(8,128)(2,1)} %all-to-all-done.3), kind=kLoop, calls=%fused_computation.19 | loop fusion | flops 4915200 | bytes 3932160 | tf_op jit(solution)/shard_map/convert_element_type | solution.py:418
  119.0 4.4 %all-to-all-start.4 = ((f32[128,24,128]{2,1,0:T(8,128)}), f32[128,24,128]{2,1,0:T(8,128)S(1)}, u32[]{:S(2)}, u32[]{:S(2)}) async-start(f32[128,24,128]{2,1,0:T(8,128)} %bitcast.245), calls=%async_computation.4 | async-start | bytes 3145728 | tf_op jit(solution)/shard_map/all_to_all | solution.py:342
  126.8 3.5 %pad_slice_fusion = (bf16[1,32,120,128]{3,2,1,0:T(8,128)(2,1)}, bf16[1,32,120,128]{3,2,1,0:T(8,128)(2,1)S(1)}, bf16[1,32,120,128]{3,2,1,0:T(8,128)(2,1)S(1)}, bf...) fusion(bf16[1,32,120,128]{3,2,1,0:T(8,128)(2,1)S(1)} %multiply_, ...), kind=kLoop, calls=%fused_computation.63 | loop fusion | bytes 8847360 | tf_op jit(solution)/shard_map/slice | solution.py:51
  132.7 2.5 %convolution_add_fusion.6 = f32[3840,128]{1,0:T(8,128)} fusion(f32[3840,128]{1,0:T(8,128)S(1)} %convolution_add_fusion.7, bf16[3840,128]{1,0:T(8,128)(2,1)S(1)} %bitcast.260, bf16[9,128,128]{2,1,0:T(8,128)(2,1)} %param.8), kind=kOutput, calls=%fused_computation.6 | convolution fusion | flops 126320640 | bytes 4947968 | tf_op jit(solution)/shard_map/dot_general | solution.py:54
  136.9 11.1 %all-to-all-done.4 = f32[128,24,128]{2,1,0:T(8,128)S(1)} async-done(((f32[128,24,128]{2,1,0:T(8,128)}), f32[128,24,128]{2,1,0:T(8,128)S(1)}, u32[]{:S(2)}, u32[]{:S(2)}) %all-to-all-start.4) | async-done | bytes 1572896 | tf_op jit(solution)/shard_map/all_to_all | solution.py:342
  148.0 4.8 %all-to-all-start.1 = ((bf16[32,128,128]{2,0,1:T(8,128)(2,1)}), bf16[32,128,128]{2,0,1:T(8,128)(2,1)}, u32[]{:S(2)}, u32[]{:S(2)}) async-start(bf16[32,128,128]{2,0,1:T(8,128)(2,1)} %bitcast.246), calls=%async_computation.1 | async-start | bytes 2097152 | tf_op jit(solution)/shard_map/all_to_all | solution.py:172
  157.2 14.2 %all-to-all-done.1 = bf16[32,128,128]{2,0,1:T(8,128)(2,1)} async-done(((bf16[32,128,128]{2,0,1:T(8,128)(2,1)}), bf16[32,128,128]{2,0,1:T(8,128)(2,1)}, u32[]{:S(2)}, u32[]{:S(2)}) %all-to-all-start.1) | async-done | bytes 1048608 | tf_op jit(solution)/shard_map/all_to_all | solution.py:172
  172.5 4.4 %all-to-all-start.5 = ((bf16[128,24,128]{2,1,0:T(8,128)(2,1)}), bf16[128,24,128]{2,1,0:T(8,128)(2,1)S(1)}, u32[]{:S(2)}, u32[]{:S(2)}) async-start(bf16[128,24,128]{2,1,0:T(8,128)(2,1)} %broadcast_in_dim.8), calls=%async_computation.5 | async-start | bytes 1572864 | tf_op jit(solution)/shard_map/all_to_all | solution.py:345
  178.5 2.6 %copy.44 = bf16[30,128,128]{2,1,0:T(8,128)(2,1)} copy(bf16[30,128,128]{2,0,1:T(8,128)(2,1)} %bitcast.237) | data formatting | bytes 1966080 | tf_op jit(solution)/shard_map/slice | solution.py:173
  182.4 2.1 %fusion = bf16[3840,128]{1,0:T(8,128)(2,1)} fusion(f32[3840,128]{1,0:T(8,128)S(1)} %convolution_add_fusion.1, bf16[3840,128]{1,0:T(8,128)(2,1)S(1)} %bitcast.275, bf16[9,128,128]{2,1,0:T(8,128)(2,1)} %param.8), kind=kOutput, calls=%fused_computation.16 | convolution fusion | flops 126812160 | bytes 3964928 | tf_op jit(solution)/shard_map/dot_general | solution.py:54
  184.5 8.7 %all-to-all-done.5 = bf16[128,24,128]{2,1,0:T(8,128)(2,1)S(1)} async-done(((bf16[128,24,128]{2,1,0:T(8,128)(2,1)}), bf16[128,24,128]{2,1,0:T(8,128)(2,1)S(1)}, u32[]{:S(2)}, u32[]{:S(2)}) %all-to-all-start.5) | async-done | bytes 786464 | tf_op jit(solution)/shard_map/all_to_all | solution.py:345
  (92 shorter events, 45.0 us)
Async XLA Ops:
  2.5 12.6 %copy-start = (bf16[1,32,120,128]{3,2,1,0:T(8,128)(2,1)S(1)}, bf16[1,32,120,128]{3,2,1,0:T(8,128)(2,1)}, u32[]{:S(2)}) copy-start(bf16[1,32,120,128]{3,2,1,0:T(8,128)(2,1)} %param.7) | copy-start | bytes 2949124
  3.6 30.5 %all-to-all-start.2 = ((bf16[32,128,128]{2,0,1:T(8,128)(2,1)}), bf16[32,128,128]{2,0,1:T(8,128)(2,1)S(1)}, u32[]{:S(2)}, u32[]{:S(2)}) async-start(bf16[32,128,128]{2,0,1:T(8,128)(2,1)} %pad.17.clone), calls=%async_computation.2 | async-start | bytes 2097152 | tf_op jit(solution)/shard_map/all_to_all | solution.py:166
  15.1 2.5 %copy-start.9 = (bf16[9,128,128]{2,1,0:T(8,128)(2,1)S(1)}, bf16[9,128,128]{2,1,0:T(8,128)(2,1)}, u32[]{:S(2)}) copy-start(bf16[9,128,128]{2,1,0:T(8,128)(2,1)} %param.8) | copy-start | bytes 884740
  22.6 16.4 %copy-start.14 = (s32[2]{0:T(128)S(1)}, s32[2]{0:T(128)}, u32[]{:S(2)}) copy-start(s32[2]{0:T(128)} %param.12) | copy-start | bytes 28
  22.6 16.9 %copy-start.15 = (s32[8]{0:T(128)S(1)}, s32[8]{0:T(128)}, u32[]{:S(2)}) copy-start(s32[8]{0:T(128)} %param.11) | copy-start | bytes 100
  22.6 17.0 %copy-start.12 = (bf16[2,5,128,128]{3,2,1,0:T(8,128)(2,1)S(1)}, bf16[2,5,128,128]{3,2,1,0:T(8,128)(2,1)}, u32[]{:S(2)}) copy-start(bf16[2,5,128,128]{3,2,1,0:T(8,128)(2,1)} %param.9) | copy-start | bytes 983044
  23.8 16.8 %copy-start.13 = (bf16[2,128,128]{2,1,0:T(8,128)(2,1)S(1)}, bf16[2,128,128]{2,1,0:T(8,128)(2,1)}, u32[]{:S(2)}) copy-start(bf16[2,128,128]{2,1,0:T(8,128)(2,1)} %param.10) | copy-start | bytes 196612
  34.0 23.5 %all-to-all-start = ((bf16[32,128,128]{2,0,1:T(8,128)(2,1)}), bf16[32,128,128]{2,0,1:T(8,128)(2,1)}, u32[]{:S(2)}, u32[]{:S(2)}) async-start(bf16[32,128,128]{2,0,1:T(8,128)(2,1)} %pad.16), calls=%async_computation | async-start | bytes 2097152 | tf_op jit(solution)/shard_map/all_to_all | solution.py:166
  67.8 1.6 copy-start.8
  85.7 23.5 %all-to-all-start.3 = ((bf16[32,128,128]{2,0,1:T(8,128)(2,1)}), bf16[32,128,128]{2,0,1:T(8,128)(2,1)}, u32[]{:S(2)}, u32[]{:S(2)}) async-start(bf16[32,128,128]{2,0,1:T(8,128)(2,1)} %bitcast.249), calls=%async_computation.3 | async-start | bytes 2097152 | tf_op jit(solution)/shard_map/all_to_all | solution.py:172
  96.9 1.9 copy-start.10
  96.9 1.9 copy-start.11
  96.9 2.1 %copy-start.3 = (bf16[128,32,128]{2,1,0:T(8,128)(2,1)S(1)}, bf16[128,32,128]{2,1,0:T(8,128)(2,1)}, u32[]{:S(2)}) copy-start(bf16[128,32,128]{2,1,0:T(8,128)(2,1)} %get-tuple-element.10) | copy-start | bytes 3145732
  112.0 1.2 copy-start.1
  119.0 29.0 %all-to-all-start.4 = ((f32[128,24,128]{2,1,0:T(8,128)}), f32[128,24,128]{2,1,0:T(8,128)S(1)}, u32[]{:S(2)}, u32[]{:S(2)}) async-start(f32[128,24,128]{2,1,0:T(8,128)} %bitcast.245), calls=%async_computation.4 | async-start | bytes 3145728 | tf_op jit(solution)/shard_map/all_to_all | solution.py:342
  136.9 15.9 %copy-start.2 = (f32[3840,128]{1,0:T(8,128)S(1)}, f32[3840,128]{1,0:T(8,128)}, u32[]{:S(2)}) copy-start(f32[3840,128]{1,0:T(8,128)} %convolution_add_fusion.6) | copy-start | bytes 5898244
  148.0 23.5 %all-to-all-start.1 = ((bf16[32,128,128]{2,0,1:T(8,128)(2,1)}), bf16[32,128,128]{2,0,1:T(8,128)(2,1)}, u32[]{:S(2)}, u32[]{:S(2)}) async-start(bf16[32,128,128]{2,0,1:T(8,128)(2,1)} %bitcast.246), calls=%async_computation.1 | async-start | bytes 2097152 | tf_op jit(solution)/shard_map/all_to_all | solution.py:172
  152.9 1.7 copy-start.4
  154.6 1.3 copy-start.6
  172.5 20.7 %all-to-all-start.5 = ((bf16[128,24,128]{2,1,0:T(8,128)(2,1)}), bf16[128,24,128]{2,1,0:T(8,128)(2,1)S(1)}, u32[]{:S(2)}, u32[]{:S(2)}) async-start(bf16[128,24,128]{2,1,0:T(8,128)(2,1)} %broadcast_in_dim.8), calls=%async_computation.5 | async-start | bytes 1572864 | tf_op jit(solution)/shard_map/all_to_all | solution.py:345
  178.5 2.6 %copy-start.5 = (bf16[1,32,120,128]{3,2,1,0:T(8,128)(2,1)S(1)}, bf16[1,32,120,128]{3,2,1,0:T(8,128)(2,1)}, u32[]{:S(2)}) copy-start(bf16[1,32,120,128]{3,2,1,0:T(8,128)(2,1)} %get-tuple-element.19) | copy-start | bytes 2949124
  181.1 1.3 copy-start.7
